TPU v7x, 32 devices: a whole 2x2x4 slice. The times are simulated.
32 devices in a mesh: wide: 8 (over z, x), narrow: 4 (over y, core).
Axes of the slice: x: 2, y: 2, z: 4, core: 2. Of those that a mesh axis runs over, the one named last changes fastest.
Arguments:
- tokens: bfloat16 [32, 1024, 1024], P(('wide', 'narrow')), may hold values from -6 to 6
- lengths: int32 [32, 8], P(('wide', 'narrow')), may hold values from 1 to 512, 1024 in all within a row
- cotangent: bfloat16 [32, 1024, 1024], P(('wide', 'narrow')), may hold values from -6 to 6
- mixer_weight: bfloat16 [1024, 3072], P(('wide', 'narrow')), may hold values from -0.1875 to 0.1875
- output_weight: bfloat16 [1024, 1024], P(('wide', 'narrow')), may hold values from -0.75 to 0.75
- expand_weight: bfloat16 [1024, 4096], P(('wide', 'narrow')), may hold values from -0.1875 to 0.1875
- contract_weight: bfloat16 [4096, 1024], P(('wide', 'narrow')), may hold values from -0.09375 to 0.09375
- mixer_bias: float32 [3072], replicated, may hold values from -3 to 3
- output_bias: float32 [1024], replicated, may hold values from -2 to 2
- expand_bias: float32 [4096], replicated, may hold values from -3 to 3
- contract_bias: float32 [1024], replicated, may hold values from -2 to 2
- norm_gains: float32 [2, 1024], replicated, may hold values from 0.5 to 1.5
- norm_shifts: float32 [2, 1024], replicated, may hold values from -2 to 2
- prefix_embed: float32 [10, 1024], replicated, may hold values from -6 to 6
- reparam_in: float32 [1024, 512], replicated, may hold values from -0.1875 to 0.1875
- reparam_in_bias: float32 [512], replicated, may hold values from -3 to 3
- reparam_out: float32 [512, 2048], replicated, may hold values from -0.25 to 0.25
- reparam_out_bias: float32 [2048], replicated, may hold values from -3 to 3
Outputs:
- out_tokens: bfloat16 [32, 1024, 1024], P(('wide', 'narrow'))
- grad_tokens: bfloat16 [32, 1024, 1024], P(('wide', 'narrow'))
- grad_embed: float32 [10, 1024], replicated
- grad_in: float32 [1024, 512], replicated
- grad_in_bias: float32 [512], replicated
- grad_out: float32 [512, 2048], replicated
- grad_out_bias: float32 [2048], replicated
Inputs may be any that keep to these rules, and one draw needn't show every extreme that they name: Each row of lengths holds 8 document lengths that sum to 1024; in every row one document has exactly 512 tokens.
All inputs are finite; a program needn't handle non-finite values.
Results may differ from a plain program's by a relative error of at most 0.015.
Values may be sent and summed in bfloat16 or wider, within the bound.
A program may use at most 320 MiB of HBM per device.

v0:
```python
from functools import partial

import jax
import jax.numpy as jnp
from jax import lax
from jax.sharding import PartitionSpec as P

HEADS = 16


masked_score = -1e30


def norm_layer(values, norm_gain, norm_shift):
    center = values - jnp.mean(values, axis=-1, keepdims=True)
    spread = jnp.mean(center * center, axis=-1, keepdims=True)
    return center * lax.rsqrt(spread + 1e-05) * norm_gain + norm_shift


def times_transposed(left_side, right_side):
    return lax.dot_general(
        left_side, right_side, (((1,), (1,)), ((), ())), preferred_element_type=jnp.float32
    )


def segment_ids(lengths_row, length):
    segment_ends = jnp.cumsum(lengths_row)
    places = jnp.arange(length, dtype=jnp.int32)
    return jnp.sum((places[:, None] >= segment_ends[None, :]).astype(jnp.int32), axis=1)


def reparam(embed_values, in_weight, in_shift, out_weight, out_shift):
    squashed = jnp.tanh(
        jnp.dot(embed_values, in_weight, precision=lax.Precision.HIGHEST) + in_shift
    )
    return jnp.dot(squashed, out_weight, precision=lax.Precision.HIGHEST) + out_shift


def split_row(mixed_row, prefix_low, head_count):
    length = mixed_row.shape[0]
    model_width = mixed_row.shape[1] // 3
    head_size = model_width // head_count
    prefix_count = prefix_low.shape[0]
    key_heads = mixed_row[:, model_width : 2 * model_width].reshape(length, head_count, head_size)
    value_heads = mixed_row[:, 2 * model_width :].reshape(length, head_count, head_size)
    pre_keys = prefix_low[:, :model_width].reshape(prefix_count, head_count, head_size)
    pre_values = prefix_low[:, model_width:].reshape(prefix_count, head_count, head_size)
    return (key_heads, value_heads, pre_keys, pre_values)


def block_scores(mixed_row, segments, key_heads, pre_keys, first_row, block_rows):
    length, head_count, head_size = key_heads.shape
    model_width = head_count * head_size
    score_scale = head_size ** (-0.5)
    queries = lax.dynamic_slice_in_dim(mixed_row, first_row, block_rows, 0)[:, :model_width]
    queries = queries.reshape(block_rows, head_count, head_size)
    token_scores = (
        jnp.einsum("qhd,khd->hqk", queries, key_heads, preferred_element_type=jnp.float32)
        * score_scale
    )
    prefix_scores = (
        jnp.einsum("qhd,phd->hqp", queries, pre_keys, preferred_element_type=jnp.float32)
        * score_scale
    )
    query_pos = first_row + jnp.arange(block_rows, dtype=jnp.int32)
    key_pos = jnp.arange(length, dtype=jnp.int32)
    query_seg = lax.dynamic_slice_in_dim(segments, first_row, block_rows, 0)
    visible = (query_seg[:, None] == segments[None, :]) & (key_pos[None, :] <= query_pos[:, None])
    token_scores = jnp.where(visible[None], token_scores, masked_score)
    return (queries, token_scores, prefix_scores)


def attend_forward(mixed_row, lengths_row, prefix_low, head_count):
    length = mixed_row.shape[0]
    model_width = mixed_row.shape[1] // 3
    block_rows = min(512, length)
    segments = segment_ids(lengths_row, length)
    key_heads, value_heads, pre_keys, pre_values = split_row(mixed_row, prefix_low, head_count)

    def one_block(first_row):
        queries, token_scores, prefix_scores = block_scores(
            mixed_row, segments, key_heads, pre_keys, first_row, block_rows
        )
        peak_score = jnp.maximum(jnp.max(token_scores, axis=-1), jnp.max(prefix_scores, axis=-1))
        token_probs = jnp.exp(token_scores - peak_score[..., None])
        prefix_probs = jnp.exp(prefix_scores - peak_score[..., None])
        weight_sum = jnp.sum(token_probs, axis=-1) + jnp.sum(prefix_probs, axis=-1)
        token_weights = (token_probs / weight_sum[..., None]).astype(jnp.bfloat16)
        prefix_weights = (prefix_probs / weight_sum[..., None]).astype(jnp.bfloat16)
        attended = jnp.einsum(
            "hqk,khd->qhd", token_weights, value_heads, preferred_element_type=jnp.float32
        )
        attended = attended + jnp.einsum(
            "hqp,phd->qhd", prefix_weights, pre_values, preferred_element_type=jnp.float32
        )
        return (
            attended.reshape(block_rows, model_width).astype(jnp.bfloat16),
            peak_score + jnp.log(weight_sum),
        )

    first_rows = jnp.arange(length // block_rows, dtype=jnp.int32) * block_rows
    attended, log_sums = lax.map(one_block, first_rows)
    return (attended.reshape(length, model_width), log_sums)


def attend_backward(mixed_row, lengths_row, grad_row, log_sums, prefix_low, head_count):
    length = mixed_row.shape[0]
    model_width = mixed_row.shape[1] // 3
    head_size = model_width // head_count
    score_scale = head_size ** (-0.5)
    block_rows = min(512, length)
    prefix_count = prefix_low.shape[0]
    segments = segment_ids(lengths_row, length)
    key_heads, value_heads, pre_keys, pre_values = split_row(mixed_row, prefix_low, head_count)

    def one_block(running, block_items):
        first_row, log_sum = block_items
        queries, token_scores, prefix_scores = block_scores(
            mixed_row, segments, key_heads, pre_keys, first_row, block_rows
        )
        grad_heads = lax.dynamic_slice_in_dim(grad_row, first_row, block_rows, 0)
        grad_heads = grad_heads.reshape(block_rows, head_count, head_size)
        token_probs = jnp.exp(token_scores - log_sum[..., None])
        prefix_probs = jnp.exp(prefix_scores - log_sum[..., None])
        token_dprob = jnp.einsum(
            "qhd,khd->hqk", grad_heads, value_heads, preferred_element_type=jnp.float32
        )
        prefix_dprob = jnp.einsum(
            "qhd,phd->hqp", grad_heads, pre_values, preferred_element_type=jnp.float32
        )
        prob_inner = jnp.sum(token_probs * token_dprob, axis=-1) + jnp.sum(
            prefix_probs * prefix_dprob, axis=-1
        )
        token_dscore = (token_probs * (token_dprob - prob_inner[..., None])).astype(jnp.bfloat16)
        prefix_dscore = (prefix_probs * (prefix_dprob - prob_inner[..., None])).astype(jnp.bfloat16)
        grad_queries = jnp.einsum(
            "hqk,khd->qhd", token_dscore, key_heads, preferred_element_type=jnp.float32
        )
        grad_queries = (
            grad_queries
            + jnp.einsum(
                "hqp,phd->qhd", prefix_dscore, pre_keys, preferred_element_type=jnp.float32
            )
        ) * score_scale
        key_sum, value_sum, pre_key_sum, pre_value_sum = running
        key_sum = (
            key_sum
            + jnp.einsum("hqk,qhd->khd", token_dscore, queries, preferred_element_type=jnp.float32)
            * score_scale
        )
        value_sum = value_sum + jnp.einsum(
            "hqk,qhd->khd",
            token_probs.astype(jnp.bfloat16),
            grad_heads,
            preferred_element_type=jnp.float32,
        )
        pre_key_sum = (
            pre_key_sum
            + jnp.einsum("hqp,qhd->phd", prefix_dscore, queries, preferred_element_type=jnp.float32)
            * score_scale
        )
        pre_value_sum = pre_value_sum + jnp.einsum(
            "hqp,qhd->phd",
            prefix_probs.astype(jnp.bfloat16),
            grad_heads,
            preferred_element_type=jnp.float32,
        )
        return (
            (key_sum, value_sum, pre_key_sum, pre_value_sum),
            grad_queries.reshape(block_rows, model_width),
        )

    token_zeros = jnp.zeros((length, head_count, head_size), jnp.float32)
    prefix_zeros = jnp.zeros((prefix_count, head_count, head_size), jnp.float32)
    first_rows = jnp.arange(length // block_rows, dtype=jnp.int32) * block_rows
    sums, grad_queries = lax.scan(
        one_block, (token_zeros, token_zeros, prefix_zeros, prefix_zeros), (first_rows, log_sums)
    )
    key_sum, value_sum, pre_key_sum, pre_value_sum = sums
    grad_mixed = jnp.concatenate(
        [
            grad_queries.reshape(length, model_width),
            key_sum.reshape(length, model_width),
            value_sum.reshape(length, model_width),
        ],
        axis=1,
    ).astype(jnp.bfloat16)
    grad_prefix = jnp.concatenate(
        [
            pre_key_sum.reshape(prefix_count, model_width),
            pre_value_sum.reshape(prefix_count, model_width),
        ],
        axis=1,
    )
    return (grad_mixed, grad_prefix)


def shards(
    tokens,
    lengths,
    cotangent,
    mixer_weight,
    output_weight,
    expand_weight,
    contract_weight,
    mixer_bias,
    output_bias,
    expand_bias,
    contract_bias,
    norm_gains,
    norm_shifts,
    prefix_embed,
    reparam_in,
    reparam_in_bias,
    reparam_out,
    reparam_out_bias,
):
    row_count, length, model_width = tokens.shape
    total_rows = row_count * length
    full_mixer, full_output, full_expand, full_contract = (
        lax.all_gather(mixer_weight, ("wide", "narrow"), axis=0, tiled=True),
        lax.all_gather(output_weight, ("wide", "narrow"), axis=0, tiled=True),
        lax.all_gather(expand_weight, ("wide", "narrow"), axis=0, tiled=True),
        lax.all_gather(contract_weight, ("wide", "narrow"), axis=0, tiled=True),
    )
    prefix_kv, reparam_back = jax.vjp(
        reparam, prefix_embed, reparam_in, reparam_in_bias, reparam_out, reparam_out_bias
    )
    prefix_low = prefix_kv.astype(jnp.bfloat16)
    inputs = tokens.reshape(total_rows, model_width).astype(jnp.float32)
    normed_one, norm_one_back = jax.vjp(
        lambda values: norm_layer(values, norm_gains[0], norm_shifts[0]), inputs
    )
    mixed = (
        jnp.dot(normed_one.astype(jnp.bfloat16), full_mixer, preferred_element_type=jnp.float32)
        + mixer_bias
    )
    mixed_low = mixed.astype(jnp.bfloat16).reshape(row_count, length, 3 * model_width)
    attended, log_sums = lax.map(
        lambda row_items: attend_forward(row_items[0], row_items[1], prefix_low, HEADS),
        (mixed_low, lengths),
    )
    attended = attended.reshape(total_rows, model_width)
    middle = inputs + (
        jnp.dot(attended, full_output, preferred_element_type=jnp.float32) + output_bias
    )
    normed_two, norm_two_back = jax.vjp(
        lambda values: norm_layer(values, norm_gains[1], norm_shifts[1]), middle
    )
    expanded = (
        jnp.dot(normed_two.astype(jnp.bfloat16), full_expand, preferred_element_type=jnp.float32)
        + expand_bias
    )
    activated, gelu_back = jax.vjp(partial(jax.nn.gelu, approximate=True), expanded)
    result = middle + (
        jnp.dot(activated.astype(jnp.bfloat16), full_contract, preferred_element_type=jnp.float32)
        + contract_bias
    )
    out_tokens = result.astype(jnp.bfloat16).reshape(row_count, length, model_width)
    back_mixer, back_output, back_expand, back_contract = (
        lax.all_gather(mixer_weight, ("wide", "narrow"), axis=0, tiled=True),
        lax.all_gather(output_weight, ("wide", "narrow"), axis=0, tiled=True),
        lax.all_gather(expand_weight, ("wide", "narrow"), axis=0, tiled=True),
        lax.all_gather(contract_weight, ("wide", "narrow"), axis=0, tiled=True),
    )
    grad_result = cotangent.reshape(total_rows, model_width)
    grad_activated = times_transposed(grad_result, back_contract)
    grad_expanded = gelu_back(grad_activated)[0].astype(jnp.bfloat16)
    grad_normed_two = times_transposed(grad_expanded, back_expand)
    grad_middle = grad_result.astype(jnp.float32) + norm_two_back(grad_normed_two)[0]
    grad_attended = times_transposed(grad_middle.astype(jnp.bfloat16), back_output).astype(
        jnp.bfloat16
    )
    grad_mixed, prefix_grads = lax.map(
        lambda row_items: attend_backward(
            row_items[0], row_items[1], row_items[2], row_items[3], prefix_low, HEADS
        ),
        (mixed_low, lengths, grad_attended.reshape(row_count, length, model_width), log_sums),
    )
    grad_normed_one = times_transposed(grad_mixed.reshape(total_rows, 3 * model_width), back_mixer)
    grad_inputs = (grad_middle + norm_one_back(grad_normed_one)[0]).astype(jnp.bfloat16)
    grad_inputs = grad_inputs.reshape(row_count, length, model_width)
    grad_prefix = jnp.sum(prefix_grads, axis=0)
    embed_part, in_part, in_bias_part, out_part, out_bias_part = reparam_back(grad_prefix)
    embed_share, in_share, in_bias_share, out_share, out_bias_share = (
        lax.psum_scatter(
            embed_part.astype(jnp.bfloat16), "narrow", scatter_dimension=1, tiled=True
        ).astype(jnp.float32),
        lax.psum_scatter(
            in_part.astype(jnp.bfloat16), "narrow", scatter_dimension=0, tiled=True
        ).astype(jnp.float32),
        lax.psum_scatter(
            in_bias_part.astype(jnp.bfloat16), "narrow", scatter_dimension=0, tiled=True
        ).astype(jnp.float32),
        lax.psum_scatter(
            out_part.astype(jnp.bfloat16), "narrow", scatter_dimension=0, tiled=True
        ).astype(jnp.float32),
        lax.psum_scatter(
            out_bias_part.astype(jnp.bfloat16), "narrow", scatter_dimension=0, tiled=True
        ).astype(jnp.float32),
    )
    embed_sum, in_sum, in_bias_sum, out_sum, out_bias_sum = lax.psum(
        (embed_share, in_share, in_bias_share, out_share, out_bias_share), "wide"
    )
    grad_embed, grad_in, grad_in_bias, grad_out, grad_out_bias = (
        lax.all_gather(embed_sum.astype(jnp.bfloat16), "narrow", axis=1, tiled=True).astype(
            embed_sum.dtype
        ),
        lax.all_gather(in_sum.astype(jnp.bfloat16), "narrow", axis=0, tiled=True).astype(
            in_sum.dtype
        ),
        lax.all_gather(in_bias_sum.astype(jnp.bfloat16), "narrow", axis=0, tiled=True).astype(
            in_bias_sum.dtype
        ),
        lax.all_gather(out_sum.astype(jnp.bfloat16), "narrow", axis=0, tiled=True).astype(
            out_sum.dtype
        ),
        lax.all_gather(out_bias_sum.astype(jnp.bfloat16), "narrow", axis=0, tiled=True).astype(
            out_bias_sum.dtype
        ),
    )
    return (out_tokens, grad_inputs, grad_embed, grad_in, grad_in_bias, grad_out, grad_out_bias)


def solution(mesh):
    return jax.shard_map(
        shards,
        mesh=mesh,
        in_specs=(
            P(("wide", "narrow"), None, None),
            P(("wide", "narrow"), None),
            P(("wide", "narrow"), None, None),
            P(("wide", "narrow"), None),
            P(("wide", "narrow"), None),
            P(("wide", "narrow"), None),
            P(("wide", "narrow"), None),
            P(),
            P(),
            P(),
            P(),
            P(),
            P(),
            P(),
            P(),
            P(),
            P(),
            P(),
        ),
        out_specs=(
            P(("wide", "narrow"), None, None),
            P(("wide", "narrow"), None, None),
            P(),
            P(),
            P(),
            P(),
            P(),
        ),
        check_vma=False,
    )
```

profile of v0, /device:TPU:0, one launch (start us, length us, event | category | flops | bytes accessed | tf_op | source)
XLA Modules:
  0.0 866.3 jit_solution(12630873610976105502)
XLA Ops:
  16.4 4.3 fusion.52
  20.9 4.0 copy.105
  24.9 2.0 convert_reduce_fusion
  26.9 2.2 fusion.46
  29.1 4.0 copy.113
  33.1 50.1 %all-gather.9.cloned.1.call-done = bf16[1024,3072]{1,0:T(8,128)(2,1)} async-done(((bf16[32,3072]{1,0:T(8,128)(2,1)}), bf16[1024,3072]{1,0:T(8,128)(2,1)}) %all-gather.9.cloned.1.call-update) | async-done | bytes 6291472 | tf_op jit(solution)/shard_map/all_gather | solution.py:221
  83.2 10.6 %add_convert_fusion.1 = bf16[1024,3072]{1,0:T(8,128)(2,1)S(1)} fusion(f32[3072]{0:T(1024)S(1)} %copy-done.38, bf16[1024,3072]{1,0:T(8,128)(2,1)} %all-gather.9.cloned.1.call-done, bf16[1,1024,1024]{1,2,0:T(8,128)(2,1)} %copy.105, f32[1024]{0:T(1024)S(1)} %bitcast.243, f32[1024]{0:T(1024)S(1)} %bitcast.234, f32[1024]{0:T(1024)S(1)} %fusion.81, ...), kind=kOutput, calls=%fused_computation.60 | convolution fusion | flops 6455033856 | bytes 14708736 | tf_op jit(solution)/shard_map/dot_general | solution.py:235
  93.9 2.8 copy-done.11
  96.7 2.4 fusion.96
  99.1 8.6 copy.108
  107.7 3.9 copy.107
  111.6 3.9 copy.106
  115.6 113.5 %while.52 = (s32[]{:T(128)}, bf16[2,512,1024]{2,1,0:T(8,128)(2,1)}, f32[2,16,512]{2,1,0:T(8,128)}, s32[2]{0:T(128)S(1)}, s32[1024]{0:T(1024)S(1)}, /*index=5*/bf...) while((s32[]{:T(128)}, bf16[2,512,1024]{2,1,0:T(8,128)(2,1)}, ...), condition=%wide.region_9.10_spmd, body=%wide.region_4.9_spmd.sunk | while | flops 2272305664 | bytes 138991888 | solution.py:102
  121.8 14.1 %fusion.197 = (f32[16,512]{1,0:T(8,128)S(1)}, f32[16,512,1024]{2,1,0:T(8,128)}) fusion(pred[512,1024]{1,0:T(8,128)(4,1)S(1)} %fusion.196, bf16[512,16,64]{0,2,1:T(8,128)(2,1)S(1)} %bitcast.228, bf16[1024,16,64]{0,2,1:T(8,128)(2,1)S(1)} %copy-done.1), kind=kOutput, calls=%fused_computation.3.clone.1 | convolution fusion | flops 1098899456 | bytes 37257216 | tf_op jit(solution)/shard_map/while/body/eval_jaxpr/while/body/eval_jaxpr/qhd,khd->hqk/dot_general | solution.py:58
  136.1 15.1 %fusion.199 = f32[16,512]{1,0:T(8,128)S(1)} fusion(f32[16,512,1024]{2,1,0:T(8,128)} %get-tuple-element.630, f32[16,512]{1,0:T(8,128)S(1)} %max.16, pred[512,1024]{1,0:T(8,128)(4,1)S(1)} %fusion.196), kind=kLoop, calls=%fused_computation.4.clone.1 | loop fusion | flops 33546240 | bytes 34144256 | tf_op jit(solution)/shard_map/while/body/eval_jaxpr/while/body/eval_jaxpr/reduce_sum | solution.py:87
  151.9 16.0 %fusion.201 = f32[16,512,64]{1,2,0:T(8,128)S(1)} fusion(bf16[1024,16,64]{0,2,1:T(8,128)(2,1)S(1)} %copy-done.7, f32[16,512,1024]{2,1,0:T(8,128)} %get-tuple-element.630, f32[16,512]{1,0:T(8,128)S(1)} %get-tuple-element.634, f32[16,512]{1,0:T(8,128)S(1)} %max.16, pred[512,1024]{1,0:T(8,128)(4,1)S(1)} %fusion.196), kind=kOutput, calls=%fused_computation.5.clone.1 | convolution fusion | flops 1115684864 | bytes 38338560 | tf_op jit(solution)/shard_map/while/body/eval_jaxpr/while/body/eval_jaxpr/hqk,khd->qhd/dot_general | solution.py:90
  177.9 14.9 %fusion.197 = (f32[16,512]{1,0:T(8,128)S(1)}, f32[16,512,1024]{2,1,0:T(8,128)}) fusion(pred[512,1024]{1,0:T(8,128)(4,1)S(1)} %fusion.196, bf16[512,16,64]{0,2,1:T(8,128)(2,1)S(1)} %bitcast.228, bf16[1024,16,64]{0,2,1:T(8,128)(2,1)S(1)} %copy-done.1), kind=kOutput, calls=%fused_computation.3.clone.1 | convolution fusion | flops 1098899456 | bytes 37257216 | tf_op jit(solution)/shard_map/while/body/eval_jaxpr/while/body/eval_jaxpr/qhd,khd->hqk/dot_general | solution.py:58
  193.0 15.1 %fusion.199 = f32[16,512]{1,0:T(8,128)S(1)} fusion(f32[16,512,1024]{2,1,0:T(8,128)} %get-tuple-element.630, f32[16,512]{1,0:T(8,128)S(1)} %max.16, pred[512,1024]{1,0:T(8,128)(4,1)S(1)} %fusion.196), kind=kLoop, calls=%fused_computation.4.clone.1 | loop fusion | flops 33546240 | bytes 34144256 | tf_op jit(solution)/shard_map/while/body/eval_jaxpr/while/body/eval_jaxpr/reduce_sum | solution.py:87
  208.8 16.3 %fusion.201 = f32[16,512,64]{1,2,0:T(8,128)S(1)} fusion(bf16[1024,16,64]{0,2,1:T(8,128)(2,1)S(1)} %copy-done.7, f32[16,512,1024]{2,1,0:T(8,128)} %get-tuple-element.630, f32[16,512]{1,0:T(8,128)S(1)} %get-tuple-element.634, f32[16,512]{1,0:T(8,128)S(1)} %max.16, pred[512,1024]{1,0:T(8,128)(4,1)S(1)} %fusion.196), kind=kOutput, calls=%fused_computation.5.clone.1 | convolution fusion | flops 1115684864 | bytes 38338560 | tf_op jit(solution)/shard_map/while/body/eval_jaxpr/while/body/eval_jaxpr/hqk,khd->qhd/dot_general | solution.py:90
  229.1 5.8 fusion.100
  237.5 17.3 %fusion.55 = f32[1024,4096]{1,0:T(8,128)} fusion(bf16[1024,4096]{1,0:T(8,128)(2,1)} %all-gather.13.cloned.1.call-done, f32[1024,1024]{0,1:T(8,128)} %copy-done.12, f32[1024]{0:T(1024)S(1)} %bitcast.242, f32[1024]{0:T(1024)S(1)} %bitcast.238, f32[1024]{0:T(1024)S(1)} %fusion.82, f32[1024]{0:T(1024)S(1)} %broadcast_multiply_fusion), kind=kOutput, calls=%fused_computation.95 | convolution fusion | flops 8595177472 | bytes 29376512 | tf_op jit(solution)/shard_map/dot_general | solution.py:251
  254.8 44.2 %all-gather.15.cloned.1.call-done = bf16[4096,1024]{1,0:T(8,128)(2,1)} async-done(((bf16[128,1024]{1,0:T(8,128)(2,1)}), bf16[4096,1024]{1,0:T(8,128)(2,1)}) %all-gather.15.cloned.1.call-update) | async-done | bytes 8388624 | tf_op jit(solution)/shard_map/all_gather | solution.py:224
  299.0 30.2 %multiply_reduce_fusion.2 = (f32[1024]{0:T(1024)S(1)}, f32[1024,1024]{0,1:T(8,128)}) fusion(f32[1024,1024]{0,1:T(8,128)} %copy-done.12, f32[1024]{0:T(1024)S(1)} %bitcast.239, f32[1024]{0:T(1024)S(1)} %broadcast_multiply_fusion, bf16[1024,4096]{1,0:T(8,128)(2,1)} %all-gather.13.cloned.1.call-done, f32[1024,4096]{1,0:T(8,128)} %fusion.55, ...), kind=kOutput, calls=%fused_computation.86 | convolution fusion | flops 17272143872 | bytes 44068864 | tf_op jit(solution)/shard_map/dot_general | solution.py:21
  329.2 4.7 fusion.94
  333.9 3.7 fusion.75
  337.7 250.4 %while.53 = (s32[]{:T(128)}, f32[1024,16,64]{0,2,1:T(8,128)}, f32[1024,16,64]{0,2,1:T(8,128)}, f32[10,16,64]{2,0,1:T(8,128)S(1)}, f32[10,16,64]{2,0,1:T(8,128)},...) while((s32[]{:T(128)}, f32[1024,16,64]{0,2,1:T(8,128)}, ...), condition=%wide.region_17.18_spmd.clone, body=%wide.region_14.17_spmd.clone.sunk | while | flops 5556054528 | bytes 357345792 | solution.py:176
  343.3 2.5 constant_dynamic-slice_fusion.8
  348.5 2.0 constant_dynamic-slice_fusion.7
  352.3 13.1 %fusion.222 = f32[16,512,1024]{2,1,0:T(8,128)} fusion(bf16[512,16,64]{0,2,1:T(8,128)(2,1)S(1)} %bitcast.220, bf16[1024,16,64]{0,2,1:T(8,128)(2,1)S(1)} %copy-done.2), kind=kOutput, calls=%fused_computation.155.clone.1 | convolution fusion | flops 1073741824 | bytes 36700160 | tf_op jit(solution)/shard_map/while/body/eval_jaxpr/while/body/eval_jaxpr/qhd,khd->hqk/dot_general | solution.py:58
  365.4 17.5 %bitcast_add_fusion.5 = f32[1024,16,64]{0,2,1:T(8,128)} fusion(f32[1024,16,64]{0,2,1:T(8,128)} %get-tuple-element.714, bf16[512,16,64]{0,2,1:T(8,128)(2,1)} %bitcast.224, f32[16,512,1024]{2,1,0:T(8,128)} %fusion.222, f32[16,512]{1,0:T(8,128)S(1)} %dynamic-slice_bitcast_fusion.2, pred[512,1024]{1,0:T(8,128)(4,1)} %fusion.223, pred[]{:T(512)S(6)} %compare.3), kind=kOutput, calls=%fused_computation.27.clone.1 | convolution fusion | flops 1109393408 | bytes 43548672 | tf_op jit(solution)/shard_map/while/body/eval_jaxpr/while/body/eval_jaxpr/hqk,qhd->khd/dot_general | solution.py:151
  383.0 26.0 %multiply_reduce_fusion.6 = (f32[16,512]{1,0:T(8,128)S(1)}, f32[16,512,1024]{2,1,0:T(8,128)}) fusion(f32[16,512,1024]{2,1,0:T(8,128)} %fusion.222, f32[16,512]{1,0:T(8,128)S(1)} %dynamic-slice_bitcast_fusion.2, pred[512,1024]{1,0:T(8,128)(4,1)} %fusion.223, bf16[512,16,64]{0,2,1:T(8,128)(2,1)} %bitcast.225, bf16[1024,16,64]{0,2,1:T(8,128)(2,1)} %get-tuple-element.742), kind=kOutput, calls=%fused_computation.22.clone.1 | convolution fusion | flops 1115676672 | bytes 70844416 | tf_op jit(solution)/shard_map/while/body/eval_jaxpr/while/body/eval_jaxpr/qhd,khd->hqk/dot_general | solution.py:125
  408.9 27.9 %multiply_convert_fusion.8 = bf16[16,512,1024]{2,1,0:T(8,128)(2,1)} fusion(f32[16,512,1024]{2,1,0:T(8,128)} %get-tuple-element.651, f32[16,512,1024]{2,1,0:T(8,128)} %fusion.222, f32[16,512]{1,0:T(8,128)S(1)} %add.416, f32[16,512]{1,0:T(8,128)S(1)} %dynamic-slice_bitcast_fusion.2, pred[512,1024]{1,0:T(8,128)(4,1)} %fusion.223), kind=kLoop, calls=%fused_computation.21.clone.1 | loop fusion | flops 50331648 | bytes 84475904 | tf_op jit(solution)/shard_map/while/body/eval_jaxpr/while/body/eval_jaxpr/convert_element_type | solution.py:134
  438.6 9.5 %fusion.227 = f32[16,512,64]{1,2,0:T(8,128)S(1)} fusion(bf16[16,512,1024]{2,1,0:T(8,128)(2,1)} %multiply_convert_fusion.8, bf16[1024,16,64]{0,2,1:T(8,128)(2,1)} %get-tuple-element.739), kind=kOutput, calls=%fused_computation.157.clone.1 | convolution fusion | flops 1073741824 | bytes 20971520 | tf_op jit(solution)/shard_map/while/body/eval_jaxpr/while/body/eval_jaxpr/hqk,khd->qhd/dot_general | solution.py:136
  448.1 9.3 %bitcast_add_fusion.4 = f32[1024,16,64]{0,2,1:T(8,128)S(1)} fusion(f32[1024,16,64]{0,2,1:T(8,128)S(1)} %copy-done.5, bf16[512,16,64]{0,2,1:T(8,128)(2,1)S(1)} %bitcast.222, bf16[16,512,1024]{2,1,0:T(8,128)(2,1)} %multiply_convert_fusion.8, pred[]{:T(512)S(6)} %compare.3), kind=kOutput, calls=%fused_computation.28.clone.1 | convolution fusion | flops 1076887552 | bytes 26214400 | tf_op jit(solution)/shard_map/while/body/eval_jaxpr/while/body/eval_jaxpr/hqk,qhd->khd/dot_general | solution.py:148
  467.6 2.5 constant_dynamic-slice_fusion.8
  476.5 13.1 %fusion.222 = f32[16,512,1024]{2,1,0:T(8,128)} fusion(bf16[512,16,64]{0,2,1:T(8,128)(2,1)S(1)} %bitcast.220, bf16[1024,16,64]{0,2,1:T(8,128)(2,1)S(1)} %copy-done.2), kind=kOutput, calls=%fused_computation.155.clone.1 | convolution fusion | flops 1073741824 | bytes 36700160 | tf_op jit(solution)/shard_map/while/body/eval_jaxpr/while/body/eval_jaxpr/qhd,khd->hqk/dot_general | solution.py:58
  489.7 18.8 %bitcast_add_fusion.5 = f32[1024,16,64]{0,2,1:T(8,128)} fusion(f32[1024,16,64]{0,2,1:T(8,128)} %get-tuple-element.714, bf16[512,16,64]{0,2,1:T(8,128)(2,1)} %bitcast.224, f32[16,512,1024]{2,1,0:T(8,128)} %fusion.222, f32[16,512]{1,0:T(8,128)S(1)} %dynamic-slice_bitcast_fusion.2, pred[512,1024]{1,0:T(8,128)(4,1)} %fusion.223, pred[]{:T(512)S(6)} %compare.3), kind=kOutput, calls=%fused_computation.27.clone.1 | convolution fusion | flops 1109393408 | bytes 43548672 | tf_op jit(solution)/shard_map/while/body/eval_jaxpr/while/body/eval_jaxpr/hqk,qhd->khd/dot_general | solution.py:151
  508.4 26.0 %multiply_reduce_fusion.6 = (f32[16,512]{1,0:T(8,128)S(1)}, f32[16,512,1024]{2,1,0:T(8,128)}) fusion(f32[16,512,1024]{2,1,0:T(8,128)} %fusion.222, f32[16,512]{1,0:T(8,128)S(1)} %dynamic-slice_bitcast_fusion.2, pred[512,1024]{1,0:T(8,128)(4,1)} %fusion.223, bf16[512,16,64]{0,2,1:T(8,128)(2,1)} %bitcast.225, bf16[1024,16,64]{0,2,1:T(8,128)(2,1)} %get-tuple-element.742), kind=kOutput, calls=%fused_computation.22.clone.1 | convolution fusion | flops 1115676672 | bytes 70844416 | tf_op jit(solution)/shard_map/while/body/eval_jaxpr/while/body/eval_jaxpr/qhd,khd->hqk/dot_general | solution.py:125
  534.4 27.9 %multiply_convert_fusion.8 = bf16[16,512,1024]{2,1,0:T(8,128)(2,1)} fusion(f32[16,512,1024]{2,1,0:T(8,128)} %get-tuple-element.651, f32[16,512,1024]{2,1,0:T(8,128)} %fusion.222, f32[16,512]{1,0:T(8,128)S(1)} %add.416, f32[16,512]{1,0:T(8,128)S(1)} %dynamic-slice_bitcast_fusion.2, pred[512,1024]{1,0:T(8,128)(4,1)} %fusion.223), kind=kLoop, calls=%fused_computation.21.clone.1 | loop fusion | flops 50331648 | bytes 84475904 | tf_op jit(solution)/shard_map/while/body/eval_jaxpr/while/body/eval_jaxpr/convert_element_type | solution.py:134
  564.1 9.5 %fusion.227 = f32[16,512,64]{1,2,0:T(8,128)S(1)} fusion(bf16[16,512,1024]{2,1,0:T(8,128)(2,1)} %multiply_convert_fusion.8, bf16[1024,16,64]{0,2,1:T(8,128)(2,1)} %get-tuple-element.739), kind=kOutput, calls=%fused_computation.157.clone.1 | convolution fusion | flops 1073741824 | bytes 20971520 | tf_op jit(solution)/shard_map/while/body/eval_jaxpr/while/body/eval_jaxpr/hqk,khd->qhd/dot_general | solution.py:136
  573.6 9.3 %bitcast_add_fusion.4 = f32[1024,16,64]{0,2,1:T(8,128)S(1)} fusion(f32[1024,16,64]{0,2,1:T(8,128)S(1)} %copy-done.5, bf16[512,16,64]{0,2,1:T(8,128)(2,1)S(1)} %bitcast.222, bf16[16,512,1024]{2,1,0:T(8,128)(2,1)} %multiply_convert_fusion.8, pred[]{:T(512)S(6)} %compare.3), kind=kOutput, calls=%fused_computation.28.clone.1 | convolution fusion | flops 1076887552 | bytes 26214400 | tf_op jit(solution)/shard_map/while/body/eval_jaxpr/while/body/eval_jaxpr/hqk,qhd->khd/dot_general | solution.py:148
  589.3 5.7 fusion.103
  595.0 2.8 fusion.78
  597.9 4.7 convolution_convert_fusion
  602.6 18.8 %reduce-scatter.6.cloned.1.call-done = bf16[256,512]{0,1:T(8,128)(2,1)} async-done(((bf16[1024,512]{0,1:T(8,128)(2,1)}), bf16[256,512]{0,1:T(8,128)(2,1)}) %reduce-scatter.6.cloned.1.call-update) | async-done | bytes 262160 | tf_op jit(solution)/shard_map/reduce_scatter | solution.py:289
  621.5 34.6 %reduce-scatter.8.cloned.1.call-done = bf16[128,2048]{1,0:T(8,128)(2,1)} async-done(((bf16[512,2048]{1,0:T(8,128)(2,1)}), bf16[128,2048]{1,0:T(8,128)(2,1)}) %reduce-scatter.8.cloned.1.call-update) | async-done | bytes 524304 | tf_op jit(solution)/shard_map/reduce_scatter | solution.py:295
  656.1 2.5 convolution_convert_fusion.2
  660.6 73.9 %all-reduce.7.cloned.1.call-done = (bf16[256,512]{0,1:T(8,128)(2,1)}, bf16[128,2048]{1,0:T(8,128)(2,1)}) async-done(((bf16[256,512]{0,1:T(8,128)(2,1)}, bf16[128,2048]{1,0:T(8,128)(2,1)}), (bf16[256,512]{0,1:T(8,128)(2,1)}, bf16[128,2048]{1,0:T(8,128)(2,1)})) %all-reduce.7.cloned.1.call-update) | async-done | bytes 786448 | tf_op jit(solution)/shard_map/psum | solution.py:302
  734.6 17.3 %fusion.56 = bf16[1,1024,1024]{1,2,0:T(8,128)(2,1)} fusion(f32[1024,1024]{0,1:T(8,128)} %copy-done.12, f32[1024]{0:T(1024)S(1)} %copy-done.40, bf16[4096,1024]{1,0:T(8,128)(2,1)} %all-gather.15.cloned.1.call-done, f32[1024,4096]{1,0:T(8,128)} %fusion.55, f32[4096]{0:T(1024)S(1)} %copy-done.37), kind=kOutput, calls=%fused_computation.96 | convolution fusion | flops 8635023360 | bytes 31477760 | tf_op jit(solution)/shard_map/dot_general | solution.py:256
  751.9 3.9 copy.123
  755.9 3.8 convert.13
  759.7 3.9 copy.119
  763.7 4.0 convert.14
  767.7 3.9 copy.120
  771.7 11.3 %fusion.50 = (f32[1024]{0:T(1024)S(1)}, f32[1024,1024]{0,1:T(8,128)S(1)}) fusion(bf16[1,1024,1024]{1,2,0:T(8,128)(2,1)} %copy.105, f32[1024]{0:T(1024)S(1)} %bitcast.235, f32[1024]{0:T(1024)S(1)} %copy-done.24, bf16[1024,3072]{1,0:T(8,128)(2,1)} %all-gather.9.cloned.1.call-done, bf16[1024,1024]{1,0:T(8,128)(2,1)} %copy.120, bf16[1024,1024]{1,0:T(8,128)(2,1)} %copy.119, ...), kind=kOutput, calls=%fused_computation.83 | convolution fusion | flops 6466567168 | bytes 18886656 | tf_op jit(solution)/shard_map/dot_general | solution.py:21
  786.2 3.7 fusion.57
  789.9 3.9 copy.124
  793.8 5.7 all-reduce.4
  799.7 35.7 %all-reduce.2 = (bf16[10,256]{1,0:T(8,128)(2,1)S(1)}, bf16[128]{0:T(256)(128)(2,1)S(1)}, bf16[512]{0:T(512)(128)(2,1)S(1)}) all-reduce(bf16[10,256]{1,0:T(8,128)(2,1)} %reduce-scatter.4.cloned.1.call-done, f32[128]{0:T(128)S(1)} %dynamic-slice_convert_fusion.1, ...), channel_id=1, replica_groups=mesh['wide'=8,'narrow'=4] {'wide'}, use_global_device_ids=true, to_apply=%region_21.22 | all-reduce | flops 3200 | bytes 14080 | tf_op jit(solution)/shard_map/psum | solution.py:302
  835.4 5.0 all-gather
  841.0 5.1 all-gather.1
  846.7 5.2 all_gather.35
  852.6 2.6 copy.125
  855.1 4.1 convert_element_type.175
  (227 shorter events, 67.5 us)
Async XLA Ops:
  7.2 6.6 copy-start
  7.2 76.0 %all-gather.9.cloned.1.call-start = ((), (), s32[]{:S(2)}) async-start(), calls=%async_computation.3 | async-start | bytes 6488064 | tf_op jit(solution)/shard_map/all_gather | solution.py:221
  7.9 221.2 %all-gather.11.cloned.1.call-start = ((), (), s32[]{:S(2)}) async-start(), calls=%async_computation.4 | async-start | bytes 2162688 | tf_op jit(solution)/shard_map/all_gather | solution.py:222
  8.7 228.8 %all-gather.13.cloned.1.call-start = ((), (), s32[]{:S(2)}) async-start(), calls=%async_computation.5 | async-start | bytes 8650752 | tf_op jit(solution)/shard_map/all_gather | solution.py:223
  9.4 289.6 %all-gather.15.cloned.1.call-start = ((), (), s32[]{:S(2)}) async-start(), calls=%async_computation.6 | async-start | bytes 8650752 | tf_op jit(solution)/shard_map/all_gather | solution.py:224
  10.0 611.5 %reduce-scatter.6.cloned.1.call-start = ((), (), s32[]{:S(2)}) async-start(), calls=%async_computation.8 | async-start | bytes 1310720 | tf_op jit(solution)/shard_map/reduce_scatter | solution.py:289
  12.4 70.8 %copy-start.29 = (f32[1,1024]{1,0:T(1,128)}, f32[1,1024]{1,0:T(1,128)S(1)}, u32[]{:S(2)}) copy-start(f32[1,1024]{1,0:T(1,128)S(1)} %get-tuple-element.472) | copy-start | bytes 12292
  15.7 0.6 copy-start.20
  24.9 58.4 %copy-start.38 = (f32[3072]{0:T(1024)S(1)}, f32[3072]{0:T(1024)}, u32[]{:S(2)}) copy-start(f32[3072]{0:T(1024)} %param.29) | copy-start | bytes 36868
  26.9 67.0 %copy-start.23 = (f32[1024]{0:T(1024)}, f32[1024]{0:T(1024)S(1)}, u32[]{:S(2)}) copy-start(f32[1024]{0:T(1024)S(1)} %broadcast_multiply_fusion.1) | copy-start | bytes 12292
  29.1 64.8 %copy-start.25 = (f32[1024]{0:T(1024)}, f32[1024]{0:T(1024)S(1)}, u32[]{:S(2)}) copy-start(f32[1024]{0:T(1024)S(1)} %fusion.46) | copy-start | bytes 12292
  29.1 64.8 %copy-start.27 = (f32[1024]{0:T(1024)}, f32[1024]{0:T(1024)S(1)}, u32[]{:S(2)}) copy-start(f32[1024]{0:T(1024)S(1)} %fusion.81) | copy-start | bytes 12292
  93.9 2.8 copy-start.11
  115.6 113.5 %copy-start.39 = (f32[1024]{0:T(1024)S(1)}, f32[1024]{0:T(1024)}, u32[]{:S(2)}) copy-start(f32[1024]{0:T(1024)} %param.30) | copy-start | bytes 12292
  118.3 3.6 copy-start.1
  136.1 15.8 %copy-start.7 = (bf16[1024,16,64]{0,2,1:T(8,128)(2,1)S(1)}, bf16[1024,16,64]{0,2,1:T(8,128)(2,1)}, u32[]{:S(2)}) copy-start(bf16[1024,16,64]{0,2,1:T(8,128)(2,1)} %get-tuple-element.689) | copy-start | bytes 6291460 | tf_op jit(solution)/shard_map/while/body/eval_jaxpr/while
  174.4 3.5 copy-start.1
  193.0 15.8 %copy-start.7 = (bf16[1024,16,64]{0,2,1:T(8,128)(2,1)S(1)}, bf16[1024,16,64]{0,2,1:T(8,128)(2,1)}, u32[]{:S(2)}) copy-start(bf16[1024,16,64]{0,2,1:T(8,128)(2,1)} %get-tuple-element.689) | copy-start | bytes 6291460 | tf_op jit(solution)/shard_map/while/body/eval_jaxpr/while
  234.9 2.0 copy-start.12
  234.9 2.5 copy-start.31
  235.0 2.5 copy-start.34
  237.5 61.5 %copy-start.36 = (f32[4096]{0:T(1024)S(1)}, f32[4096]{0:T(1024)}, u32[]{:S(2)}) copy-start(f32[4096]{0:T(1024)} %param.31) | copy-start | bytes 49156
  329.2 4.7 copy-start.15
  329.2 4.7 copy-start.35
  333.9 3.8 copy-start.13
  333.9 3.8 copy-start.32
  333.9 3.8 copy-start.17
  337.7 251.6 %copy-start.21 = (f32[10,512]{1,0:T(8,128)S(1)}, f32[10,512]{1,0:T(8,128)}, u32[]{:S(2)}) copy-start(f32[10,512]{1,0:T(8,128)} %copy-done.20) | copy-start | bytes 61444
  347.3 1.0 copy-start.3
  347.3 3.6 copy-start.18
  347.3 5.0 copy-start.2
  348.5 2.7 copy-start.8
  348.5 2.3 copy-start.4
  350.8 0.8 copy-start.9
  351.6 0.7 copy-start.19
  438.6 9.5 %copy-start.5 = (f32[1024,16,64]{0,2,1:T(8,128)S(1)}, f32[1024,16,64]{0,2,1:T(8,128)}, u32[]{:S(2)}) copy-start(f32[1024,16,64]{0,2,1:T(8,128)} %get-tuple-element.713) | copy-start | bytes 12582916 | tf_op jit(solution)/shard_map/while/body/eval_jaxpr/while
  457.4 2.3 copy-start.6
  471.6 1.0 copy-start.3
  471.6 3.5 copy-start.18
  471.6 4.9 copy-start.2
  472.8 2.6 copy-start.8
  472.8 2.3 copy-start.4
  475.1 0.8 copy-start.9
  475.9 0.7 copy-start.19
  564.1 9.5 %copy-start.5 = (f32[1024,16,64]{0,2,1:T(8,128)S(1)}, f32[1024,16,64]{0,2,1:T(8,128)}, u32[]{:S(2)}) copy-start(f32[1024,16,64]{0,2,1:T(8,128)} %get-tuple-element.713) | copy-start | bytes 12582916 | tf_op jit(solution)/shard_map/while/body/eval_jaxpr/while
  582.9 2.3 copy-start.6
  588.1 6.9 copy-start.22
  597.8 60.9 %copy-start.41 = (u32[32]{0:T(128)S(1)}, u32[32]{0:T(128)}, u32[]{:S(2)}) copy-start(u32[32]{0:T(128)} %constant.129) | copy-start | bytes 388
  597.8 136.8 %copy-start.37 = (f32[4096]{0:T(1024)S(1)}, f32[4096]{0:T(1024)}, u32[]{:S(2)}) copy-start(f32[4096]{0:T(1024)} %param.31) | copy-start | bytes 49156
  597.8 136.8 %copy-start.40 = (f32[1024]{0:T(1024)S(1)}, f32[1024]{0:T(1024)}, u32[]{:S(2)}) copy-start(f32[1024]{0:T(1024)} %param.32) | copy-start | bytes 12292
  597.8 58.2 %reduce-scatter.8.cloned.1.call-start = ((), (), s32[]{:S(2)}) async-start(), calls=%async_computation.10 | async-start | bytes 2621440 | tf_op jit(solution)/shard_map/reduce_scatter | solution.py:295
  602.6 131.9 %all-reduce.7.cloned.1.call-start = ((), (), s32[]{:S(2)}) async-start(), calls=%async_computation.12 | async-start | bytes 1572864 | tf_op jit(solution)/shard_map/psum | solution.py:302
  656.1 143.6 %reduce-scatter.4.cloned.1.call-start = ((), (), s32[]{:S(2)}) async-start(), calls=%async_computation.7 | async-start | bytes 40960 | tf_op jit(solution)/shard_map/reduce_scatter | solution.py:286
  658.6 193.9 %all-gather.17.cloned.1.call-start = ((), (), s32[]{:S(2)}) async-start(), calls=%async_computation.9 | async-start | bytes 1310720 | tf_op jit(solution)/shard_map/all_gather | solution.py:309
  734.5 120.6 %all-gather.19.cloned.1.call-start = ((), (), s32[]{:S(2)}) async-start(), calls=%async_computation.11 | async-start | bytes 2621440 | tf_op jit(solution)/shard_map/all_gather | solution.py:315
  763.7 8.0 copy-start.24
  763.7 8.0 copy-start.30
  771.7 11.4 %copy-start.26 = (f32[1024]{0:T(1024)S(1)}, f32[1024]{0:T(1024)}, u32[]{:S(2)}) copy-start(f32[1024]{0:T(1024)} %copy-done.25) | copy-start | bytes 12292
  771.7 11.4 %copy-start.10 = (bf16[1,1024,1024]{1,2,0:T(8,128)(2,1)S(1)}, bf16[1,1024,1024]{1,2,0:T(8,128)(2,1)}, u32[]{:S(2)}) copy-start(bf16[1,1024,1024]{1,2,0:T(8,128)(2,1)} %copy.105) | copy-start | bytes 6291460
  771.7 11.4 %copy-start.28 = (f32[1024]{0:T(1024)S(1)}, f32[1024]{0:T(1024)}, u32[]{:S(2)}) copy-start(f32[1024]{0:T(1024)} %copy-done.27) | copy-start | bytes 12292
  783.0 2.5 copy-start.14
  783.0 3.2 copy-start.16
  783.0 3.2 copy-start.33
Sparse Core Ops, SparseCore 0:
  10.9 72.2 all-gather.8
  86.1 54.9 all-gather.10
  143.9 76.1 all-gather.12
  222.8 76.1 all-gather.14
  598.0 23.4 reduce-scatter.5
  624.6 31.4 reduce-scatter.7
  659.6 74.8 all-reduce.6
  737.6 18.3 reduce-scatter.3
  757.5 16.8 all-gather.16
  775.8 22.5 all-gather.18
where the time goes:
time: 876 us; the launch traced here: 866 us
  matrix products  341 us (39%)
  waiting for transfers between devices  224 us (26%)
  other arithmetic  126 us (14%)
  local copies, waits for them, and re-layouts  92 us (11%)
  blocking collectives  56.7 us (6%)
  between operations  16.2 us (2%)
  loops' own time  8.98 us (1%)
    psum x1, waiting for transfers between devices, shards(): lax.psum((embed_share, in_share, in_bias_share, out_share, out_bias_share...  73.9 us
    convert_element_type x2, other arithmetic, one_block(): (token_probs * (token_dprob - prob_inner[..., None])).astype(jnp.bfloat16)  55.9 us
    dot_general x4, matrix products, block_scores(): jnp.einsum('qhd,khd->hqk', queries, key_heads, preferred_element_type=jnp...  55.3 us
    dot_general x2, matrix products, one_block(): jnp.einsum('qhd,khd->hqk', grad_heads, value_heads, preferred_element_typ...  51.9 us
    all_gather x1, waiting for transfers between devices, shards(): lax.all_gather(mixer_weight, ('wide', 'narrow'), axis=0, tiled=True)  50.1 us
    dot_general x3, matrix products, times_transposed(): lax.dot_general(left_side, right_side, (((1,), (1,)), ((), ())), preferre...  45.2 us
    all_gather x1, waiting for transfers between devices, shards(): lax.all_gather(contract_weight, ('wide', 'narrow'), axis=0, tiled=True)  44.2 us
    dot_general x2, matrix products, one_block(): jnp.einsum('hqk,qhd->khd', token_probs.astype(jnp.bfloat16), grad_heads,...  36.3 us
  transfers between devices with their start and end apart: 10, of which 5 were waited for; matrix products, arithmetic and copies ran while one was open for 29% of the time, Pallas kernels for 0%

commit v1 on v0

v1 whole, which is shorter than its diff:
```python
import functools
from functools import partial

import jax
import jax.numpy as jnp
from jax import lax
from jax.experimental import pallas as pl
from jax.experimental.pallas import tpu as pltpu
from jax.sharding import PartitionSpec as P

MOST = 512


def norm_layer(values, norm_gain, norm_shift):
    center = values - jnp.mean(values, axis=-1, keepdims=True)
    spread = jnp.mean(center * center, axis=-1, keepdims=True)
    return center * lax.rsqrt(spread + 1e-05) * norm_gain + norm_shift


def times_transposed(left_side, right_side):
    return lax.dot_general(
        left_side, right_side, (((1,), (1,)), ((), ())), preferred_element_type=jnp.float32
    )


def reparam(embed_values, in_weight, in_shift, out_weight, out_shift):
    squashed = jnp.tanh(
        jnp.dot(embed_values, in_weight, precision=lax.Precision.HIGHEST) + in_shift
    )
    return jnp.dot(squashed, out_weight, precision=lax.Precision.HIGHEST) + out_shift


BLOCK = 256
PAD = 16
F32, BF16 = jnp.float32, jnp.bfloat16


def dot_nt(a, b):
    return lax.dot_general(a, b, (((1,), (1,)), ((), ())), preferred_element_type=F32)


def dot_nn(a, b):
    return lax.dot_general(a, b, (((1,), (0,)), ((), ())), preferred_element_type=F32)


def start_row(lengths_ref, count, length):
    place = lax.broadcasted_iota(jnp.int32, (1, length), 1)
    start = jnp.zeros((1, length), jnp.int32)
    total = jnp.int32(0)
    for j in range(count):
        total = total + lengths_ref[0, j]
        start = jnp.where(place >= total, total, start)
    return start


def visible(start, first_key, keys, first_query, queries, diagonal):
    key = lax.broadcasted_iota(jnp.int32, (keys, queries), 0) + first_key
    seen = key >= start
    if diagonal:
        query = lax.broadcasted_iota(jnp.int32, (keys, queries), 1) + first_query
        seen = seen & (key <= query)
    return seen


def span(qi, most):
    return max(0, qi - most // BLOCK)


def fwd_pair(q2, k_ref, v_ref, pk, pv, start, prefix, most, o_ref, lse_ref):
    length = q2.shape[0]
    lane = lax.broadcasted_iota(jnp.int32, (1, 128), 1)
    pre_seen = lax.broadcasted_iota(jnp.int32, (PAD, BLOCK), 0) < prefix
    v_t = v_ref[...].T
    pv_t = pv.T
    for qi in range(length // BLOCK):
        rows = slice(qi * BLOCK, (qi + 1) * BLOCK)
        lo = span(qi, most)
        st = start[:, rows]
        halves = []
        for h in range(2):
            qh = jnp.where((lane // 64) == h, q2[rows], jnp.zeros((), BF16))
            s_pre = jnp.where(pre_seen, dot_nt(pk, qh), -1e30)
            peak = jnp.max(s_pre, axis=0, keepdims=True)
            parts = []
            for kj in range(lo, qi + 1):
                s = dot_nt(k_ref[kj * BLOCK:(kj + 1) * BLOCK, :], qh)
                s = jnp.where(visible(st, kj * BLOCK, BLOCK, qi * BLOCK, BLOCK, kj == qi), s, -1e30)
                peak = jnp.maximum(peak, jnp.max(s, axis=0, keepdims=True))
                parts.append(s)
            p = jnp.exp(s_pre - peak)
            total = jnp.sum(p, axis=0, keepdims=True)
            o = dot_nn(pv_t[h * 64:(h + 1) * 64], p.astype(BF16))
            for n, kj in enumerate(range(lo, qi + 1)):
                p = jnp.exp(parts[n] - peak)
                total = total + jnp.sum(p, axis=0, keepdims=True)
                o = o + dot_nn(v_t[h * 64:(h + 1) * 64, kj * BLOCK:(kj + 1) * BLOCK], p.astype(BF16))
            halves.append(o / total)
            lse_ref[h:h + 1, rows] = peak + jnp.log(total)
        o_ref[rows, :] = jnp.concatenate(halves, axis=0).T.astype(BF16)


def fwd_kernel(prefix, most, count, len_ref, q_ref, k_ref, v_ref, pk_ref, pv_ref, o_ref, lse_ref):
    start = start_row(len_ref, count, q_ref.shape[0])
    q2 = q_ref[...] * jnp.asarray(0.125, BF16)
    fwd_pair(q2, k_ref, v_ref, pk_ref[...], pv_ref[...], start, prefix, most, o_ref, lse_ref.at[0])


def attend(mixed, lengths, pre, prefix, most):
    length, width = mixed.shape[0], mixed.shape[1] // 3
    pairs = width // 128
    count = lengths.shape[1]
    col = lambda off: pl.BlockSpec((length, 128), lambda p: (0, p + off))
    pcol = lambda off: pl.BlockSpec((PAD, 128), lambda p: (0, p + off))
    return pl.pallas_call(
        functools.partial(fwd_kernel, prefix, most, count),
        grid=(pairs,),
        in_specs=[pl.BlockSpec(memory_space=pltpu.SMEM), col(0), col(pairs), col(2 * pairs), pcol(0), pcol(pairs)],
        out_specs=[col(0), pl.BlockSpec((1, 2, length), lambda p: (p, 0, 0))],
        out_shape=[jax.ShapeDtypeStruct((length, width), BF16), jax.ShapeDtypeStruct((pairs, 2, length), F32)],
        compiler_params=pltpu.CompilerParams(vmem_limit_bytes=48 << 20),
        name="attend",
    )(lengths, mixed, mixed, mixed, pre, pre)


def bwd_kernel(prefix, most, count, len_ref, q_ref, k_ref, v_ref, pk_ref, pv_ref, do_ref, o_ref, lse_ref,
               dq_ref, dk_ref, dv_ref, dpk_ref, dpv_ref, dk_acc, dv_acc):
    length = q_ref.shape[0]
    start = start_row(len_ref, count, length)
    lane = lax.broadcasted_iota(jnp.int32, (1, 128), 1)
    pre_seen = lax.broadcasted_iota(jnp.int32, (PAD, BLOCK), 0) < prefix
    pk, pv = pk_ref[...], pv_ref[...]
    k_t = k_ref[...].T
    pk_t = pk.T
    head_of = lax.broadcasted_iota(jnp.int32, (8, 128), 0)
    pick = ((lax.broadcasted_iota(jnp.int32, (8, 128), 1) // 64) == head_of).astype(F32).astype(BF16)
    for qi in range(length // BLOCK):
        rows = slice(qi * BLOCK, (qi + 1) * BLOCK)
        lo = span(qi, most)
        st = start[:, rows]
        q2 = q_ref[rows, :] * jnp.asarray(0.125, BF16)
        do2 = do_ref[rows, :]
        prod = do2.astype(F32) * o_ref[rows, :].astype(F32)
        high = prod.astype(BF16)
        low = (prod - high.astype(F32)).astype(BF16)
        delta2 = dot_nt(pick, high) + dot_nt(pick, low)
        halves = []
        for h in range(2):
            mine = (lane // 64) == h
            qh = jnp.where(mine, q2, jnp.zeros((), BF16))
            doh = jnp.where(mine, do2, jnp.zeros((), BF16))
            lse = lse_ref[0, h:h + 1, rows]
            delta = delta2[h:h + 1]
            p = jnp.where(pre_seen, jnp.exp(dot_nt(pk, qh) - lse), 0.0)
            ds = (p * (dot_nt(pv, doh) - delta)).astype(BF16)
            dpk = dot_nn(ds, qh)
            dpv = dot_nn(p.astype(BF16), doh)
            if qi == 0 and h == 0:
                dpk_ref[...], dpv_ref[...] = dpk, dpv
            else:
                dpk_ref[...] += dpk
                dpv_ref[...] += dpv
            dq = dot_nn(pk_t[h * 64:(h + 1) * 64], ds)
            for kj in range(lo, qi + 1):
                keys = slice(kj * BLOCK, (kj + 1) * BLOCK)
                s = dot_nt(k_ref[keys, :], qh)
                p = jnp.exp(s - lse)
                p = jnp.where(visible(st, kj * BLOCK, BLOCK, qi * BLOCK, BLOCK, kj == qi), p, 0.0)
                dp = dot_nt(v_ref[keys, :], doh)
                ds = (p * (dp - delta)).astype(BF16)
                dv = dot_nn(p.astype(BF16), doh)
                dk = dot_nn(ds, qh)
                if kj == qi and h == 0:
                    dv_acc[keys, :], dk_acc[keys, :] = dv, dk
                else:
                    dv_acc[keys, :] += dv
                    dk_acc[keys, :] += dk
                dq = dq + dot_nn(k_t[h * 64:(h + 1) * 64, keys], ds)
            halves.append(dq * 0.125)
        dq_ref[rows, :] = jnp.concatenate(halves, axis=0).T.astype(BF16)
    dk_ref[...] = dk_acc[...].astype(BF16)
    dv_ref[...] = dv_acc[...].astype(BF16)


def attend_back(mixed, lengths, pre, grad, attended, lse, prefix, most):
    length, width = grad.shape
    pairs = width // 128
    count = lengths.shape[1]
    col = lambda off: pl.BlockSpec((length, 128), lambda p: (0, p + off))
    pcol = lambda off: pl.BlockSpec((PAD, 128), lambda p: (0, p + off))
    return pl.pallas_call(
        functools.partial(bwd_kernel, prefix, most, count),
        grid=(pairs,),
        in_specs=[pl.BlockSpec(memory_space=pltpu.SMEM), col(0), col(pairs), col(2 * pairs), pcol(0), pcol(pairs),
                  col(0), col(0), pl.BlockSpec((1, 2, length), lambda p: (p, 0, 0))],
        out_specs=[col(0), col(0), col(0), pcol(0), pcol(0)],
        out_shape=[jax.ShapeDtypeStruct((length, width), BF16)] * 3 + [jax.ShapeDtypeStruct((PAD, width), F32)] * 2,
        scratch_shapes=[pltpu.VMEM((length, 128), F32)] * 2,
        compiler_params=pltpu.CompilerParams(vmem_limit_bytes=48 << 20),
        name="attend_back",
    )(lengths, mixed, mixed, mixed, pre, pre, grad, attended, lse)


def shards(
    tokens,
    lengths,
    cotangent,
    mixer_weight,
    output_weight,
    expand_weight,
    contract_weight,
    mixer_bias,
    output_bias,
    expand_bias,
    contract_bias,
    norm_gains,
    norm_shifts,
    prefix_embed,
    reparam_in,
    reparam_in_bias,
    reparam_out,
    reparam_out_bias,
):
    row_count, length, model_width = tokens.shape
    total_rows = row_count * length
    full_mixer, full_output, full_expand, full_contract = (
        lax.all_gather(mixer_weight, ("wide", "narrow"), axis=0, tiled=True),
        lax.all_gather(output_weight, ("wide", "narrow"), axis=0, tiled=True),
        lax.all_gather(expand_weight, ("wide", "narrow"), axis=0, tiled=True),
        lax.all_gather(contract_weight, ("wide", "narrow"), axis=0, tiled=True),
    )
    prefix_kv, reparam_back = jax.vjp(
        reparam, prefix_embed, reparam_in, reparam_in_bias, reparam_out, reparam_out_bias
    )
    prefix_low = prefix_kv.astype(jnp.bfloat16)
    inputs = tokens.reshape(total_rows, model_width).astype(jnp.float32)
    normed_one, norm_one_back = jax.vjp(
        lambda values: norm_layer(values, norm_gains[0], norm_shifts[0]), inputs
    )
    mixed = (
        jnp.dot(normed_one.astype(jnp.bfloat16), full_mixer, preferred_element_type=jnp.float32)
        + mixer_bias
    )
    mixed_low = mixed.astype(jnp.bfloat16)
    prefix_count = prefix_low.shape[0]
    pre = jnp.pad(prefix_low, ((0, PAD - prefix_count), (0, 0)))
    row_of = lambda array, row: array[row * length : (row + 1) * length]
    forward = [
        attend(row_of(mixed_low, row), lengths[row : row + 1], pre, prefix_count, MOST)
        for row in range(row_count)
    ]
    attended = jnp.concatenate([item[0] for item in forward], axis=0)
    middle = inputs + (
        jnp.dot(attended, full_output, preferred_element_type=jnp.float32) + output_bias
    )
    normed_two, norm_two_back = jax.vjp(
        lambda values: norm_layer(values, norm_gains[1], norm_shifts[1]), middle
    )
    expanded = (
        jnp.dot(normed_two.astype(jnp.bfloat16), full_expand, preferred_element_type=jnp.float32)
        + expand_bias
    )
    activated, gelu_back = jax.vjp(partial(jax.nn.gelu, approximate=True), expanded)
    result = middle + (
        jnp.dot(activated.astype(jnp.bfloat16), full_contract, preferred_element_type=jnp.float32)
        + contract_bias
    )
    out_tokens = result.astype(jnp.bfloat16).reshape(row_count, length, model_width)
    back_mixer, back_output, back_expand, back_contract = (
        lax.all_gather(mixer_weight, ("wide", "narrow"), axis=0, tiled=True),
        lax.all_gather(output_weight, ("wide", "narrow"), axis=0, tiled=True),
        lax.all_gather(expand_weight, ("wide", "narrow"), axis=0, tiled=True),
        lax.all_gather(contract_weight, ("wide", "narrow"), axis=0, tiled=True),
    )
    grad_result = cotangent.reshape(total_rows, model_width)
    grad_activated = times_transposed(grad_result, back_contract)
    grad_expanded = gelu_back(grad_activated)[0].astype(jnp.bfloat16)
    grad_normed_two = times_transposed(grad_expanded, back_expand)
    grad_middle = grad_result.astype(jnp.float32) + norm_two_back(grad_normed_two)[0]
    grad_attended = times_transposed(grad_middle.astype(jnp.bfloat16), back_output).astype(
        jnp.bfloat16
    )
    back = [
        attend_back(
            row_of(mixed_low, row), lengths[row : row + 1], pre, row_of(grad_attended, row),
            forward[row][0], forward[row][1], prefix_count, MOST,
        )
        for row in range(row_count)
    ]
    grad_mixed = jnp.concatenate(
        [jnp.concatenate([item[part] for item in back], axis=0) for part in range(3)], axis=1
    )
    grad_prefix = jnp.concatenate(
        [sum(item[part] for item in back)[:prefix_count] for part in (3, 4)], axis=1
    )
    grad_prefix = lax.psum(grad_prefix, ("wide", "narrow"))
    grad_normed_one = times_transposed(grad_mixed, back_mixer)
    grad_inputs = (grad_middle + norm_one_back(grad_normed_one)[0]).astype(jnp.bfloat16)
    grad_inputs = grad_inputs.reshape(row_count, length, model_width)
    grad_embed, grad_in, grad_in_bias, grad_out, grad_out_bias = reparam_back(grad_prefix)
    return (out_tokens, grad_inputs, grad_embed, grad_in, grad_in_bias, grad_out, grad_out_bias)


def solution(mesh):
    return jax.shard_map(
        shards,
        mesh=mesh,
        in_specs=(
            P(("wide", "narrow"), None, None),
            P(("wide", "narrow"), None),
            P(("wide", "narrow"), None, None),
            P(("wide", "narrow"), None),
            P(("wide", "narrow"), None),
            P(("wide", "narrow"), None),
            P(("wide", "narrow"), None),
            P(),
            P(),
            P(),
            P(),
            P(),
            P(),
            P(),
            P(),
            P(),
            P(),
            P(),
        ),
        out_specs=(
            P(("wide", "narrow"), None, None),
            P(("wide", "narrow"), None, None),
            P(),
            P(),
            P(),
            P(),
            P(),
        ),
        check_vma=False,
    )
```

time: 876 us -> 547 us (0.62)
  matrix products: 341 us -> 120 us
  other arithmetic: 126 us -> 15.3 us
  Pallas kernels: 0 us -> 78.3 us
  local copies, waits for them, and re-layouts: 92 us -> 25.7 us
  waiting for transfers between devices: 224 us -> 285 us
  blocking collectives: 56.7 us -> 0 us
  loops' own time: 8.98 us -> 0 us
    dot_general x28 -> x0, matrix products: 223 us -> none  [the longest x4 55.3 us: block_scores(): jnp.einsum('qhd,khd->hqk', queries, key_heads, preferred_element_type=jnp...]
    pallas_call x0 -> x2, Pallas kernels: none -> 78.3 us  [the longest x1 48.9 us: attend_back(): pl.pallas_call(functools.partial(bwd_kernel, prefix, most, count), grid=(...]
    all_gather x1, waiting for transfers between devices: 0.02 us -> 71.1 us  [shards(): lax.all_gather(expand_weight, ('wide', 'narrow'), axis=0, tiled=True)]
    convert_element_type x10 -> x0, other arithmetic: 64.6 us -> none  [the longest x2 55.9 us: one_block(): (token_probs * (token_dprob - prob_inner[..., None])).astype(jnp.bfloat16)]
    reduce_scatter x3 -> x0, waiting for transfers between devices: 53.4 us -> none  [the longest x1 34.6 us: shards(): lax.psum_scatter(out_part.astype(jnp.bfloat16), 'narrow', scatter_dimensi...]
    psum x1 -> x0, blocking collectives: 35.7 us -> none  [shards(): lax.psum((embed_share, in_share, in_bias_share, out_share, out_bias_share...]
    reduce_sum x5 -> x0, other arithmetic: 30.7 us -> none  [the longest x4 30.6 us: one_block(): weight_sum = jnp.sum(token_probs, axis=-1) + jnp.sum(prefix_probs, axis=-1)]
    all_gather x1, waiting for transfers between devices: 44.2 us -> 62.1 us  [shards(): lax.all_gather(contract_weight, ('wide', 'narrow'), axis=0, tiled=True)]
  transfers between devices with their start and end apart: 10 -> 5, of which waited for: 5 -> 5; matrix products, arithmetic and copies ran while one was open for 29% -> 18% of each run, Pallas kernels for 0% -> 5%
where the time goes in v1:
time: 547 us; the launch traced here: 539 us
  waiting for transfers between devices  285 us (52%)
  matrix products  120 us (22%)
  Pallas kernels  78.3 us (14%)
  local copies, waits for them, and re-layouts  25.7 us (5%)
  other arithmetic  15.3 us (3%)
  between operations  14.3 us (3%)
    psum x1, waiting for transfers between devices, shards(): grad_prefix = lax.psum(grad_prefix, ('wide', 'narrow'))  75.5 us
    all_gather x1, waiting for transfers between devices, shards(): lax.all_gather(expand_weight, ('wide', 'narrow'), axis=0, tiled=True)  71.1 us
    all_gather x1, waiting for transfers between devices, shards(): lax.all_gather(contract_weight, ('wide', 'narrow'), axis=0, tiled=True)  62.1 us
    all_gather x1, waiting for transfers between devices, shards(): lax.all_gather(mixer_weight, ('wide', 'narrow'), axis=0, tiled=True)  58.7 us
    pallas_call x1, Pallas kernels, attend_back(): pl.pallas_call(functools.partial(bwd_kernel, prefix, most, count), grid=(...  48.9 us
    dot_general x3, matrix products, times_transposed(): lax.dot_general(left_side, right_side, (((1,), (1,)), ((), ())), preferre...  45.6 us
    pallas_call x1, Pallas kernels, attend(): pl.pallas_call(functools.partial(fwd_kernel, prefix, most, count), grid=(...  29.5 us
    unnamed x55, local copies, waits for them, and re-layouts  25.7 us
  transfers between devices with their start and end apart: 5, of which 5 were waited for; matrix products, arithmetic and copies ran while one was open for 18% of the time, Pallas kernels for 5%

profile of v1, /device:TPU:0, one launch (start us, length us, event | category | flops | bytes accessed | tf_op | source)
XLA Modules:
  0.0 539.0 jit_solution(2697272624740212413)
XLA Ops:
  7.2 0.0 copy-start
  7.2 0.0 all-gather.5.cloned.1.call-start
  7.2 0.7 all-gather.5.cloned.1.call-update
  7.9 0.0 all-gather.7.cloned.1.call-start
  8.0 0.7 all-gather.7.cloned.1.call-update
  8.7 0.0 all-gather.9.cloned.1.call-start
  8.7 0.7 all-gather.9.cloned.1.call-update
  9.4 0.0 all-gather.11.cloned.1.call-start
  9.4 0.5 all-gather.11.cloned.1.call-update
  10.0 0.0 copy-start.14
  10.0 0.0 all-reduce.3.cloned.1.call-start
  10.0 3.9 copy.25
  14.0 3.9 copy.27
  17.9 0.0 copy-start.5
  18.0 1.1 fusion.54
  19.1 0.0 copy-start.12
  19.1 0.0 copy-start.17
  19.1 0.0 copy-start.18
  19.1 0.0 copy-start.22
  19.1 4.3 fusion.28
  23.5 0.4 convert_reduce_fusion
  23.9 0.6 fusion.22
  24.5 0.0 copy-done.12
  24.5 0.0 copy-done.17
  24.5 58.7 %all-gather.5.cloned.1.call-done = bf16[1024,3072]{1,0:T(8,128)(2,1)} async-done(((bf16[32,3072]{1,0:T(8,128)(2,1)}), bf16[1024,3072]{1,0:T(8,128)(2,1)}) %all-gather.5.cloned.1.call-update) | async-done | bytes 6291472 | tf_op jit(solution)/shard_map/all_gather | solution.py:226
  83.3 0.0 copy-done.22
  83.3 12.2 %add_convert_fusion.q_ref.k_ref.v_ref = bf16[1024,3072]{1,0:T(8,128)(2,1)} fusion(f32[3072]{0:T(1024)S(1)} %copy-done.22, bf16[1024,3072]{1,0:T(8,128)(2,1)} %all-gather.5.cloned.1.call-done, bf16[1,1024,1024]{1,2,0:T(8,128)(2,1)} %copy.25, f32[1024]{0:T(1024)S(1)} %bitcast.91, f32[1024]{0:T(1024)S(1)} %bitcast.83, f32[1024]{0:T(1024)S(1)} %fusion.56, ...), kind=kOutput, calls=%fused_computation.10 | convolution fusion | flops 6455033856 | bytes 14708736 | tf_op jit(solution)/shard_map/dot_general | solution.py:240
  95.5 29.5 %attend.1 = (bf16[1024,1024]{1,0:T(8,128)(2,1)S(1)}, f32[8,2,1024]{2,1,0:T(2,128)S(1)}) custom-call(s32[1,8]{1,0:T(1,128)S(1)} %copy-done.2, bf16[1024,3072]{1,0:T(8,128)(2,1)} %add_convert_fusion.q_ref.k_ref.v_ref, bf16[1024,3072]{1,0:T(8,128)(2,1)} %add_convert_fusion.q_ref.k_ref.v_ref, bf16[1024,3072]{1,0:T(8,128)(2,1)} %add_convert_fusion.q_ref.k_ref.v_ref, ...), custom_call_target="tpu_custom_call" | custom-call | tf_op jit(solution)/shard_map/attend/pallas_call | solution.py:114
  125.0 0.0 copy-start.1
  125.0 1.3 copy-done.1
  126.3 14.7 %all-gather.7.cloned.1.call-done = bf16[1024,1024]{1,0:T(8,128)(2,1)} async-done(((bf16[32,1024]{1,0:T(8,128)(2,1)}), bf16[1024,1024]{1,0:T(8,128)(2,1)}) %all-gather.7.cloned.1.call-update) | async-done | bytes 2097168 | tf_op jit(solution)/shard_map/all_gather | solution.py:227
  141.1 0.0 copy-done.23
  141.1 5.7 %fusion.72 = (f32[1024]{0:T(1024)S(1)}, f32[1024,1024]{0,1:T(8,128)S(1)}) fusion(f32[1024]{0:T(1024)S(1)} %copy-done.23, bf16[1024,1024]{1,0:T(8,128)(2,1)} %copy-done.1, bf16[1024,1024]{1,0:T(8,128)(2,1)} %all-gather.7.cloned.1.call-done, bf16[1,1024,1024]{1,2,0:T(8,128)(2,1)} %copy.25), kind=kOutput, calls=%fused_computation.90 | convolution fusion | flops 2151676928 | bytes 10493952 | tf_op jit(solution)/shard_map/dot_general | solution.py:253
  146.7 0.0 copy-start.7
  146.8 2.0 copy-done.7
  148.7 0.5 multiply_reduce_fusion.1
  149.2 71.1 %all-gather.9.cloned.1.call-done = bf16[1024,4096]{1,0:T(8,128)(2,1)} async-done(((bf16[32,4096]{1,0:T(8,128)(2,1)}), bf16[1024,4096]{1,0:T(8,128)(2,1)}) %all-gather.9.cloned.1.call-update) | async-done | bytes 8388624 | tf_op jit(solution)/shard_map/all_gather | solution.py:228
  220.4 16.8 %fusion.31 = f32[1024,4096]{1,0:T(8,128)} fusion(bf16[1024,4096]{1,0:T(8,128)(2,1)} %all-gather.9.cloned.1.call-done, f32[1024,1024]{0,1:T(8,128)} %copy-done.7, f32[1024]{0:T(1024)S(1)} %bitcast.90, f32[1024]{0:T(1024)S(1)} %bitcast.87, f32[1024]{0:T(1024)S(1)} %fusion.57, f32[1024]{0:T(1024)S(1)} %broadcast_multiply_fusion), kind=kOutput, calls=%fused_computation.44 | convolution fusion | flops 8595177472 | bytes 29376512 | tf_op jit(solution)/shard_map/dot_general | solution.py:259
  237.2 62.1 %all-gather.11.cloned.1.call-done = bf16[4096,1024]{1,0:T(8,128)(2,1)} async-done(((bf16[128,1024]{1,0:T(8,128)(2,1)}), bf16[4096,1024]{1,0:T(8,128)(2,1)}) %all-gather.11.cloned.1.call-update) | async-done | bytes 8388624 | tf_op jit(solution)/shard_map/all_gather | solution.py:229
  299.3 30.6 %multiply_reduce_fusion = (f32[1024]{0:T(1024)S(1)}, f32[1024,1024]{0,1:T(8,128)}) fusion(f32[1024,1024]{0,1:T(8,128)} %copy-done.7, f32[1024]{0:T(1024)S(1)} %bitcast.88, f32[1024]{0:T(1024)S(1)} %broadcast_multiply_fusion, bf16[1024,4096]{1,0:T(8,128)(2,1)} %all-gather.9.cloned.1.call-done, f32[1024,4096]{1,0:T(8,128)} %fusion.31, ...), kind=kOutput, calls=%fused_computation.36 | convolution fusion | flops 17272143872 | bytes 44068864 | tf_op jit(solution)/shard_map/dot_general | solution.py:21
  329.9 0.0 copy-start.10
  329.9 4.7 fusion.69
  334.6 3.8 fusion.51.do_ref
  338.4 48.9 %attend_back.1 = (bf16[1024,1024]{1,0:T(8,128)(2,1)S(1)}, bf16[1024,1024]{1,0:T(8,128)(2,1)S(1)}, bf16[1024,1024]{1,0:T(8,128)(2,1)}, f32[16,1024]{1,0:T(8,128)S(1)}, f32[16,1024]{1,0:T(8,128)S(1)}) custom-call(s32[1,8]{1,0:T(1,128)S(1)} %copy-done.2, bf16[1024,3072]{1,0:T(8,128)(2,1)} %add_convert_fusion.q_ref.k_ref.v_ref, ...), custom_call_target="tpu_custom_call" | custom-call | tf_op jit(solution)/shard_map/attend_back/pallas_call | solution.py:190
  387.2 1.3 copy-done.3
  388.5 1.3 copy-done.4
  389.9 0.7 pad_maximum_fusion
  390.5 0.0 all-reduce.3.cloned.1.call-update
  390.6 0.0 copy-start.6
  390.6 11.3 %fusion.26 = (f32[1024]{0:T(1024)S(1)}, f32[1024,1024]{0,1:T(8,128)S(1)}) fusion(bf16[1,1024,1024]{1,2,0:T(8,128)(2,1)} %copy.25, f32[1024]{0:T(1024)S(1)} %bitcast.84, f32[1024]{0:T(1024)S(1)} %broadcast_multiply_fusion.1, bf16[1024,3072]{1,0:T(8,128)(2,1)} %all-gather.5.cloned.1.call-done, bf16[1024,1024]{1,0:T(8,128)(2,1)} %get-tuple-element.18, ...), kind=kOutput, calls=%fused_computation.33 | convolution fusion | flops 6466567168 | bytes 18886656 | tf_op jit(solution)/shard_map/dot_general | solution.py:21
  401.8 0.0 copy-start.24
  401.9 1.1 fusion.55
  403.0 0.8 copy-done.9
  403.8 17.5 %fusion.32 = bf16[1,1024,1024]{1,2,0:T(8,128)(2,1)} fusion(f32[1024,1024]{0,1:T(8,128)} %copy-done.7, f32[1024]{0:T(1024)S(1)} %copy-done.24, bf16[4096,1024]{1,0:T(8,128)(2,1)} %all-gather.11.cloned.1.call-done, f32[1024,4096]{1,0:T(8,128)} %fusion.31, f32[4096]{0:T(1024)S(1)} %copy-done.21), kind=kOutput, calls=%fused_computation.45 | convolution fusion | flops 8635023360 | bytes 31477760 | tf_op jit(solution)/shard_map/dot_general | solution.py:264
  421.3 6.7 %fusion.33 = bf16[1,1024,1024]{1,2,0:T(8,128)(2,1)} fusion(f32[1024,1024]{0,1:T(8,128)} %copy-done.8, bf16[1,1024,1024]{1,2,0:T(8,128)(2,1)} %copy.27, f32[1024]{0:T(1024)S(1)} %negate_multiply_fusion, f32[1024]{0:T(1024)S(1)} %negate_multiply_fusion.1, f32[1024]{0:T(1024)S(1)} %multiply_multiply_fusion.2, f32[1024]{0:T(1024)S(1)} %broadcast_multiply_fusion.1, ...), kind=kLoop, calls=%fused_computation.46 | loop fusion | flops 13631488 | bytes 14704640 | tf_op jit(solution)/shard_map/reshape | solution.py:298
  428.0 4.0 copy.29
  432.0 4.2 copy.28
  436.2 75.5 %all-reduce.3.cloned.1.call-done = f32[10,2048]{1,0:T(8,128)} async-done(((f32[10,2048]{1,0:T(8,128)}), f32[10,2048]{1,0:T(8,128)}) %all-reduce.3.cloned.1.call-update) | async-done | bytes 81936 | tf_op jit(solution)/shard_map/psum | solution.py:295
  511.7 6.3 %fusion.75 = (f32[512]{0:T(512)}, f32[10,512]{1,0:T(8,128)S(1)}) fusion(f32[10,512]{1,0:T(8,128)S(1)} %copy-done.13, f32[10,2048]{1,0:T(8,128)} %all-reduce.3.cloned.1.call-done, f32[512,2048]{1,0:T(8,128)} %param.34), kind=kOutput, calls=%fused_computation.91 | convolution fusion | flops 125854208 | bytes 4319232 | tf_op jit(solution)/shard_map/transpose(jvp())/dot_general | solution.py:30
  518.1 3.2 convolution_bitcast_fusion
  521.2 2.5 fusion.76
  523.7 2.9 copy.30
  526.6 5.0 fusion.77
  531.6 0.6 reduce_sum.104
  (40 shorter events, 0.1 us)
Async XLA Ops:
  7.2 10.8 %copy-start = (f32[1024,512]{1,0:T(8,128)S(1)}, f32[1024,512]{1,0:T(8,128)}, u32[]{:S(2)}) copy-start(f32[1024,512]{1,0:T(8,128)} %param.32) | copy-start | bytes 6291460
  7.2 76.1 %all-gather.5.cloned.1.call-start = ((), (), s32[]{:S(2)}) async-start(), calls=%async_computation | async-start | bytes 6488064 | tf_op jit(solution)/shard_map/all_gather | solution.py:226
  7.9 133.1 %all-gather.7.cloned.1.call-start = ((), (), s32[]{:S(2)}) async-start(), calls=%async_computation.1 | async-start | bytes 2162688 | tf_op jit(solution)/shard_map/all_gather | solution.py:227
  8.7 211.7 %all-gather.9.cloned.1.call-start = ((), (), s32[]{:S(2)}) async-start(), calls=%async_computation.2 | async-start | bytes 8650752 | tf_op jit(solution)/shard_map/all_gather | solution.py:228
  9.4 289.9 %all-gather.11.cloned.1.call-start = ((), (), s32[]{:S(2)}) async-start(), calls=%async_computation.3 | async-start | bytes 8650752 | tf_op jit(solution)/shard_map/all_gather | solution.py:229
  10.0 8.0 %copy-start.14 = (f32[10,1024]{1,0:T(8,128)S(1)}, f32[10,1024]{1,0:T(8,128)}, u32[]{:S(2)}) copy-start(f32[10,1024]{1,0:T(8,128)} %param.31) | copy-start | bytes 122884
  10.0 8.0 %copy-start.19 = (f32[512]{0:T(512)S(1)}, f32[512]{0:T(512)}, u32[]{:S(2)}) copy-start(f32[512]{0:T(512)} %param.33) | copy-start | bytes 6148
  10.0 501.7 %all-reduce.3.cloned.1.call-start = ((), (), s32[]{:S(2)}) async-start(), calls=%async_computation.4 | async-start | bytes 262144 | tf_op jit(solution)/shard_map/psum | solution.py:295
  14.0 5.1 copy-start.16
  17.9 5.5 %copy-start.5 = (bf16[1,1024,1024]{1,2,0:T(8,128)(2,1)S(1)}, bf16[1,1024,1024]{1,2,0:T(8,128)(2,1)}, u32[]{:S(2)}) copy-start(bf16[1,1024,1024]{1,2,0:T(8,128)(2,1)} %copy.25) | copy-start | bytes 6291460
  19.1 5.4 copy-start.12
  19.1 5.4 copy-start.17
  19.1 5.4 %copy-start.18 = (f32[2,1024]{1,0:T(2,128)S(1)}, f32[2,1024]{1,0:T(2,128)}, u32[]{:S(2)}) copy-start(f32[2,1024]{1,0:T(2,128)} %param.30) | copy-start | bytes 24580
  19.1 64.1 %copy-start.22 = (f32[3072]{0:T(1024)S(1)}, f32[3072]{0:T(1024)}, u32[]{:S(2)}) copy-start(f32[3072]{0:T(1024)} %param.25) | copy-start | bytes 36868
  83.3 12.2 %copy-start.2 = (s32[1,8]{1,0:T(1,128)S(1)}, s32[1,8]{1,0:T(1,128)}, u32[]{:S(2)}) copy-start(s32[1,8]{1,0:T(1,128)} %len_ref.3) | copy-start | bytes 100
  95.5 45.6 %copy-start.23 = (f32[1024]{0:T(1024)S(1)}, f32[1024]{0:T(1024)}, u32[]{:S(2)}) copy-start(f32[1024]{0:T(1024)} %param.26) | copy-start | bytes 12292
  125.0 1.3 copy-start.1
  146.7 2.0 copy-start.7
  220.4 78.9 %copy-start.21 = (f32[4096]{0:T(1024)S(1)}, f32[4096]{0:T(1024)}, u32[]{:S(2)}) copy-start(f32[4096]{0:T(1024)} %param.27) | copy-start | bytes 49156
  329.9 4.7 copy-start.10
  329.9 4.7 copy-start.20
  334.6 3.8 copy-start.8
  387.2 1.3 copy-start.3
  388.5 1.3 copy-start.4
  390.6 11.3 %copy-start.6 = (bf16[1,1024,1024]{1,2,0:T(8,128)(2,1)S(1)}, bf16[1,1024,1024]{1,2,0:T(8,128)(2,1)}, u32[]{:S(2)}) copy-start(bf16[1,1024,1024]{1,2,0:T(8,128)(2,1)} %copy.25) | copy-start | bytes 6291460
  401.8 1.9 copy-start.9
  401.8 1.9 copy-start.24
  428.0 83.7 %copy-start.13 = (f32[10,512]{1,0:T(8,128)S(1)}, f32[10,512]{1,0:T(8,128)}, u32[]{:S(2)}) copy-start(f32[10,512]{1,0:T(8,128)} %copy-done.12) | copy-start | bytes 61444
  432.0 86.1 %copy-start.15 = (f32[10,1024]{1,0:T(8,128)S(1)}, f32[10,1024]{1,0:T(8,128)}, u32[]{:S(2)}) copy-start(f32[10,1024]{1,0:T(8,128)} %param.31) | copy-start | bytes 122884
  518.1 8.5 %copy-start.11 = (f32[10,2048]{1,0:T(8,128)S(1)}, f32[10,2048]{1,0:T(8,128)}, u32[]{:S(2)}) copy-start(f32[10,2048]{1,0:T(8,128)} %all-reduce.3.cloned.1.call-done) | copy-start | bytes 245764
Sparse Core Ops, SparseCore 0:
  10.9 72.3 all-gather.4
  86.1 54.8 all-gather.6
  143.9 76.4 all-gather.8
  223.1 76.1 all-gather.10
  390.7 120.9 all-reduce.2

commit v2 on v1

--- a/solution.py
+++ b/solution.py
@@ -1,5 +1,5 @@
 import functools
-from functools import partial
+import math
 
 import jax
 import jax.numpy as jnp
@@ -200,7 +200,256 @@
     )(lengths, mixed, mixed, mixed, pre, pre, grad, attended, lse)
 
 
+MESH = pl.DeviceIdType.MESH
+CHUNKS = 8
+LAG = 2
+AHEAD = 3
+TILE = 256
+
+
+def grid_dims(mesh_shape):
+    wide, narrow = mesh_shape["wide"], mesh_shape["narrow"]
+    return (wide // 2, 2, narrow // 2, 2)
+
+
+class Gather:
+    def __init__(self, dims, families):
+        self.dims = dims
+        wide, narrow = lax.axis_index("wide"), lax.axis_index("narrow")
+        self.at = (wide // dims[1], lax.rem(wide, dims[1]), narrow // dims[3], lax.rem(narrow, dims[3]))
+        self.families = families
+
+    def device(self, dim, index):
+        at = list(self.at)
+        at[dim] = index
+        return (at[0] * self.dims[1] + at[1], at[2] * self.dims[3] + at[3])
+
+    def greet(self):
+        barrier = pltpu.get_barrier_semaphore()
+        count = 0
+        for dim, size in enumerate(self.dims):
+            for step in range(1, size):
+                peer = self.device(dim, lax.rem(self.at[dim] + step, size))
+                pl.semaphore_signal(barrier, inc=1, device_id=peer, device_id_type=MESH)
+                count += 1
+        pl.semaphore_wait(barrier, count)
+
+    def view(self, family, j, stage, index):
+        _, target, order, _, _, _ = family
+        done, dim = order[:stage], order[stage]
+        return target.at[
+            (j,) + tuple(slice(None) if d in done else (index if d == dim else self.at[d]) for d in range(4))
+        ]
+
+    def own(self, family, j):
+        source, target, _, _, _, own = family
+        return pltpu.make_async_copy(source.at[j], target.at[(j,) + self.at], own.at[j])
+
+    def start(self, j, stage):
+        for family in self.families:
+            source, _, order, send, recv, _ = family
+            dim = order[stage]
+            size = self.dims[dim]
+            if stage == 0:
+                self.own(family, j).start()
+            mine = self.view(family, j, stage, self.at[dim])
+            for step in range(1, size):
+                pltpu.make_async_remote_copy(
+                    src_ref=source.at[j] if stage == 0 else mine,
+                    dst_ref=mine,
+                    send_sem=send.at[j, stage],
+                    recv_sem=recv.at[j, stage],
+                    device_id=self.device(dim, lax.rem(self.at[dim] + step, size)),
+                    device_id_type=MESH,
+                ).start()
+
+    def whole(self, family, j, stage):
+        _, _, order, send, recv, _ = family
+        size = self.dims[order[stage]]
+        part = self.view(family, j, stage, pl.ds(0, size - 1))
+        return pltpu.make_async_remote_copy(
+            src_ref=part, dst_ref=part, send_sem=send.at[j, stage], recv_sem=recv.at[j, stage],
+            device_id=self.device(order[stage], lax.rem(self.at[order[stage]] + 1, size)), device_id_type=MESH,
+        )
+
+    def arrive(self, j, stage):
+        for family in self.families:
+            if stage == 0:
+                self.own(family, j).wait()
+            self.whole(family, j, stage).wait_recv()
+
+    def finish(self, count):
+        @pl.loop(0, count)
+        def _(j):
+            for family in self.families:
+                for stage in range(4):
+                    self.whole(family, j, stage).wait_send()
+
+    def tick(self, t, count):
+        @pl.when(t + AHEAD < count)
+        def _():
+            self.start(t + AHEAD, 0)
+
+        for stage in (2, 1, 0):
+            j = t - LAG * stage
+
+            @pl.when((j >= 0) & (j < count))
+            def _():
+                self.arrive(j, stage)
+                self.start(j, stage + 1)
+
+        j = t - LAG * 3
+
+        @pl.when((j >= 0) & (j < count))
+        def _():
+            self.arrive(j, 3)
+
+
+XY, YX = (0, 1, 2, 3), (0, 2, 1, 3)
+
+
+def norm_parts(values):
+    center = values - jnp.mean(values, axis=-1, keepdims=True)
+    rate = lax.rsqrt(jnp.mean(center * center, axis=-1, keepdims=True) + 1e-05)
+    return center * rate, rate
+
+
+def norm_back(hat, rate, grad, gain):
+    inner = grad * gain
+    return rate * (
+        inner - jnp.mean(inner, axis=-1, keepdims=True) - hat * jnp.mean(inner * hat, axis=-1, keepdims=True)
+    )
+
+
+ROOT = math.sqrt(2.0 / math.pi)
+
+
+def gelu_both(v):
+    square = v * v
+    th = jnp.tanh(ROOT * v * (1.0 + 0.044715 * square))
+    half = 0.5 * (1.0 + th)
+    slope = half + 0.5 * v * (1.0 - th * th) * (ROOT * (1.0 + 3 * 0.044715 * square))
+    return v * half, slope
+
+
+def ff_kernel(dims, x_hbm, cot_hbm, att_hbm, wo_hbm, e_hbm, c_hbm, bo_ref, be_ref, bc_ref, gain_ref, shift_ref,
+              out_hbm, gm_hbm, ga_hbm,
+              ew, cw, x, cot, att, wo, n2, mid, acc, gacc,
+              e_send, e_recv, e_own, c_send, c_recv, c_own, in_sems, out_sems):
+    length, width = x.shape
+    count = e_hbm.shape[0]
+    gather = Gather(dims, [(e_hbm, ew, XY, e_send, e_recv, e_own), (c_hbm, cw, YX, c_send, c_recv, c_own)])
+    loads = [
+        pltpu.make_async_copy(src, dst, in_sems.at[n])
+        for n, (src, dst) in enumerate(((x_hbm, x), (att_hbm, att), (wo_hbm, wo), (cot_hbm, cot)))
+    ]
+    for load in loads:
+        load.start()
+    gather.greet()
+    for j in range(min(AHEAD, count)):
+        gather.start(j, 0)
+    for load in loads:
+        load.wait()
+    gain, shift = gain_ref[...], shift_ref[...]
+    tiles = length // TILE
+
+    def rows_of(i):
+        return pl.ds(pl.multiple_of(i * TILE, TILE), TILE)
+
+    def before(i):
+        rows = rows_of(i)
+        value = x[rows, :].astype(F32) + (dot_nn(att[rows, :], wo[...]) + bo_ref[...])
+        mid[rows, :] = value
+        hat, _ = norm_parts(value)
+        n2[rows, :] = (hat * gain + shift).astype(BF16)
+        acc[rows, :] = jnp.zeros((TILE, width), F32)
+        gacc[rows, :] = jnp.zeros((TILE, width), F32)
+
+    def chunk(j):
+        e = ew.at[j]
+        c = cw.at[j]
+        bias = be_ref[pl.ds(j, 1), :]
+
+        @pl.loop(0, tiles)
+        def _(i):
+            rows = rows_of(i)
+            ev = e[...].reshape(width, -1)
+            cv = c[...].reshape(-1, width)
+            active, slope = gelu_both(dot_nn(n2[rows, :], ev) + bias)
+            grad = (dot_nt(cot[rows, :], cv) * slope).astype(BF16)
+            acc[rows, :] += dot_nn(active.astype(BF16), cv)
+            gacc[rows, :] += dot_nt(grad, ev)
+
+    @pl.loop(0, max(count + 3 * LAG, tiles))
+    def _(t):
+        gather.tick(t, count)
+
+        @pl.when(t < tiles)
+        def _():
+            before(t)
+
+        j = t - 3 * LAG
+
+        @pl.when((j >= 0) & (j < count))
+        def _():
+            chunk(j)
+
+    def stores(i):
+        rows = rows_of(i)
+        return [
+            pltpu.make_async_copy(src.at[rows, :], dst.at[rows, :], out_sems.at[n, i])
+            for n, (src, dst) in enumerate(((x, out_hbm), (gacc, gm_hbm), (att, ga_hbm)))
+        ]
+
+    @pl.loop(0, tiles)
+    def _(i):
+        rows = rows_of(i)
+        value = mid[rows, :]
+        x[rows, :] = (value + (acc[rows, :] + bc_ref[...])).astype(BF16)
+        hat, rate = norm_parts(value)
+        grad = cot[rows, :].astype(F32) + norm_back(hat, rate, gacc[rows, :], gain)
+        gacc[rows, :] = grad
+        att[rows, :] = dot_nt(grad.astype(BF16), wo[...]).astype(BF16)
+        for store in stores(i):
+            store.start()
+
+    gather.finish(count)
+
+    @pl.loop(0, tiles)
+    def _(i):
+        for store in stores(i):
+            store.wait()
+
+
+def feed_forward(dims, x, cot, attended, full_output, e_shard, c_shard, bo, be, bc, gain, shift):
+    length, width = x.shape
+    chunks = e_shard.shape[0]
+    columns = be.shape[1]
+    anyspace = pl.BlockSpec(memory_space=pl.ANY)
+    vmem = pl.BlockSpec(memory_space=pltpu.VMEM)
+    dma = pltpu.SemaphoreType.DMA
+    full = lambda kind: pltpu.VMEM((length, width), kind)
+    return pl.pallas_call(
+        functools.partial(ff_kernel, dims),
+        in_specs=[anyspace] * 6 + [vmem] * 5,
+        out_specs=[anyspace] * 3,
+        out_shape=[jax.ShapeDtypeStruct((length, width), kind) for kind in (BF16, F32, BF16)],
+        scratch_shapes=[
+            pltpu.VMEM((chunks,) + dims + e_shard.shape[1:], BF16),
+            pltpu.VMEM((chunks,) + dims + c_shard.shape[1:], BF16),
+            full(BF16), full(BF16), full(BF16), pltpu.VMEM((width, width), BF16),
+            full(BF16), full(F32), full(F32), full(F32),
+            dma((chunks, 4)), dma((chunks, 4)), dma((chunks,)),
+            dma((chunks, 4)), dma((chunks, 4)), dma((chunks,)),
+            dma((4,)), dma((3, length // TILE)),
+        ],
+        compiler_params=pltpu.CompilerParams(collective_id=1, has_side_effects=True, vmem_limit_bytes=58 << 20),
+        name="feed_forward",
+    )(x, cot, attended, full_output, e_shard, c_shard, bo, be, bc, gain, shift)
+
+
 def shards(
+    dims,
     tokens,
     lengths,
     cotangent,
@@ -222,12 +471,15 @@
 ):
     row_count, length, model_width = tokens.shape
     total_rows = row_count * length
-    full_mixer, full_output, full_expand, full_contract = (
-        lax.all_gather(mixer_weight, ("wide", "narrow"), axis=0, tiled=True),
-        lax.all_gather(output_weight, ("wide", "narrow"), axis=0, tiled=True),
-        lax.all_gather(expand_weight, ("wide", "narrow"), axis=0, tiled=True),
-        lax.all_gather(contract_weight, ("wide", "narrow"), axis=0, tiled=True),
-    )
+    full_mixer = lax.all_gather(mixer_weight, ("wide", "narrow"), axis=0, tiled=True)
+    full_output = lax.all_gather(output_weight, ("wide", "narrow"), axis=0, tiled=True)
+    devices = math.prod(dims)
+    hidden = expand_weight.shape[1]
+    part = hidden // devices // CHUNKS
+    by_chunk = lambda array: array.reshape(-1, devices, CHUNKS, part).transpose(2, 0, 1, 3).reshape(CHUNKS, -1, devices * part)
+    expand_parts = by_chunk(expand_weight)
+    expand_bias_parts = by_chunk(expand_bias)[:, 0]
+    contract_parts = contract_weight.reshape(CHUNKS, part, model_width)
     prefix_kv, reparam_back = jax.vjp(
         reparam, prefix_embed, reparam_in, reparam_in_bias, reparam_out, reparam_out_bias
     )
@@ -249,36 +501,13 @@
         for row in range(row_count)
     ]
     attended = jnp.concatenate([item[0] for item in forward], axis=0)
-    middle = inputs + (
-        jnp.dot(attended, full_output, preferred_element_type=jnp.float32) + output_bias
-    )
-    normed_two, norm_two_back = jax.vjp(
-        lambda values: norm_layer(values, norm_gains[1], norm_shifts[1]), middle
-    )
-    expanded = (
-        jnp.dot(normed_two.astype(jnp.bfloat16), full_expand, preferred_element_type=jnp.float32)
-        + expand_bias
-    )
-    activated, gelu_back = jax.vjp(partial(jax.nn.gelu, approximate=True), expanded)
-    result = middle + (
-        jnp.dot(activated.astype(jnp.bfloat16), full_contract, preferred_element_type=jnp.float32)
-        + contract_bias
-    )
-    out_tokens = result.astype(jnp.bfloat16).reshape(row_count, length, model_width)
-    back_mixer, back_output, back_expand, back_contract = (
-        lax.all_gather(mixer_weight, ("wide", "narrow"), axis=0, tiled=True),
-        lax.all_gather(output_weight, ("wide", "narrow"), axis=0, tiled=True),
-        lax.all_gather(expand_weight, ("wide", "narrow"), axis=0, tiled=True),
-        lax.all_gather(contract_weight, ("wide", "narrow"), axis=0, tiled=True),
-    )
-    grad_result = cotangent.reshape(total_rows, model_width)
-    grad_activated = times_transposed(grad_result, back_contract)
-    grad_expanded = gelu_back(grad_activated)[0].astype(jnp.bfloat16)
-    grad_normed_two = times_transposed(grad_expanded, back_expand)
-    grad_middle = grad_result.astype(jnp.float32) + norm_two_back(grad_normed_two)[0]
-    grad_attended = times_transposed(grad_middle.astype(jnp.bfloat16), back_output).astype(
-        jnp.bfloat16
-    )
+    as_row = lambda array: array.reshape(1, -1)
+    out_tokens, grad_middle, grad_attended = feed_forward(
+        dims, tokens.reshape(total_rows, model_width), cotangent.reshape(total_rows, model_width), attended, full_output,
+        expand_parts, contract_parts, as_row(output_bias), expand_bias_parts, as_row(contract_bias),
+        norm_gains[1:2], norm_shifts[1:2],
+    )
+    out_tokens = out_tokens.reshape(row_count, length, model_width)
     back = [
         attend_back(
             row_of(mixed_low, row), lengths[row : row + 1], pre, row_of(grad_attended, row),
@@ -293,7 +522,7 @@
         [sum(item[part] for item in back)[:prefix_count] for part in (3, 4)], axis=1
     )
     grad_prefix = lax.psum(grad_prefix, ("wide", "narrow"))
-    grad_normed_one = times_transposed(grad_mixed, back_mixer)
+    grad_normed_one = times_transposed(grad_mixed, full_mixer)
     grad_inputs = (grad_middle + norm_one_back(grad_normed_one)[0]).astype(jnp.bfloat16)
     grad_inputs = grad_inputs.reshape(row_count, length, model_width)
     grad_embed, grad_in, grad_in_bias, grad_out, grad_out_bias = reparam_back(grad_prefix)
@@ -302,7 +531,7 @@
 
 def solution(mesh):
     return jax.shard_map(
-        shards,
+        functools.partial(shards, grid_dims(mesh.shape)),
         mesh=mesh,
         in_specs=(
             P(("wide", "narrow"), None, None),

time: 547 us -> 466 us (0.85); the launches traced: 539 us -> 466 us
  Pallas kernels: 78.3 us -> 187 us
  waiting for transfers between devices: 285 us -> 196 us
  matrix products: 120 us -> 44.6 us
  local copies, waits for them, and re-layouts: 25.7 us -> 13.7 us
    all_gather x2 -> x0, waiting for transfers between devices: 133 us -> none  [the longest x1 71.1 us: shards(): lax.all_gather(expand_weight, ('wide', 'narrow'), axis=0, tiled=True)]
    pallas_call x0 -> x1, Pallas kernels: none -> 109 us  [feed_forward(): pl.pallas_call(functools.partial(ff_kernel, dims), in_specs=[anyspace] *...]
    psum x1, waiting for transfers between devices: 75.5 us -> 118 us  [shards(): grad_prefix = lax.psum(grad_prefix, ('wide', 'narrow'))]
    dot_general x3 -> x0, matrix products: 40 us -> none  [the longest x1 17.5 us: shards(): jnp.dot(activated.astype(jnp.bfloat16), full_contract, preferred_element_...]
    dot_general x3 -> x1, matrix products: 45.6 us -> 10.3 us  [times_transposed(): lax.dot_general(left_side, right_side, (((1,), (1,)), ((), ())), preferre...]
    unnamed x55 -> x31, local copies, waits for them, and re-layouts: 25.7 us -> 9.84 us
  transfers between devices with their start and end apart: 5 -> 3, of which waited for: 5 -> 3; matrix products, arithmetic and copies ran while one was open for 18% -> 7% of each run, Pallas kernels for 5% -> 6%
where the time goes in v2:
time: 466 us
  waiting for transfers between devices  196 us (42%)
  Pallas kernels  187 us (40%)
  matrix products  44.6 us (10%)
  between operations  14 us (3%)
  local copies, waits for them, and re-layouts  13.7 us (3%)
  other arithmetic  9.97 us (2%)
    psum x1, waiting for transfers between devices, shards(): grad_prefix = lax.psum(grad_prefix, ('wide', 'narrow'))  118 us
    pallas_call x1, Pallas kernels, feed_forward(): pl.pallas_call(functools.partial(ff_kernel, dims), in_specs=[anyspace] *...  109 us
    all_gather x1, waiting for transfers between devices, shards(): lax.all_gather(mixer_weight, ('wide', 'narrow'), axis=0, tiled=True)  61.8 us
    pallas_call x1, Pallas kernels, attend_back(): pl.pallas_call(functools.partial(bwd_kernel, prefix, most, count), grid=(...  49 us
    pallas_call x1, Pallas kernels, attend(): pl.pallas_call(functools.partial(fwd_kernel, prefix, most, count), grid=(...  29.2 us
    dot_general x3, matrix products, reparam(): jnp.dot(squashed, out_weight, precision=lax.Precision.HIGHEST) + out_shift  15.6 us
    all_gather x1, waiting for transfers between devices, shards(): lax.all_gather(output_weight, ('wide', 'narrow'), axis=0, tiled=True)  15.3 us
    dot_general x1, matrix products, shards(): jnp.dot(normed_one.astype(jnp.bfloat16), full_mixer, preferred_element_ty...  12 us
  transfers between devices with their start and end apart: 3, of which 3 were waited for; matrix products, arithmetic and copies ran while one was open for 7% of the time, Pallas kernels for 6%

profile of v2, /device:TPU:0, one launch (start us, length us, event | category | flops | bytes accessed | tf_op | source)
XLA Modules:
  0.0 465.6 jit_solution(2505868625129497044)
XLA Ops:
  7.2 0.0 copy-start
  7.2 0.0 copy-start.8
  7.2 0.0 copy-start.7
  7.2 0.0 copy-start.12
  7.2 0.0 copy-start.9
  7.2 0.0 all-gather.3.cloned.1.call-start
  7.3 0.7 all-gather.3.cloned.1.call-update
  8.0 0.0 all-gather.5.cloned.1.call-start
  8.0 0.7 all-gather.5.cloned.1.call-update
  8.7 0.0 all-reduce.3.cloned.1.call-start
  8.8 2.3 copy.28
  11.0 1.4 copy.29
  12.4 1.0 copy.31.e_hbm
  13.5 0.0 copy-done.8
  13.5 0.1 reshape.84
  13.6 0.7 squeeze_reshape.3.be_ref
  14.3 0.0 copy-done
  14.3 0.0 copy-done.7
  14.3 0.0 copy-done.12
  14.3 0.0 copy-start.3
  14.3 1.1 fusion.22
  15.5 0.0 copy-done.9
  15.5 0.0 copy-start.10
  15.5 0.0 copy-start.11
  15.5 0.0 copy-start.13
  15.5 4.3 fusion.15
  19.8 0.0 copy-done.3
  19.8 0.3 convert_reduce_fusion
  20.2 0.7 fusion.10
  20.9 0.0 copy-done.10
  20.9 0.0 copy-done.11
  20.9 0.6 fusion.27
  21.5 61.8 %all-gather.3.cloned.1.call-done = bf16[1024,3072]{1,0:T(8,128)(2,1)} async-done(((bf16[32,3072]{1,0:T(8,128)(2,1)}), bf16[1024,3072]{1,0:T(8,128)(2,1)}) %all-gather.3.cloned.1.call-update) | async-done | bytes 6291472 | tf_op jit(solution)/shard_map/all_gather | solution.py:474
  83.3 0.0 copy-done.13
  83.3 0.0 copy-start.2
  83.3 12.0 %add_convert_fusion.q_ref.k_ref.v_ref = bf16[1024,3072]{1,0:T(8,128)(2,1)} fusion(f32[3072]{0:T(1024)S(1)} %copy-done.13, bf16[1024,3072]{1,0:T(8,128)(2,1)} %all-gather.3.cloned.1.call-done, f32[1024]{0:T(1024)S(1)} %bitcast.64, f32[1024]{0:T(1024)S(1)} %bitcast.58, f32[1024]{0:T(1024)S(1)} %fusion.23, f32[1024]{0:T(1024)S(1)} %broadcast_multiply_fusion, ...), kind=kOutput, calls=%fused_computation | convolution fusion | flops 6455033856 | bytes 14708736 | tf_op jit(solution)/shard_map/dot_general | solution.py:492
  95.3 0.0 copy-done.2
  95.3 29.2 %attend.1 = (bf16[1024,1024]{1,0:T(8,128)(2,1)S(1)}, f32[8,2,1024]{2,1,0:T(2,128)S(1)}) custom-call(s32[1,8]{1,0:T(1,128)S(1)} %copy-done.2, bf16[1024,3072]{1,0:T(8,128)(2,1)} %add_convert_fusion.q_ref.k_ref.v_ref, bf16[1024,3072]{1,0:T(8,128)(2,1)} %add_convert_fusion.q_ref.k_ref.v_ref, bf16[1024,3072]{1,0:T(8,128)(2,1)} %add_convert_fusion.q_ref.k_ref.v_ref, ...), custom_call_target="tpu_custom_call" | custom-call | tf_op jit(solution)/shard_map/attend/pallas_call | solution.py:114
  124.5 0.0 copy-start.1
  124.5 1.3 copy-done.1
  125.8 15.3 %all-gather.5.cloned.1.call-done.wo_hbm = bf16[1024,1024]{1,0:T(8,128)(2,1)} async-done(((bf16[32,1024]{1,0:T(8,128)(2,1)}), bf16[1024,1024]{1,0:T(8,128)(2,1)}) %all-gather.5.cloned.1.call-update) | async-done | bytes 2097168 | tf_op jit(solution)/shard_map/all_gather | solution.py:475
  141.1 108.9 %feed_forward.1 = (bf16[1024,1024]{1,0:T(8,128)(2,1)}, f32[1024,1024]{1,0:T(8,128)}, bf16[1024,1024]{1,0:T(8,128)(2,1)}) custom-call(bf16[1024,1024]{1,0:T(8,128)(2,1)} %bitcast.51, bf16[1024,1024]{1,0:T(8,128)(2,1)} %bitcast.54, bf16[1024,1024]{1,0:T(8,128)(2,1)} %copy-done.1, bf16[1024,1024]{1,0:T(8,128)(2,1)} %all-gather.5.cloned.1.call-done.wo_hbm, ...), custom_call_target="tpu_custom_call" | custom-call | tf_op jit(solution)/shard_map/feed_forward/pallas_call | solution.py:432
  249.9 0.0 copy-start.4
  249.9 49.0 %attend_back.1 = (bf16[1024,1024]{1,0:T(8,128)(2,1)S(1)}, bf16[1024,1024]{1,0:T(8,128)(2,1)S(1)}, bf16[1024,1024]{1,0:T(8,128)(2,1)}, f32[16,1024]{1,0:T(8,128)S(1)}, f32[16,1024]{1,0:T(8,128)S(1)}) custom-call(s32[1,8]{1,0:T(1,128)S(1)} %copy-done.2, bf16[1024,3072]{1,0:T(8,128)(2,1)} %add_convert_fusion.q_ref.k_ref.v_ref, ...), custom_call_target="tpu_custom_call" | custom-call | tf_op jit(solution)/shard_map/attend_back/pallas_call | solution.py:190
  299.0 0.0 copy-done.4
  299.0 10.3 %fusion.14 = (f32[1024]{0:T(1024)S(1)}, f32[1024,1024]{1,0:T(8,128)S(1)}) fusion(f32[1024]{0:T(1024)S(1)} %bitcast.59, f32[1024]{0:T(1024)S(1)} %broadcast_multiply_fusion, bf16[1,1024,1024]{2,1,0:T(8,128)(2,1)S(1)} %copy-done.4, bf16[1024,3072]{1,0:T(8,128)(2,1)} %all-gather.3.cloned.1.call-done, bf16[1024,1024]{1,0:T(8,128)(2,1)} %get-tuple-element.24, ...), kind=kOutput, calls=%fused_computation.18 | convolution fusion | flops 6466567168 | bytes 18886656 | tf_op jit(solution)/shard_map/dot_general | solution.py:21
  309.3 0.0 copy-start.5
  309.3 1.7 fusion.26
  311.0 0.2 copy-done.5
  311.3 0.7 pad_maximum_fusion
  311.9 0.0 all-reduce.3.cloned.1.call-update
  312.0 5.9 %fusion.16 = bf16[1,1024,1024]{2,1,0:T(8,128)(2,1)} fusion(f32[1024,1024]{1,0:T(8,128)} %get-tuple-element.19, f32[1024]{0:T(1024)S(1)} %negate_multiply_fusion, f32[1024]{0:T(1024)S(1)} %multiply_multiply_fusion, f32[1024]{0:T(1024)S(1)} %broadcast_multiply_fusion, bf16[1,1024,1024]{2,1,0:T(8,128)(2,1)} %param.18, f32[1024]{0:T(1024)S(1)} %fusion.23, ...), kind=kLoop, calls=%fused_computation.22 | loop fusion | flops 10485760 | bytes 12603392 | tf_op jit(solution)/shard_map/reshape | solution.py:527
  317.8 117.7 %all-reduce.3.cloned.1.call-done = f32[10,2048]{1,0:T(8,128)} async-done(((f32[10,2048]{1,0:T(8,128)}), f32[10,2048]{1,0:T(8,128)}) %all-reduce.3.cloned.1.call-update) | async-done | bytes 81936 | tf_op jit(solution)/shard_map/psum | solution.py:524
  435.6 6.3 %fusion.29 = (f32[512]{0:T(512)}, f32[10,512]{1,0:T(8,128)S(1)}) fusion(f32[10,512]{1,0:T(8,128)S(1)} %fusion.22, f32[10,2048]{1,0:T(8,128)} %all-reduce.3.cloned.1.call-done, f32[512,2048]{1,0:T(8,128)} %param.34), kind=kOutput, calls=%fused_computation.42 | convolution fusion | flops 125854208 | bytes 4319232 | tf_op jit(solution)/shard_map/transpose(jvp())/dot_general | solution.py:30
  441.9 0.0 copy-start.6
  441.9 2.5 fusion.30
  444.4 3.2 convolution_bitcast_fusion
  447.5 2.9 copy.33
  450.4 0.0 copy-done.6
  450.4 5.0 %fusion.31 = f32[512,2048]{1,0:T(8,128)} fusion(f32[10,512]{1,0:T(8,128)S(1)} %fusion.22, f32[10,2048]{1,0:T(8,128)S(1)} %copy-done.6), kind=kOutput, calls=%fused_computation.44 | convolution fusion | flops 125829120 | bytes 4296704 | tf_op jit(solution)/shard_map/transpose(jvp())/dot_general | solution.py:30
  455.4 0.6 reduce_sum.62
  456.0 3.1 copy.37
  (6 shorter events, 0.1 us)
Async XLA Ops:
  7.2 7.2 %copy-start = (f32[1024,512]{1,0:T(8,128)S(1)}, f32[1024,512]{1,0:T(8,128)}, u32[]{:S(2)}) copy-start(f32[1024,512]{1,0:T(8,128)} %param.32) | copy-start | bytes 6291460
  7.2 6.3 %copy-start.8 = (f32[4096]{0:T(1024)S(1)}, f32[4096]{0:T(1024)}, u32[]{:S(2)}) copy-start(f32[4096]{0:T(1024)} %param.27) | copy-start | bytes 49156
  7.2 7.1 %copy-start.7 = (f32[10,1024]{1,0:T(8,128)S(1)}, f32[10,1024]{1,0:T(8,128)}, u32[]{:S(2)}) copy-start(f32[10,1024]{1,0:T(8,128)} %param.31) | copy-start | bytes 122884
  7.2 7.1 %copy-start.12 = (f32[512]{0:T(512)S(1)}, f32[512]{0:T(512)}, u32[]{:S(2)}) copy-start(f32[512]{0:T(512)} %param.33) | copy-start | bytes 6148
  7.2 8.2 %copy-start.9 = (f32[2048]{0:T(1024)S(1)}, f32[2048]{0:T(1024)}, u32[]{:S(2)}) copy-start(f32[2048]{0:T(1024)} %param.35) | copy-start | bytes 24580
  7.2 76.1 %all-gather.3.cloned.1.call-start = ((), (), s32[]{:S(2)}) async-start(), calls=%async_computation | async-start | bytes 6488064 | tf_op jit(solution)/shard_map/all_gather | solution.py:474
  8.0 133.1 %all-gather.5.cloned.1.call-start = ((), (), s32[]{:S(2)}) async-start(), calls=%async_computation.1 | async-start | bytes 2162688 | tf_op jit(solution)/shard_map/all_gather | solution.py:475
  8.7 426.9 %all-reduce.3.cloned.1.call-start = ((), (), s32[]{:S(2)}) async-start(), calls=%async_computation.2 | async-start | bytes 262144 | tf_op jit(solution)/shard_map/psum | solution.py:524
  14.3 5.5 %copy-start.3 = (bf16[1,1024,1024]{2,1,0:T(8,128)(2,1)S(1)}, bf16[1,1024,1024]{2,1,0:T(8,128)(2,1)}, u32[]{:S(2)}) copy-start(bf16[1,1024,1024]{2,1,0:T(8,128)(2,1)} %param.18) | copy-start | bytes 6291460
  15.5 5.4 %copy-start.10 = (f32[2,1024]{1,0:T(2,128)S(1)}, f32[2,1024]{1,0:T(2,128)}, u32[]{:S(2)}) copy-start(f32[2,1024]{1,0:T(2,128)} %param.30) | copy-start | bytes 24580
  15.5 5.4 %copy-start.11 = (f32[2,1024]{1,0:T(2,128)S(1)}, f32[2,1024]{1,0:T(2,128)}, u32[]{:S(2)}) copy-start(f32[2,1024]{1,0:T(2,128)} %param.29) | copy-start | bytes 24580
  15.5 67.8 %copy-start.13 = (f32[3072]{0:T(1024)S(1)}, f32[3072]{0:T(1024)}, u32[]{:S(2)}) copy-start(f32[3072]{0:T(1024)} %param.25) | copy-start | bytes 36868
  83.3 12.0 %copy-start.2 = (s32[1,8]{1,0:T(1,128)S(1)}, s32[1,8]{1,0:T(1,128)}, u32[]{:S(2)}) copy-start(s32[1,8]{1,0:T(1,128)} %len_ref.3) | copy-start | bytes 100
  124.5 1.3 copy-start.1
  249.9 49.1 %copy-start.4 = (bf16[1,1024,1024]{2,1,0:T(8,128)(2,1)S(1)}, bf16[1,1024,1024]{2,1,0:T(8,128)(2,1)}, u32[]{:S(2)}) copy-start(bf16[1,1024,1024]{2,1,0:T(8,128)(2,1)} %param.18) | copy-start | bytes 6291460
  309.3 2.0 copy-start.5
  441.9 8.5 %copy-start.6 = (f32[10,2048]{1,0:T(8,128)S(1)}, f32[10,2048]{1,0:T(8,128)}, u32[]{:S(2)}) copy-start(f32[10,2048]{1,0:T(8,128)} %all-reduce.3.cloned.1.call-done) | copy-start | bytes 245764
Sparse Core Ops, SparseCore 0:
  10.9 72.2 all-gather.2
  86.1 54.8 all-gather.4
  312.1 123.4 all-reduce.2

commit v3 on v2

--- a/solution.py
+++ b/solution.py
@@ -15,19 +15,6 @@
     center = values - jnp.mean(values, axis=-1, keepdims=True)
     spread = jnp.mean(center * center, axis=-1, keepdims=True)
     return center * lax.rsqrt(spread + 1e-05) * norm_gain + norm_shift
-
-
-def times_transposed(left_side, right_side):
-    return lax.dot_general(
-        left_side, right_side, (((1,), (1,)), ((), ())), preferred_element_type=jnp.float32
-    )
-
-
-def reparam(embed_values, in_weight, in_shift, out_weight, out_shift):
-    squashed = jnp.tanh(
-        jnp.dot(embed_values, in_weight, precision=lax.Precision.HIGHEST) + in_shift
-    )
-    return jnp.dot(squashed, out_weight, precision=lax.Precision.HIGHEST) + out_shift
 
 
 BLOCK = 256
@@ -122,84 +109,6 @@
     )(lengths, mixed, mixed, mixed, pre, pre)
 
 
-def bwd_kernel(prefix, most, count, len_ref, q_ref, k_ref, v_ref, pk_ref, pv_ref, do_ref, o_ref, lse_ref,
-               dq_ref, dk_ref, dv_ref, dpk_ref, dpv_ref, dk_acc, dv_acc):
-    length = q_ref.shape[0]
-    start = start_row(len_ref, count, length)
-    lane = lax.broadcasted_iota(jnp.int32, (1, 128), 1)
-    pre_seen = lax.broadcasted_iota(jnp.int32, (PAD, BLOCK), 0) < prefix
-    pk, pv = pk_ref[...], pv_ref[...]
-    k_t = k_ref[...].T
-    pk_t = pk.T
-    head_of = lax.broadcasted_iota(jnp.int32, (8, 128), 0)
-    pick = ((lax.broadcasted_iota(jnp.int32, (8, 128), 1) // 64) == head_of).astype(F32).astype(BF16)
-    for qi in range(length // BLOCK):
-        rows = slice(qi * BLOCK, (qi + 1) * BLOCK)
-        lo = span(qi, most)
-        st = start[:, rows]
-        q2 = q_ref[rows, :] * jnp.asarray(0.125, BF16)
-        do2 = do_ref[rows, :]
-        prod = do2.astype(F32) * o_ref[rows, :].astype(F32)
-        high = prod.astype(BF16)
-        low = (prod - high.astype(F32)).astype(BF16)
-        delta2 = dot_nt(pick, high) + dot_nt(pick, low)
-        halves = []
-        for h in range(2):
-            mine = (lane // 64) == h
-            qh = jnp.where(mine, q2, jnp.zeros((), BF16))
-            doh = jnp.where(mine, do2, jnp.zeros((), BF16))
-            lse = lse_ref[0, h:h + 1, rows]
-            delta = delta2[h:h + 1]
-            p = jnp.where(pre_seen, jnp.exp(dot_nt(pk, qh) - lse), 0.0)
-            ds = (p * (dot_nt(pv, doh) - delta)).astype(BF16)
-            dpk = dot_nn(ds, qh)
-            dpv = dot_nn(p.astype(BF16), doh)
-            if qi == 0 and h == 0:
-                dpk_ref[...], dpv_ref[...] = dpk, dpv
-            else:
-                dpk_ref[...] += dpk
-                dpv_ref[...] += dpv
-            dq = dot_nn(pk_t[h * 64:(h + 1) * 64], ds)
-            for kj in range(lo, qi + 1):
-                keys = slice(kj * BLOCK, (kj + 1) * BLOCK)
-                s = dot_nt(k_ref[keys, :], qh)
-                p = jnp.exp(s - lse)
-                p = jnp.where(visible(st, kj * BLOCK, BLOCK, qi * BLOCK, BLOCK, kj == qi), p, 0.0)
-                dp = dot_nt(v_ref[keys, :], doh)
-                ds = (p * (dp - delta)).astype(BF16)
-                dv = dot_nn(p.astype(BF16), doh)
-                dk = dot_nn(ds, qh)
-                if kj == qi and h == 0:
-                    dv_acc[keys, :], dk_acc[keys, :] = dv, dk
-                else:
-                    dv_acc[keys, :] += dv
-                    dk_acc[keys, :] += dk
-                dq = dq + dot_nn(k_t[h * 64:(h + 1) * 64, keys], ds)
-            halves.append(dq * 0.125)
-        dq_ref[rows, :] = jnp.concatenate(halves, axis=0).T.astype(BF16)
-    dk_ref[...] = dk_acc[...].astype(BF16)
-    dv_ref[...] = dv_acc[...].astype(BF16)
-
-
-def attend_back(mixed, lengths, pre, grad, attended, lse, prefix, most):
-    length, width = grad.shape
-    pairs = width // 128
-    count = lengths.shape[1]
-    col = lambda off: pl.BlockSpec((length, 128), lambda p: (0, p + off))
-    pcol = lambda off: pl.BlockSpec((PAD, 128), lambda p: (0, p + off))
-    return pl.pallas_call(
-        functools.partial(bwd_kernel, prefix, most, count),
-        grid=(pairs,),
-        in_specs=[pl.BlockSpec(memory_space=pltpu.SMEM), col(0), col(pairs), col(2 * pairs), pcol(0), pcol(pairs),
-                  col(0), col(0), pl.BlockSpec((1, 2, length), lambda p: (p, 0, 0))],
-        out_specs=[col(0), col(0), col(0), pcol(0), pcol(0)],
-        out_shape=[jax.ShapeDtypeStruct((length, width), BF16)] * 3 + [jax.ShapeDtypeStruct((PAD, width), F32)] * 2,
-        scratch_shapes=[pltpu.VMEM((length, 128), F32)] * 2,
-        compiler_params=pltpu.CompilerParams(vmem_limit_bytes=48 << 20),
-        name="attend_back",
-    )(lengths, mixed, mixed, mixed, pre, pre, grad, attended, lse)
-
-
 MESH = pl.DeviceIdType.MESH
 CHUNKS = 8
 LAG = 2
@@ -446,6 +355,283 @@
         compiler_params=pltpu.CompilerParams(collective_id=1, has_side_effects=True, vmem_limit_bytes=58 << 20),
         name="feed_forward",
     )(x, cot, attended, full_output, e_shard, c_shard, bo, be, bc, gain, shift)
+
+
+def back_kernel(dims, prefix, most, count, len_ref, q_ref, k_ref, v_ref, pk_ref, pv_ref, do_ref, o_ref, lse_ref,
+                gain_ref, w_hbm, x_hbm, gm_hbm, gx_hbm, total_ref,
+                dk_acc, dv_acc, dpk, dpv, gmix, w, x, gm, tiles, inbox, sums,
+                in_sems, out_sems, give_send, give_recv, tell_send, tell_recv):
+    length = q_ref.shape[0]
+    width = x.shape[1]
+    pair = pl.program_id(0)
+    pairs = width // 128
+    devices = math.prod(dims)
+    narrow_size = dims[2] * dims[3]
+    me = lax.axis_index("wide") * narrow_size + lax.axis_index("narrow")
+    tile_count = 4 * pairs
+    ratio = devices // tile_count
+    owns = lax.rem(me, ratio) == 0
+    own_tile = me // ratio
+    place = lambda device: (device // narrow_size, lax.rem(device, narrow_size))
+    loads = [
+        pltpu.make_async_copy(src, dst, in_sems.at[n])
+        for n, (src, dst) in enumerate(((w_hbm, w), (x_hbm, x), (gm_hbm, gm)))
+    ]
+    barrier = pltpu.get_barrier_semaphore()
+
+    @pl.when(pair == 0)
+    def _():
+        for load in loads:
+            load.start()
+
+        @pl.loop(1, devices)
+        def _(step):
+            peer = place(lax.rem(me + step, devices))
+            pl.semaphore_signal(barrier, inc=1, device_id=peer, device_id_type=MESH)
+
+    start = start_row(len_ref, count, length)
+    lane = lax.broadcasted_iota(jnp.int32, (1, 128), 1)
+    pre_seen = lax.broadcasted_iota(jnp.int32, (PAD, BLOCK), 0) < prefix
+    pk, pv = pk_ref[...], pv_ref[...]
+    k_t = k_ref[...].T
+    pk_t = pk.T
+    head_of = lax.broadcasted_iota(jnp.int32, (8, 128), 0)
+    pick = ((lax.broadcasted_iota(jnp.int32, (8, 128), 1) // 64) == head_of).astype(F32).astype(BF16)
+    columns = [pl.ds(pl.multiple_of(part * width + pair * 128, 128), 128) for part in range(3)]
+    for qi in range(length // BLOCK):
+        rows = slice(qi * BLOCK, (qi + 1) * BLOCK)
+        lo = span(qi, most)
+        st = start[:, rows]
+        q2 = q_ref[rows, :] * jnp.asarray(0.125, BF16)
+        do2 = do_ref[rows, :]
+        prod = do2.astype(F32) * o_ref[rows, :].astype(F32)
+        high = prod.astype(BF16)
+        low = (prod - high.astype(F32)).astype(BF16)
+        delta2 = dot_nt(pick, high) + dot_nt(pick, low)
+        halves = []
+        for h in range(2):
+            mine = (lane // 64) == h
+            qh = jnp.where(mine, q2, jnp.zeros((), BF16))
+            doh = jnp.where(mine, do2, jnp.zeros((), BF16))
+            lse = lse_ref[0, h:h + 1, rows]
+            delta = delta2[h:h + 1]
+            p = jnp.where(pre_seen, jnp.exp(dot_nt(pk, qh) - lse), 0.0)
+            ds = (p * (dot_nt(pv, doh) - delta)).astype(BF16)
+            one_dpk = dot_nn(ds, qh)
+            one_dpv = dot_nn(p.astype(BF16), doh)
+            if qi == 0 and h == 0:
+                dpk[...], dpv[...] = one_dpk, one_dpv
+            else:
+                dpk[...] += one_dpk
+                dpv[...] += one_dpv
+            dq = dot_nn(pk_t[h * 64:(h + 1) * 64], ds)
+            for kj in range(lo, qi + 1):
+                keys = slice(kj * BLOCK, (kj + 1) * BLOCK)
+                s = dot_nt(k_ref[keys, :], qh)
+                p = jnp.exp(s - lse)
+                p = jnp.where(visible(st, kj * BLOCK, BLOCK, qi * BLOCK, BLOCK, kj == qi), p, 0.0)
+                dp = dot_nt(v_ref[keys, :], doh)
+                ds = (p * (dp - delta)).astype(BF16)
+                dv = dot_nn(p.astype(BF16), doh)
+                dk = dot_nn(ds, qh)
+                if kj == qi and h == 0:
+                    dv_acc[keys, :], dk_acc[keys, :] = dv, dk
+                else:
+                    dv_acc[keys, :] += dv
+                    dk_acc[keys, :] += dk
+                dq = dq + dot_nn(k_t[h * 64:(h + 1) * 64, keys], ds)
+            halves.append(dq * 0.125)
+        gmix[rows, columns[0]] = jnp.concatenate(halves, axis=0).T.astype(BF16)
+    gmix[:, columns[1]] = dk_acc[...].astype(BF16)
+    gmix[:, columns[2]] = dv_acc[...].astype(BF16)
+
+    def give(part):
+        tile = part * pairs + pair
+        return pltpu.make_async_remote_copy(
+            src_ref=tiles.at[tile], dst_ref=inbox.at[me], send_sem=give_send, recv_sem=give_recv,
+            device_id=place(tile * ratio), device_id_type=MESH,
+        )
+
+    @pl.when(pair == 0)
+    def _():
+        pl.semaphore_wait(barrier, devices - 1)
+
+    for part, (ref, half) in enumerate(((dpk, 0), (dpk, 1), (dpv, 0), (dpv, 1))):
+        value = ref[half * 8:(half + 1) * 8, :]
+        tile = part * pairs + pair
+        tiles[pl.ds(tile, 1)] = value[None]
+        to_me = owns & (tile == own_tile)
+
+        @pl.when(to_me)
+        def _():
+            inbox[pl.ds(me, 1)] = value[None]
+
+        @pl.when(jnp.logical_not(to_me))
+        def _():
+            give(part).start()
+
+    @pl.when(pair == pairs - 1)
+    def _():
+        for load in loads:
+            load.wait()
+        tall = 256
+
+        def store(i):
+            rows = pl.ds(i * tall, tall)
+            return pltpu.make_async_copy(x.at[rows, :], gx_hbm.at[rows, :], out_sems.at[i])
+
+        def finish_rows(i):
+            rows = pl.ds(i * tall, tall)
+            grad = dot_nt(gmix[rows, :], w[...])
+            hat, rate = norm_parts(x[rows, :].astype(F32))
+            x[rows, :] = (gm[rows, :] + norm_back(hat, rate, grad, gain_ref[...])).astype(BF16)
+            store(i).start()
+
+        def bytes_of(ref, n, send, recv):
+            part = ref.at[pl.ds(0, n)]
+            return pltpu.make_async_remote_copy(
+                src_ref=part, dst_ref=part, send_sem=send, recv_sem=recv,
+                device_id=place(lax.rem(me + 1, devices)), device_id_type=MESH,
+            )
+
+        finish_rows(0)
+        finish_rows(1)
+
+        @pl.when(owns)
+        def _():
+            bytes_of(inbox, devices - 1, give_send, give_recv).wait_recv()
+            summed = inbox[0]
+            for device in range(1, devices):
+                summed = summed + inbox[device]
+            sums[pl.ds(own_tile, 1)] = summed[None]
+
+            @pl.loop(1, devices)
+            def _(step):
+                pltpu.make_async_remote_copy(
+                    src_ref=sums.at[own_tile], dst_ref=sums.at[own_tile], send_sem=tell_send,
+                    recv_sem=tell_recv, device_id=place(lax.rem(me + step, devices)), device_id_type=MESH,
+                ).start()
+
+        finish_rows(2)
+        finish_rows(3)
+
+        @pl.when(owns)
+        def _():
+            bytes_of(tiles, tile_count - 1, give_send, give_recv).wait_send()
+            bytes_of(inbox, devices - 1, tell_send, tell_recv).wait_send()
+            bytes_of(tiles, tile_count - 1, tell_send, tell_recv).wait_recv()
+
+        @pl.when(jnp.logical_not(owns))
+        def _():
+            bytes_of(tiles, tile_count, give_send, give_recv).wait_send()
+            bytes_of(tiles, tile_count, tell_send, tell_recv).wait_recv()
+
+        total_ref[...] = sums[...]
+        for i in range(length // tall):
+            store(i).wait()
+
+
+def attend_back(dims, mixed, lengths, pre, grad, attended, lse, gain, full_mixer, x, grad_middle, prefix, most):
+    length, width = grad.shape
+    pairs = width // 128
+    count = lengths.shape[1]
+    devices = math.prod(dims)
+    col = lambda off: pl.BlockSpec((length, 128), lambda p: (0, p + off))
+    pcol = lambda off: pl.BlockSpec((PAD, 128), lambda p: (0, p + off))
+    anyspace = pl.BlockSpec(memory_space=pl.ANY)
+    dma = pltpu.SemaphoreType.DMA
+    return pl.pallas_call(
+        functools.partial(back_kernel, dims, prefix, most, count),
+        grid=(pairs,),
+        in_specs=[pl.BlockSpec(memory_space=pltpu.SMEM), col(0), col(pairs), col(2 * pairs), pcol(0), pcol(pairs),
+                  col(0), col(0), pl.BlockSpec((1, 2, length), lambda p: (p, 0, 0)),
+                  pl.BlockSpec((1, width), lambda p: (0, 0)), anyspace, anyspace, anyspace],
+        out_specs=[anyspace, pl.BlockSpec((4 * pairs, 8, 128), lambda p: (0, 0, 0))],
+        out_shape=[jax.ShapeDtypeStruct((length, width), BF16), jax.ShapeDtypeStruct((4 * pairs, 8, 128), F32)],
+        scratch_shapes=[pltpu.VMEM((length, 128), F32)] * 2 + [pltpu.VMEM((PAD, 128), F32)] * 2 + [
+            pltpu.VMEM((length, 3 * width), BF16), pltpu.VMEM((width, 3 * width), BF16),
+            pltpu.VMEM((length, width), BF16), pltpu.VMEM((length, width), F32),
+            pltpu.VMEM((4 * pairs, 8, 128), F32), pltpu.VMEM((devices, 8, 128), F32),
+            pltpu.VMEM((4 * pairs, 8, 128), F32),
+            dma((3,)), dma((length // 256,)), dma(()), dma(()), dma(()), dma(()),
+        ],
+        compiler_params=pltpu.CompilerParams(collective_id=2, has_side_effects=True, vmem_limit_bytes=56 << 20),
+        name="attend_back",
+    )(lengths, mixed, mixed, mixed, pre, pre, grad, attended, lse, gain, full_mixer, x, grad_middle)
+
+
+def split(value):
+    high = value.astype(BF16)
+    return high, (value - high.astype(F32)).astype(BF16)
+
+
+def dot_fine(left, right, dims):
+    lh, ll = split(left)
+    rh, rl = split(right)
+    one = lambda a, b: lax.dot_general(a, b, (dims, ((), ())), preferred_element_type=F32)
+    return one(lh, rh) + (one(lh, rl) + one(ll, rh))
+
+
+def reparam_kernel(prefix, total_ref, sq_ref, embed_ref, ro_ref, ri_ref, gx_hbm, out_hbm,
+                   gx_out, out_out, ge_ref, gi_ref, gib_ref, go_ref, gob_ref, gs, sems):
+    step = pl.program_id(0)
+    steps = pl.num_programs(0)
+    pairs = total_ref.shape[0] // 4
+    moves = [pltpu.make_async_copy(gx_hbm, gx_out, sems.at[0]), pltpu.make_async_copy(out_hbm, out_out, sems.at[1])]
+
+    @pl.when(step == 0)
+    def _():
+        for move in moves:
+            move.start()
+        gs[...] = jnp.zeros_like(gs)
+
+    per = 2 * pairs // steps
+    blocks = []
+    for n in range(per):
+        block = step * per + n
+        part, pair = block // pairs, lax.rem(block, pairs)
+        top = total_ref[pl.ds(2 * part * pairs + pair, 1)][0]
+        low = total_ref[pl.ds((2 * part + 1) * pairs + pair, 1)][0]
+        blocks.append(jnp.concatenate([top, low], axis=0))
+    grad = jnp.concatenate(blocks, axis=1)
+    go_ref[...] = dot_fine(sq_ref[...], grad, ((0,), (0,)))
+    gob_ref[...] = jnp.sum(grad, axis=0, keepdims=True)
+    gs[...] += dot_fine(grad, ro_ref[...], ((1,), (1,)))
+
+    @pl.when(step == steps - 1)
+    def _():
+        squashed = sq_ref[...]
+        inner = gs[...] * (1.0 - squashed * squashed)
+        gi_ref[...] = dot_fine(embed_ref[...], inner, ((0,), (0,)))
+        gib_ref[...] = jnp.sum(inner, axis=0, keepdims=True)
+        ge_ref[...] = dot_fine(inner, ri_ref[...], ((1,), (1,)))[:prefix]
+        for move in moves:
+            move.wait()
+
+
+def reparam_back(total, squashed, embed, reparam_out, reparam_in, grad_tokens, out_tokens, prefix):
+    width2 = reparam_out.shape[1]
+    rep = reparam_out.shape[0]
+    width = embed.shape[1]
+    steps = 4
+    whole = lambda array: pl.BlockSpec(array.shape, lambda i: (0,) * array.ndim)
+    anyspace = pl.BlockSpec(memory_space=pl.ANY)
+    shape = jax.ShapeDtypeStruct
+    return pl.pallas_call(
+        functools.partial(reparam_kernel, prefix),
+        grid=(steps,),
+        in_specs=[whole(total), whole(squashed), whole(embed), pl.BlockSpec((rep, width2 // steps), lambda i: (0, i)),
+                  whole(reparam_in), anyspace, anyspace],
+        out_specs=[anyspace, anyspace,
+                   pl.BlockSpec((prefix, width), lambda i: (0, 0)), pl.BlockSpec((width, rep), lambda i: (0, 0)),
+                   pl.BlockSpec((1, rep), lambda i: (0, 0)), pl.BlockSpec((rep, width2 // steps), lambda i: (0, i)),
+                   pl.BlockSpec((1, width2 // steps), lambda i: (0, i))],
+        out_shape=[shape(grad_tokens.shape, BF16), shape(out_tokens.shape, BF16), shape((prefix, width), F32),
+                   shape((width, rep), F32), shape((1, rep), F32), shape((rep, width2), F32), shape((1, width2), F32)],
+        scratch_shapes=[pltpu.VMEM(squashed.shape, F32), pltpu.SemaphoreType.DMA((2,))],
+        compiler_params=pltpu.CompilerParams(vmem_limit_bytes=40 << 20),
+        name="reparam_back",
+    )(total, squashed, embed, reparam_out, reparam_in, grad_tokens, out_tokens)
 
 
 def shards(
@@ -480,53 +666,38 @@
     expand_parts = by_chunk(expand_weight)
     expand_bias_parts = by_chunk(expand_bias)[:, 0]
     contract_parts = contract_weight.reshape(CHUNKS, part, model_width)
-    prefix_kv, reparam_back = jax.vjp(
-        reparam, prefix_embed, reparam_in, reparam_in_bias, reparam_out, reparam_out_bias
+    prefix_count = prefix_embed.shape[0]
+    tall = lambda array: jnp.pad(array, ((0, PAD - prefix_count), (0, 0)))
+    squashed = jnp.tanh(
+        jnp.dot(prefix_embed, reparam_in, precision=lax.Precision.HIGHEST) + reparam_in_bias
     )
-    prefix_low = prefix_kv.astype(jnp.bfloat16)
+    prefix_kv = jnp.dot(squashed, reparam_out, precision=lax.Precision.HIGHEST) + reparam_out_bias
+    pre = tall(prefix_kv.astype(jnp.bfloat16))
     inputs = tokens.reshape(total_rows, model_width).astype(jnp.float32)
-    normed_one, norm_one_back = jax.vjp(
-        lambda values: norm_layer(values, norm_gains[0], norm_shifts[0]), inputs
-    )
+    normed_one = norm_layer(inputs, norm_gains[0], norm_shifts[0])
     mixed = (
         jnp.dot(normed_one.astype(jnp.bfloat16), full_mixer, preferred_element_type=jnp.float32)
         + mixer_bias
     )
     mixed_low = mixed.astype(jnp.bfloat16)
-    prefix_count = prefix_low.shape[0]
-    pre = jnp.pad(prefix_low, ((0, PAD - prefix_count), (0, 0)))
-    row_of = lambda array, row: array[row * length : (row + 1) * length]
-    forward = [
-        attend(row_of(mixed_low, row), lengths[row : row + 1], pre, prefix_count, MOST)
-        for row in range(row_count)
-    ]
-    attended = jnp.concatenate([item[0] for item in forward], axis=0)
+    attended, log_sums = attend(mixed_low, lengths, pre, prefix_count, MOST)
     as_row = lambda array: array.reshape(1, -1)
     out_tokens, grad_middle, grad_attended = feed_forward(
         dims, tokens.reshape(total_rows, model_width), cotangent.reshape(total_rows, model_width), attended, full_output,
         expand_parts, contract_parts, as_row(output_bias), expand_bias_parts, as_row(contract_bias),
         norm_gains[1:2], norm_shifts[1:2],
     )
-    out_tokens = out_tokens.reshape(row_count, length, model_width)
-    back = [
-        attend_back(
-            row_of(mixed_low, row), lengths[row : row + 1], pre, row_of(grad_attended, row),
-            forward[row][0], forward[row][1], prefix_count, MOST,
-        )
-        for row in range(row_count)
-    ]
-    grad_mixed = jnp.concatenate(
-        [jnp.concatenate([item[part] for item in back], axis=0) for part in range(3)], axis=1
+    grad_tokens, total = attend_back(
+        dims, mixed_low, lengths, pre, grad_attended, attended, log_sums, norm_gains[0:1], full_mixer,
+        tokens.reshape(total_rows, model_width), grad_middle, prefix_count, MOST,
     )
-    grad_prefix = jnp.concatenate(
-        [sum(item[part] for item in back)[:prefix_count] for part in (3, 4)], axis=1
+    grad_tokens, out_tokens, grad_embed, grad_in, grad_in_bias, grad_out, grad_out_bias = reparam_back(
+        total, tall(squashed), tall(prefix_embed), reparam_out, reparam_in, grad_tokens, out_tokens, prefix_count
     )
-    grad_prefix = lax.psum(grad_prefix, ("wide", "narrow"))
-    grad_normed_one = times_transposed(grad_mixed, full_mixer)
-    grad_inputs = (grad_middle + norm_one_back(grad_normed_one)[0]).astype(jnp.bfloat16)
-    grad_inputs = grad_inputs.reshape(row_count, length, model_width)
-    grad_embed, grad_in, grad_in_bias, grad_out, grad_out_bias = reparam_back(grad_prefix)
-    return (out_tokens, grad_inputs, grad_embed, grad_in, grad_in_bias, grad_out, grad_out_bias)
+    return (
+        out_tokens.reshape(tokens.shape), grad_tokens.reshape(tokens.shape), grad_embed, grad_in, grad_in_bias[0],
+        grad_out, grad_out_bias[0],
+    )
 
 
 def solution(mesh):

time: 466 us -> 331 us (0.71)
  waiting for transfers between devices: 196 us -> 77.7 us
  matrix products: 44.6 us -> 17.4 us
  Pallas kernels: 187 us -> 208 us
  other arithmetic: 9.97 us -> 1.05 us
    psum x1 -> x0, waiting for transfers between devices: 118 us -> none  [shards(): grad_prefix = lax.psum(grad_prefix, ('wide', 'narrow'))]
    dot_general x7 -> x2, matrix products: 32.6 us -> 5.4 us  [the longest x1 4.28 us: shards(): jnp.dot(squashed, reparam_out, precision=lax.Precision.HIGHEST)]
    pallas_call x1 -> x2, Pallas kernels: 49 us -> 69.9 us  [the longest x1 61.9 us: attend_back(): pl.pallas_call(functools.partial(back_kernel, dims, prefix, most, count),...]
    reshape x1 -> x0, other arithmetic: 5.87 us -> none  [shards(): grad_inputs = grad_inputs.reshape(row_count, length, model_width)]
    unnamed x31 -> x37, local copies, waits for them, and re-layouts: 9.84 us -> 8.35 us
  transfers between devices with their start and end apart: 3 -> 2, of which waited for: 3 -> 2; matrix products, arithmetic and copies ran while one was open for 7% -> 7% of each run, Pallas kernels for 6% -> 9%
where the time goes in v3:
time: 331 us
  Pallas kernels  208 us (63%)
  waiting for transfers between devices  77.7 us (23%)
  matrix products  17.4 us (5%)
  between operations  14.3 us (4%)
  local copies, waits for them, and re-layouts  12.3 us (4%)
    pallas_call x1, Pallas kernels, feed_forward(): pl.pallas_call(functools.partial(ff_kernel, dims), in_specs=[anyspace] *...  109 us
    pallas_call x1, Pallas kernels, attend_back(): pl.pallas_call(functools.partial(back_kernel, dims, prefix, most, count),...  61.9 us
    all_gather x1, waiting for transfers between devices, shards(): lax.all_gather(mixer_weight, ('wide', 'narrow'), axis=0, tiled=True)  61.8 us
    pallas_call x1, Pallas kernels, attend(): pl.pallas_call(functools.partial(fwd_kernel, prefix, most, count), grid=(...  29.2 us
    all_gather x1, waiting for transfers between devices, shards(): lax.all_gather(output_weight, ('wide', 'narrow'), axis=0, tiled=True)  14.6 us
    dot_general x1, matrix products, shards(): jnp.dot(normed_one.astype(jnp.bfloat16), full_mixer, preferred_element_ty...  12 us
    unnamed x37, local copies, waits for them, and re-layouts  8.35 us
    pallas_call x1, Pallas kernels, reparam_back(): pl.pallas_call(functools.partial(reparam_kernel, prefix), grid=(steps,),...  7.96 us
  transfers between devices with their start and end apart: 2, of which 2 were waited for; matrix products, arithmetic and copies ran while one was open for 7% of the time, Pallas kernels for 9%

profile of v3, /device:TPU:0, one launch (start us, length us, event | category | flops | bytes accessed | tf_op | source)
XLA Modules:
  0.0 330.8 jit_solution(8832528878590130639)
XLA Ops:
  7.2 0.0 copy-start.12
  7.2 0.0 copy-start.10
  7.2 0.0 copy-start.2
  7.2 0.0 copy-start.16
  7.2 0.0 copy-start.13
  7.2 0.0 all-gather.3.cloned.1.call-start
  7.3 0.7 all-gather.3.cloned.1.call-update
  8.0 0.0 all-gather.5.cloned.1.call-start
  8.0 0.7 all-gather.5.cloned.1.call-update
  8.7 2.3 copy.26
  11.0 1.4 copy.27
  12.4 1.0 copy.29.e_hbm
  13.4 0.0 copy-done.12
  13.4 0.1 reshape.67
  13.6 0.7 squeeze_reshape.3.be_ref
  14.3 0.0 copy-done.10
  14.3 0.0 copy-start.9
  14.3 0.0 copy-done.2
  14.3 0.0 copy-done.16
  14.3 1.1 fusion.12
  15.4 0.0 copy-done.13
  15.4 0.0 copy-start.14
  15.5 0.0 copy-start.15
  15.5 0.0 copy-start.17
  15.5 4.3 %fusion.6 = bf16[10,2048]{1,0:T(8,128)(2,1)S(1)} fusion(f32[10,512]{1,0:T(8,128)S(1)} %fusion.12, f32[512,2048]{1,0:T(8,128)} %ro_ref.1, f32[2048]{0:T(1024)S(1)} %copy-done.13), kind=kOutput, calls=%fused_computation.10 | convolution fusion | flops 125870080 | bytes 4263936 | tf_op jit(solution)/shard_map/dot_general | solution.py:674
  19.8 0.0 copy-done.9
  19.8 0.0 copy-start.5
  19.8 0.3 convert_reduce_fusion
  20.2 0.7 fusion.2
  20.9 0.0 copy-done.14
  20.9 0.0 copy-done.15
  20.9 0.6 fusion.14
  21.5 0.0 copy-start.11
  21.5 61.8 %all-gather.3.cloned.1.call-done.w_hbm = bf16[1024,3072]{1,0:T(8,128)(2,1)} async-done(((bf16[32,3072]{1,0:T(8,128)(2,1)}), bf16[1024,3072]{1,0:T(8,128)(2,1)}) %all-gather.3.cloned.1.call-update) | async-done | bytes 6291472 | tf_op jit(solution)/shard_map/all_gather | solution.py:660
  83.3 0.0 copy-done.17
  83.3 0.0 copy-start.8
  83.3 12.0 %add_convert_fusion.q_ref.k_ref.v_ref = bf16[1024,3072]{1,0:T(8,128)(2,1)} fusion(f32[3072]{0:T(1024)S(1)} %copy-done.17, bf16[1024,3072]{1,0:T(8,128)(2,1)} %all-gather.3.cloned.1.call-done.w_hbm, f32[1024]{0:T(1024)S(1)} %bitcast.41, f32[1024]{0:T(1024)S(1)} %bitcast.38, f32[1024]{0:T(1024)S(1)} %add_rsqrt_fusion, f32[1024]{0:T(1024)S(1)} %broadcast_multiply_fusion, ...), kind=kOutput, calls=%fused_computation | convolution fusion | flops 6455033856 | bytes 14708736 | tf_op jit(solution)/shard_map/dot_general | solution.py:679
  95.3 0.0 copy-done.5
  95.3 0.0 copy-done.11
  95.3 0.0 copy-done.8
  95.3 29.2 %attend.1 = (bf16[1024,1024]{1,0:T(8,128)(2,1)S(1)}, f32[8,2,1024]{2,1,0:T(2,128)S(1)}) custom-call(s32[1,8]{1,0:T(1,128)S(1)} %copy-done.8, bf16[1024,3072]{1,0:T(8,128)(2,1)} %add_convert_fusion.q_ref.k_ref.v_ref, bf16[1024,3072]{1,0:T(8,128)(2,1)} %add_convert_fusion.q_ref.k_ref.v_ref, bf16[1024,3072]{1,0:T(8,128)(2,1)} %add_convert_fusion.q_ref.k_ref.v_ref, ...), custom_call_target="tpu_custom_call" | custom-call | tf_op jit(solution)/shard_map/attend/pallas_call | solution.py:101
  124.5 0.0 copy-start.1
  124.5 1.3 copy-done.1
  125.8 0.0 copy-start.7
  125.9 0.6 copy-done.7
  126.5 14.6 %all-gather.5.cloned.1.call-done.wo_hbm = bf16[1024,1024]{1,0:T(8,128)(2,1)} async-done(((bf16[32,1024]{1,0:T(8,128)(2,1)}), bf16[1024,1024]{1,0:T(8,128)(2,1)}) %all-gather.5.cloned.1.call-update) | async-done | bytes 2097168 | tf_op jit(solution)/shard_map/all_gather | solution.py:661
  141.1 108.9 %feed_forward.1 = (bf16[1024,1024]{1,0:T(8,128)(2,1)}, f32[1024,1024]{1,0:T(8,128)}, bf16[1024,1024]{1,0:T(8,128)(2,1)}) custom-call(bf16[1024,1024]{1,0:T(8,128)(2,1)} %bitcast.31, bf16[1024,1024]{1,0:T(8,128)(2,1)} %bitcast.35, bf16[1024,1024]{1,0:T(8,128)(2,1)} %copy-done.1, bf16[1024,1024]{1,0:T(8,128)(2,1)} %all-gather.5.cloned.1.call-done.wo_hbm, ...), custom_call_target="tpu_custom_call" | custom-call | tf_op jit(solution)/shard_map/feed_forward/pallas_call | solution.py:341
  249.9 0.0 copy-start
  249.9 61.9 %attend_back.1 = (bf16[1024,1024]{1,0:T(8,128)(2,1)}, f32[32,8,128]{2,1,0:T(8,128)}) custom-call(s32[1,8]{1,0:T(1,128)} %len_ref.3, bf16[1024,3072]{1,0:T(8,128)(2,1)} %add_convert_fusion.q_ref.k_ref.v_ref, bf16[1024,3072]{1,0:T(8,128)(2,1)} %add_convert_fusion.q_ref.k_ref.v_ref, bf16[1024,3072]{1,0:T(8,128)(2,1)} %add_convert_fusion.q_ref.k_ref.v_ref, ...), custom_call_target="tpu_custom_call" | custom-call | tf_op jit(solution)/shard_map/attend_back/pallas_call | solution.py:543
  311.9 0.0 copy-done
  311.9 0.0 copy-start.3
  311.9 1.6 copy-done.3
  313.5 0.0 copy-start.4
  313.5 1.6 copy-done.4
  315.1 0.0 copy-start.6
  315.1 0.9 copy-done.6
  316.0 8.0 %reparam_back.1 = (bf16[1024,1024]{1,0:T(8,128)(2,1)}, bf16[1024,1024]{1,0:T(8,128)(2,1)}, f32[10,1024]{1,0:T(8,128)}, f32[1024,512]{1,0:T(8,128)}, f32[1,512]{1...) custom-call(f32[32,8,128]{2,1,0:T(8,128)S(1)} %copy-done.6, f32[16,512]{1,0:T(8,128)S(1)} %pad.13.sq_ref, ...), custom_call_target="tpu_custom_call" | custom-call | tf_op jit(solution)/shard_map/reparam_back/pallas_call | solution.py:620
  (6 shorter events, 0.1 us)
Async XLA Ops:
  7.2 6.2 %copy-start.12 = (f32[4096]{0:T(1024)S(1)}, f32[4096]{0:T(1024)}, u32[]{:S(2)}) copy-start(f32[4096]{0:T(1024)} %param.27) | copy-start | bytes 49156
  7.2 7.1 %copy-start.10 = (f32[10,1024]{1,0:T(8,128)S(1)}, f32[10,1024]{1,0:T(8,128)}, u32[]{:S(2)}) copy-start(f32[10,1024]{1,0:T(8,128)} %param.31) | copy-start | bytes 122884
  7.2 7.1 %copy-start.2 = (f32[1024,512]{1,0:T(8,128)S(1)}, f32[1024,512]{1,0:T(8,128)}, u32[]{:S(2)}) copy-start(f32[1024,512]{1,0:T(8,128)} %ri_ref.1) | copy-start | bytes 6291460
  7.2 7.1 %copy-start.16 = (f32[512]{0:T(512)S(1)}, f32[512]{0:T(512)}, u32[]{:S(2)}) copy-start(f32[512]{0:T(512)} %param.33) | copy-start | bytes 6148
  7.2 8.2 %copy-start.13 = (f32[2048]{0:T(1024)S(1)}, f32[2048]{0:T(1024)}, u32[]{:S(2)}) copy-start(f32[2048]{0:T(1024)} %param.35) | copy-start | bytes 24580
  7.2 76.1 %all-gather.3.cloned.1.call-start = ((), (), s32[]{:S(2)}) async-start(), calls=%async_computation | async-start | bytes 6488064 | tf_op jit(solution)/shard_map/all_gather | solution.py:660
  8.0 133.1 %all-gather.5.cloned.1.call-start = ((), (), s32[]{:S(2)}) async-start(), calls=%async_computation.1 | async-start | bytes 2162688 | tf_op jit(solution)/shard_map/all_gather | solution.py:661
  14.3 5.5 %copy-start.9 = (bf16[1,1024,1024]{2,1,0:T(8,128)(2,1)S(1)}, bf16[1,1024,1024]{2,1,0:T(8,128)(2,1)}, u32[]{:S(2)}) copy-start(bf16[1,1024,1024]{2,1,0:T(8,128)(2,1)} %param.18) | copy-start | bytes 6291460
  15.4 5.4 %copy-start.14 = (f32[2,1024]{1,0:T(2,128)S(1)}, f32[2,1024]{1,0:T(2,128)}, u32[]{:S(2)}) copy-start(f32[2,1024]{1,0:T(2,128)} %param.30) | copy-start | bytes 24580
  15.5 5.4 %copy-start.15 = (f32[2,1024]{1,0:T(2,128)S(1)}, f32[2,1024]{1,0:T(2,128)}, u32[]{:S(2)}) copy-start(f32[2,1024]{1,0:T(2,128)} %param.29) | copy-start | bytes 24580
  15.5 67.8 %copy-start.17 = (f32[3072]{0:T(1024)S(1)}, f32[3072]{0:T(1024)}, u32[]{:S(2)}) copy-start(f32[3072]{0:T(1024)} %param.25) | copy-start | bytes 36868
  19.8 75.5 %copy-start.5 = (bf16[16,2048]{1,0:T(8,128)(2,1)}, bf16[16,2048]{1,0:T(8,128)(2,1)S(1)}, u32[]{:S(2)}) copy-start(bf16[16,2048]{1,0:T(8,128)(2,1)S(1)} %pad.12.pk_ref.pv_ref) | copy-start | bytes 196612
  21.5 73.8 %copy-start.11 = (f32[1,1024]{1,0:T(1,128)}, f32[1,1024]{1,0:T(1,128)S(1)}, u32[]{:S(2)}) copy-start(f32[1,1024]{1,0:T(1,128)S(1)} %get-tuple-element.39.gain_ref) | copy-start | bytes 12292
  83.3 12.1 %copy-start.8 = (s32[1,8]{1,0:T(1,128)S(1)}, s32[1,8]{1,0:T(1,128)}, u32[]{:S(2)}) copy-start(s32[1,8]{1,0:T(1,128)} %len_ref.3) | copy-start | bytes 100
  124.5 1.3 copy-start.1
  125.8 0.6 copy-start.7
  249.9 62.0 %copy-start = (f32[512,2048]{1,0:T(8,128)S(1)}, f32[512,2048]{1,0:T(8,128)}, u32[]{:S(2)}) copy-start(f32[512,2048]{1,0:T(8,128)} %ro_ref.1) | copy-start | bytes 12582916
  311.9 1.6 copy-start.3
  313.5 1.6 copy-start.4
  315.1 0.9 copy-start.6
Sparse Core Ops, SparseCore 0:
  10.9 72.2 all-gather.2
  86.1 54.8 all-gather.4

commit v4 on v3

--- a/solution.py
+++ b/solution.py
@@ -9,12 +9,6 @@
 from jax.sharding import PartitionSpec as P
 
 MOST = 512
-
-
-def norm_layer(values, norm_gain, norm_shift):
-    center = values - jnp.mean(values, axis=-1, keepdims=True)
-    spread = jnp.mean(center * center, axis=-1, keepdims=True)
-    return center * lax.rsqrt(spread + 1e-05) * norm_gain + norm_shift
 
 
 BLOCK = 256
@@ -86,39 +80,29 @@
         o_ref[rows, :] = jnp.concatenate(halves, axis=0).T.astype(BF16)
 
 
-def fwd_kernel(prefix, most, count, len_ref, q_ref, k_ref, v_ref, pk_ref, pv_ref, o_ref, lse_ref):
-    start = start_row(len_ref, count, q_ref.shape[0])
-    q2 = q_ref[...] * jnp.asarray(0.125, BF16)
-    fwd_pair(q2, k_ref, v_ref, pk_ref[...], pv_ref[...], start, prefix, most, o_ref, lse_ref.at[0])
-
-
-def attend(mixed, lengths, pre, prefix, most):
-    length, width = mixed.shape[0], mixed.shape[1] // 3
-    pairs = width // 128
-    count = lengths.shape[1]
-    col = lambda off: pl.BlockSpec((length, 128), lambda p: (0, p + off))
-    pcol = lambda off: pl.BlockSpec((PAD, 128), lambda p: (0, p + off))
-    return pl.pallas_call(
-        functools.partial(fwd_kernel, prefix, most, count),
-        grid=(pairs,),
-        in_specs=[pl.BlockSpec(memory_space=pltpu.SMEM), col(0), col(pairs), col(2 * pairs), pcol(0), pcol(pairs)],
-        out_specs=[col(0), pl.BlockSpec((1, 2, length), lambda p: (p, 0, 0))],
-        out_shape=[jax.ShapeDtypeStruct((length, width), BF16), jax.ShapeDtypeStruct((pairs, 2, length), F32)],
-        compiler_params=pltpu.CompilerParams(vmem_limit_bytes=48 << 20),
-        name="attend",
-    )(lengths, mixed, mixed, mixed, pre, pre)
-
-
+CHUNKS = 8
+TILE = 256
 MESH = pl.DeviceIdType.MESH
-CHUNKS = 8
-LAG = 2
-AHEAD = 3
-TILE = 256
+XY, YX = (0, 1, 2, 3), (0, 2, 1, 3)
 
 
 def grid_dims(mesh_shape):
     wide, narrow = mesh_shape["wide"], mesh_shape["narrow"]
     return (wide // 2, 2, narrow // 2, 2)
+
+
+class Family:
+    def __init__(self, source, target, order, sems, count, first=0, stride=1, offset=0, pace=1, lag=1, ahead=3):
+        self.source, self.target, self.order = source, target, order
+        self.send, self.recv, self.own = sems
+        self.count, self.first, self.stride = count, first, stride
+        self.offset, self.pace, self.lag, self.ahead = offset, pace, lag, ahead
+
+    def block(self, j):
+        return self.first + self.stride * j
+
+    def end(self):
+        return self.offset + self.pace * (self.count - 1) + 3 * self.lag + 1
 
 
 class Gather:
@@ -144,77 +128,77 @@
         pl.semaphore_wait(barrier, count)
 
     def view(self, family, j, stage, index):
-        _, target, order, _, _, _ = family
-        done, dim = order[:stage], order[stage]
-        return target.at[
-            (j,) + tuple(slice(None) if d in done else (index if d == dim else self.at[d]) for d in range(4))
+        done, dim = family.order[:stage], family.order[stage]
+        return family.target.at[
+            (family.block(j),)
+            + tuple(slice(None) if d in done else (index if d == dim else self.at[d]) for d in range(4))
         ]
 
-    def own(self, family, j):
-        source, target, _, _, _, own = family
-        return pltpu.make_async_copy(source.at[j], target.at[(j,) + self.at], own.at[j])
-
-    def start(self, j, stage):
-        for family in self.families:
-            source, _, order, send, recv, _ = family
-            dim = order[stage]
-            size = self.dims[dim]
-            if stage == 0:
-                self.own(family, j).start()
-            mine = self.view(family, j, stage, self.at[dim])
-            for step in range(1, size):
-                pltpu.make_async_remote_copy(
-                    src_ref=source.at[j] if stage == 0 else mine,
-                    dst_ref=mine,
-                    send_sem=send.at[j, stage],
-                    recv_sem=recv.at[j, stage],
-                    device_id=self.device(dim, lax.rem(self.at[dim] + step, size)),
-                    device_id_type=MESH,
-                ).start()
+    def keep(self, family, j):
+        block = family.block(j)
+        return pltpu.make_async_copy(family.source.at[block], family.target.at[(block,) + self.at], family.own.at[j])
+
+    def start(self, family, j, stage):
+        dim = family.order[stage]
+        size = self.dims[dim]
+        if stage == 0:
+            self.keep(family, j).start()
+        mine = self.view(family, j, stage, self.at[dim])
+        for step in range(1, size):
+            pltpu.make_async_remote_copy(
+                src_ref=family.source.at[family.block(j)] if stage == 0 else mine,
+                dst_ref=mine,
+                send_sem=family.send.at[j, stage],
+                recv_sem=family.recv.at[j, stage],
+                device_id=self.device(dim, lax.rem(self.at[dim] + step, size)),
+                device_id_type=MESH,
+            ).start()
 
     def whole(self, family, j, stage):
-        _, _, order, send, recv, _ = family
-        size = self.dims[order[stage]]
+        dim = family.order[stage]
+        size = self.dims[dim]
         part = self.view(family, j, stage, pl.ds(0, size - 1))
         return pltpu.make_async_remote_copy(
-            src_ref=part, dst_ref=part, send_sem=send.at[j, stage], recv_sem=recv.at[j, stage],
-            device_id=self.device(order[stage], lax.rem(self.at[order[stage]] + 1, size)), device_id_type=MESH,
+            src_ref=part, dst_ref=part, send_sem=family.send.at[j, stage], recv_sem=family.recv.at[j, stage],
+            device_id=self.device(dim, lax.rem(self.at[dim] + 1, size)), device_id_type=MESH,
         )
 
-    def arrive(self, j, stage):
+    def arrive(self, family, j, stage):
+        if stage == 0:
+            self.keep(family, j).wait()
+        self.whole(family, j, stage).wait_recv()
+
+    def begin(self):
         for family in self.families:
-            if stage == 0:
-                self.own(family, j).wait()
-            self.whole(family, j, stage).wait_recv()
-
-    def finish(self, count):
-        @pl.loop(0, count)
-        def _(j):
+            for j in range(family.count):
+                if family.offset + family.pace * j < family.ahead:
+                    self.start(family, j, 0)
+
+    def tick(self, t):
+        for stage in (3, 2, 1, 0, -1):
             for family in self.families:
+                past = t - family.offset - (family.lag * stage if stage >= 0 else -family.ahead)
+                j = past // family.pace
+
+                @pl.when((past >= 0) & (j < family.count) & (lax.rem(past, family.pace) == 0))
+                def _():
+                    if stage >= 0:
+                        self.arrive(family, j, stage)
+                    if stage < 3:
+                        self.start(family, j, stage + 1)
+
+    def finish(self):
+        for family in self.families:
+
+            @pl.loop(0, family.count)
+            def _(j):
                 for stage in range(4):
                     self.whole(family, j, stage).wait_send()
 
-    def tick(self, t, count):
-        @pl.when(t + AHEAD < count)
-        def _():
-            self.start(t + AHEAD, 0)
-
-        for stage in (2, 1, 0):
-            j = t - LAG * stage
-
-            @pl.when((j >= 0) & (j < count))
-            def _():
-                self.arrive(j, stage)
-                self.start(j, stage + 1)
-
-        j = t - LAG * 3
-
-        @pl.when((j >= 0) & (j < count))
-        def _():
-            self.arrive(j, 3)
-
-
-XY, YX = (0, 1, 2, 3), (0, 2, 1, 3)
+
+def gather_sems(count):
+    dma = pltpu.SemaphoreType.DMA
+    return [dma((count, 4)), dma((count, 4)), dma((count,))]
 
 
 def norm_parts(values):
@@ -228,6 +212,18 @@
     return rate * (
         inner - jnp.mean(inner, axis=-1, keepdims=True) - hat * jnp.mean(inner * hat, axis=-1, keepdims=True)
     )
+
+
+def split(value):
+    high = value.astype(BF16)
+    return high, (value - high.astype(F32)).astype(BF16)
+
+
+def dot_fine(left, right, dims):
+    lh, ll = split(left)
+    rh, rl = split(right)
+    one = lambda a, b: lax.dot_general(a, b, (dims, ((), ())), preferred_element_type=F32)
+    return one(lh, rh) + (one(lh, rl) + one(ll, rh))
 
 
 ROOT = math.sqrt(2.0 / math.pi)
@@ -241,38 +237,115 @@
     return v * half, slope
 
 
-def ff_kernel(dims, x_hbm, cot_hbm, att_hbm, wo_hbm, e_hbm, c_hbm, bo_ref, be_ref, bc_ref, gain_ref, shift_ref,
-              out_hbm, gm_hbm, ga_hbm,
-              ew, cw, x, cot, att, wo, n2, mid, acc, gacc,
-              e_send, e_recv, e_own, c_send, c_recv, c_own, in_sems, out_sems):
+PAIR_TICK = 3
+FF_TICK = 12
+
+
+def layer_kernel(dims, prefix, most, count, len_ref, x_hbm, cot_hbm, m_hbm, w_hbm, e_hbm, c_hbm, ri_hbm, ro_hbm,
+                 embed_ref, rib_ref, rob_ref, mb_ref, bo_ref, be_ref, bc_ref, gain_ref, shift_ref,
+                 mixed_hbm, att_hbm, lse_ref, pre_ref, sq_ref, mixer_hbm, out_hbm, gm_hbm, ga_hbm,
+                 x, norm, mixer, mixed, att, cot, wo, mid, acc, gacc, ew, cw,
+                 m0_send, m0_recv, m0_own, m1_send, m1_recv, m1_own, w0_send, w0_recv, w0_own, w1_send, w1_recv, w1_own,
+                 e_send, e_recv, e_own, c_send, c_recv, c_own,
+                 in_sems, mixed_sems, att_sems, mixer_sems, out_sems):
     length, width = x.shape
-    count = e_hbm.shape[0]
-    gather = Gather(dims, [(e_hbm, ew, XY, e_send, e_recv, e_own), (c_hbm, cw, YX, c_send, c_recv, c_own)])
+    pairs, chunks = m_hbm.shape[0], e_hbm.shape[0]
+    rep = sq_ref.shape[1]
+    half = pairs // 2
+    gather = Gather(dims, [
+        Family(m_hbm, mixer, XY, (m0_send, m0_recv, m0_own), half, first=0, stride=2, offset=0, pace=2),
+        Family(m_hbm, mixer, YX, (m1_send, m1_recv, m1_own), half, first=1, stride=2, offset=1, pace=2),
+        Family(w_hbm, wo, XY, (w0_send, w0_recv, w0_own), 1, first=0, offset=FF_TICK - 6),
+        Family(w_hbm, wo, YX, (w1_send, w1_recv, w1_own), 1, first=1, offset=FF_TICK - 6),
+        Family(e_hbm, ew, XY, (e_send, e_recv, e_own), chunks, offset=FF_TICK - 6, lag=2),
+        Family(c_hbm, cw, YX, (c_send, c_recv, c_own), chunks, offset=FF_TICK - 6, lag=2),
+    ])
     loads = [
         pltpu.make_async_copy(src, dst, in_sems.at[n])
-        for n, (src, dst) in enumerate(((x_hbm, x), (att_hbm, att), (wo_hbm, wo), (cot_hbm, cot)))
+        for n, (src, dst) in enumerate((
+            (x_hbm, x), (ri_hbm, mid.at[:, :rep]), (ro_hbm.at[:, :width], acc.at[:rep]), (ro_hbm.at[:, width:], gacc.at[:rep]),
+            (cot_hbm, cot),
+        ))
     ]
     for load in loads:
         load.start()
     gather.greet()
-    for j in range(min(AHEAD, count)):
-        gather.start(j, 0)
-    for load in loads:
-        load.wait()
-    gain, shift = gain_ref[...], shift_ref[...]
+    gather.begin()
     tiles = length // TILE
 
     def rows_of(i):
         return pl.ds(pl.multiple_of(i * TILE, TILE), TILE)
 
-    def before(i):
-        rows = rows_of(i)
-        value = x[rows, :].astype(F32) + (dot_nn(att[rows, :], wo[...]) + bo_ref[...])
-        mid[rows, :] = value
-        hat, _ = norm_parts(value)
-        n2[rows, :] = (hat * gain + shift).astype(BF16)
-        acc[rows, :] = jnp.zeros((TILE, width), F32)
-        gacc[rows, :] = jnp.zeros((TILE, width), F32)
+    def first_norm():
+        loads[0].wait()
+
+        @pl.loop(0, tiles)
+        def _(i):
+            rows = rows_of(i)
+            hat, _ = norm_parts(x[rows, :].astype(F32))
+            norm[rows, :] = (hat * gain_ref[0:1, :] + shift_ref[0:1, :]).astype(BF16)
+
+    def prefix_rows():
+        for load in loads[1:]:
+            load.wait()
+        seen = lax.broadcasted_iota(jnp.int32, (PAD, 1), 0) < prefix
+        squashed = jnp.where(seen, jnp.tanh(dot_fine(embed_ref[...], mid[:, :rep], ((1,), (0,))) + rib_ref[...]), 0.0)
+        sq_ref[...] = squashed
+        for part, ref in enumerate((acc, gacc)):
+            columns = slice(part * width, (part + 1) * width)
+            whole = dot_fine(squashed, ref[:rep, :], ((1,), (0,))) + rob_ref[:, columns]
+            pre_ref[:, columns] = jnp.where(seen, whole, 0.0).astype(BF16)
+
+    def stores(p, slot):
+        columns = pl.ds(pl.multiple_of(p * 128, 128), 128)
+        return [
+            pltpu.make_async_copy(mixed.at[slot], mixed_hbm.at[p], mixed_sems.at[slot]),
+            pltpu.make_async_copy(att.at[:, columns], att_hbm.at[:, columns], att_sems.at[slot]),
+        ]
+
+    def keep_mixer(p):
+        return pltpu.make_async_copy(mixer.at[p], mixer_hbm.at[p], mixer_sems.at[p])
+
+    def pair(p):
+        slot = lax.rem(p, 2)
+
+        @pl.when(p >= 2)
+        def _():
+            for store in stores(p - 2, slot):
+                store.wait()
+
+        keep_mixer(p).start()
+        weight = mixer[pl.ds(p, 1)].reshape(width, 384)
+        at = [pl.ds(pl.multiple_of(part * width + p * 128, 128), 128) for part in range(3)]
+        bias = jnp.concatenate([mb_ref[:, columns] for columns in at], axis=1)
+        mixed[pl.ds(slot, 1)] = (dot_nn(norm[...], weight) + bias).astype(BF16)[None]
+        here = mixed.at[slot]
+        q2 = here[:, 0:128] * jnp.asarray(0.125, BF16)
+        start = start_row(len_ref, count, length)
+        fwd_pair(
+            q2, here.at[:, 128:256], here.at[:, 256:384], pre_ref[:, at[0]], pre_ref[:, at[1]],
+            start, prefix, most, att.at[:, pl.ds(pl.multiple_of(p * 128, 128), 128)], lse_ref.at[p],
+        )
+        for store in stores(p, slot):
+            store.start()
+
+    def output_weight():
+        return jnp.concatenate([wo[n].reshape(-1, wo.shape[5], width) for n in range(2)], axis=1).reshape(width, width)
+
+    def second_norm():
+        for p in (pairs - 2, pairs - 1):
+            for store in stores(p, p % 2):
+                store.wait()
+
+        @pl.loop(0, tiles)
+        def _(i):
+            rows = rows_of(i)
+            value = x[rows, :].astype(F32) + (dot_nn(att[rows, :], output_weight()) + bo_ref[...])
+            mid[rows, :] = value
+            hat, _ = norm_parts(value)
+            norm[rows, :] = (hat * gain_ref[1:2, :] + shift_ref[1:2, :]).astype(BF16)
+            acc[rows, :] = jnp.zeros((TILE, width), F32)
+            gacc[rows, :] = jnp.zeros((TILE, width), F32)
 
     def chunk(j):
         e = ew.at[j]
@@ -284,26 +357,30 @@
             rows = rows_of(i)
             ev = e[...].reshape(width, -1)
             cv = c[...].reshape(-1, width)
-            active, slope = gelu_both(dot_nn(n2[rows, :], ev) + bias)
+            active, slope = gelu_both(dot_nn(norm[rows, :], ev) + bias)
             grad = (dot_nt(cot[rows, :], cv) * slope).astype(BF16)
             acc[rows, :] += dot_nn(active.astype(BF16), cv)
             gacc[rows, :] += dot_nt(grad, ev)
 
-    @pl.loop(0, max(count + 3 * LAG, tiles))
+    @pl.loop(0, FF_TICK + chunks)
     def _(t):
-        gather.tick(t, count)
-
-        @pl.when(t < tiles)
+        gather.tick(t)
+        pl.when(t == 0)(first_norm)
+        pl.when(t == 1)(prefix_rows)
+        p = t - PAIR_TICK
+
+        @pl.when((p >= 0) & (p < pairs))
         def _():
-            before(t)
-
-        j = t - 3 * LAG
-
-        @pl.when((j >= 0) & (j < count))
+            pair(p)
+
+        pl.when(t == PAIR_TICK + pairs)(second_norm)
+        j = t - FF_TICK
+
+        @pl.when(j >= 0)
         def _():
             chunk(j)
 
-    def stores(i):
+    def results(i):
         rows = rows_of(i)
         return [
             pltpu.make_async_copy(src.at[rows, :], dst.at[rows, :], out_sems.at[n, i])
@@ -316,53 +393,64 @@
         value = mid[rows, :]
         x[rows, :] = (value + (acc[rows, :] + bc_ref[...])).astype(BF16)
         hat, rate = norm_parts(value)
-        grad = cot[rows, :].astype(F32) + norm_back(hat, rate, gacc[rows, :], gain)
+        grad = cot[rows, :].astype(F32) + norm_back(hat, rate, gacc[rows, :], gain_ref[1:2, :])
         gacc[rows, :] = grad
-        att[rows, :] = dot_nt(grad.astype(BF16), wo[...]).astype(BF16)
-        for store in stores(i):
-            store.start()
-
-    gather.finish(count)
+        att[rows, :] = dot_nt(grad.astype(BF16), output_weight()).astype(BF16)
+        for result in results(i):
+            result.start()
+
+    gather.finish()
+
+    @pl.loop(0, pairs)
+    def _(p):
+        keep_mixer(p).wait()
 
     @pl.loop(0, tiles)
     def _(i):
-        for store in stores(i):
-            store.wait()
-
-
-def feed_forward(dims, x, cot, attended, full_output, e_shard, c_shard, bo, be, bc, gain, shift):
+        for result in results(i):
+            result.wait()
+
+
+def layer(dims, x, lengths, cot, m_shard, w_shard, e_shard, c_shard, reparam_in, reparam_out, embed, reparam_in_bias,
+          reparam_out_bias, mixer_bias, output_bias, expand_bias, contract_bias, gains, shifts, prefix, most):
     length, width = x.shape
-    chunks = e_shard.shape[0]
-    columns = be.shape[1]
+    pairs, chunks = m_shard.shape[0], e_shard.shape[0]
+    rep = reparam_in.shape[1]
     anyspace = pl.BlockSpec(memory_space=pl.ANY)
     vmem = pl.BlockSpec(memory_space=pltpu.VMEM)
     dma = pltpu.SemaphoreType.DMA
+    shape = jax.ShapeDtypeStruct
+    held = lambda shard: (shard.shape[0],) + dims + shard.shape[1:]
     full = lambda kind: pltpu.VMEM((length, width), kind)
     return pl.pallas_call(
-        functools.partial(ff_kernel, dims),
-        in_specs=[anyspace] * 6 + [vmem] * 5,
-        out_specs=[anyspace] * 3,
-        out_shape=[jax.ShapeDtypeStruct((length, width), kind) for kind in (BF16, F32, BF16)],
+        functools.partial(layer_kernel, dims, prefix, most, lengths.shape[1]),
+        in_specs=[pl.BlockSpec(memory_space=pltpu.SMEM)] + [anyspace] * 8 + [vmem] * 9,
+        out_specs=[anyspace, anyspace, vmem, vmem, vmem] + [anyspace] * 4,
+        out_shape=[
+            shape((pairs, length, 384), BF16), shape((length, width), BF16), shape((pairs, 2, length), F32),
+            shape((PAD, 2 * width), BF16), shape((PAD, rep), F32), shape(held(m_shard), BF16),
+            shape((length, width), BF16), shape((length, width), F32), shape((length, width), BF16),
+        ],
         scratch_shapes=[
-            pltpu.VMEM((chunks,) + dims + e_shard.shape[1:], BF16),
-            pltpu.VMEM((chunks,) + dims + c_shard.shape[1:], BF16),
-            full(BF16), full(BF16), full(BF16), pltpu.VMEM((width, width), BF16),
-            full(BF16), full(F32), full(F32), full(F32),
-            dma((chunks, 4)), dma((chunks, 4)), dma((chunks,)),
-            dma((chunks, 4)), dma((chunks, 4)), dma((chunks,)),
-            dma((4,)), dma((3, length // TILE)),
+            full(BF16), full(BF16), pltpu.VMEM(held(m_shard), BF16), pltpu.VMEM((2, length, 384), BF16), full(BF16),
+            full(BF16), pltpu.VMEM(held(w_shard), BF16), full(F32), full(F32), full(F32),
+            pltpu.VMEM(held(e_shard), BF16), pltpu.VMEM(held(c_shard), BF16),
+            *gather_sems(pairs // 2), *gather_sems(pairs // 2), *gather_sems(1), *gather_sems(1),
+            *gather_sems(chunks), *gather_sems(chunks),
+            dma((5,)), dma((2,)), dma((2,)), dma((pairs,)), dma((3, length // TILE)),
         ],
-        compiler_params=pltpu.CompilerParams(collective_id=1, has_side_effects=True, vmem_limit_bytes=58 << 20),
-        name="feed_forward",
-    )(x, cot, attended, full_output, e_shard, c_shard, bo, be, bc, gain, shift)
-
-
-def back_kernel(dims, prefix, most, count, len_ref, q_ref, k_ref, v_ref, pk_ref, pv_ref, do_ref, o_ref, lse_ref,
+        compiler_params=pltpu.CompilerParams(collective_id=0, has_side_effects=True, vmem_limit_bytes=60 << 20),
+        name="layer",
+    )(lengths, x, cot, m_shard, w_shard, e_shard, c_shard, reparam_in, reparam_out, embed, reparam_in_bias,
+      reparam_out_bias, mixer_bias, output_bias, expand_bias, contract_bias, gains, shifts)
+
+
+def back_kernel(dims, prefix, most, count, len_ref, mixed_ref, pk_ref, pv_ref, do_ref, o_ref, lse_ref,
                 gain_ref, w_hbm, x_hbm, gm_hbm, gx_hbm, total_ref,
                 dk_acc, dv_acc, dpk, dpv, gmix, w, x, gm, tiles, inbox, sums,
                 in_sems, out_sems, give_send, give_recv, tell_send, tell_recv):
-    length = q_ref.shape[0]
-    width = x.shape[1]
+    length, width = x.shape
+    q_ref, k_ref, v_ref = (mixed_ref.at[0, :, part * 128:(part + 1) * 128] for part in range(3))
     pair = pl.program_id(0)
     pairs = width // 128
     devices = math.prod(dims)
@@ -375,7 +463,9 @@
     place = lambda device: (device // narrow_size, lax.rem(device, narrow_size))
     loads = [
         pltpu.make_async_copy(src, dst, in_sems.at[n])
-        for n, (src, dst) in enumerate(((w_hbm, w), (x_hbm, x), (gm_hbm, gm)))
+        for n, (src, dst) in enumerate(((x_hbm, x), (gm_hbm, gm)))
+    ] + [
+        pltpu.make_async_copy(w_hbm.at[n], w.at[:, n * 384:(n + 1) * 384], in_sems.at[2 + n]) for n in range(pairs)
     ]
     barrier = pltpu.get_barrier_semaphore()
 
@@ -397,7 +487,7 @@
     pk_t = pk.T
     head_of = lax.broadcasted_iota(jnp.int32, (8, 128), 0)
     pick = ((lax.broadcasted_iota(jnp.int32, (8, 128), 1) // 64) == head_of).astype(F32).astype(BF16)
-    columns = [pl.ds(pl.multiple_of(part * width + pair * 128, 128), 128) for part in range(3)]
+    columns = [pl.ds(pl.multiple_of(pair * 384 + part * 128, 128), 128) for part in range(3)]
     for qi in range(length // BLOCK):
         rows = slice(qi * BLOCK, (qi + 1) * BLOCK)
         lo = span(qi, most)
@@ -543,8 +633,8 @@
     return pl.pallas_call(
         functools.partial(back_kernel, dims, prefix, most, count),
         grid=(pairs,),
-        in_specs=[pl.BlockSpec(memory_space=pltpu.SMEM), col(0), col(pairs), col(2 * pairs), pcol(0), pcol(pairs),
-                  col(0), col(0), pl.BlockSpec((1, 2, length), lambda p: (p, 0, 0)),
+        in_specs=[pl.BlockSpec(memory_space=pltpu.SMEM), pl.BlockSpec((1, length, 384), lambda p: (p, 0, 0)),
+                  pcol(0), pcol(pairs), col(0), col(0), pl.BlockSpec((1, 2, length), lambda p: (p, 0, 0)),
                   pl.BlockSpec((1, width), lambda p: (0, 0)), anyspace, anyspace, anyspace],
         out_specs=[anyspace, pl.BlockSpec((4 * pairs, 8, 128), lambda p: (0, 0, 0))],
         out_shape=[jax.ShapeDtypeStruct((length, width), BF16), jax.ShapeDtypeStruct((4 * pairs, 8, 128), F32)],
@@ -553,23 +643,11 @@
             pltpu.VMEM((length, width), BF16), pltpu.VMEM((length, width), F32),
             pltpu.VMEM((4 * pairs, 8, 128), F32), pltpu.VMEM((devices, 8, 128), F32),
             pltpu.VMEM((4 * pairs, 8, 128), F32),
-            dma((3,)), dma((length // 256,)), dma(()), dma(()), dma(()), dma(()),
+            dma((2 + pairs,)), dma((length // 256,)), dma(()), dma(()), dma(()), dma(()),
         ],
         compiler_params=pltpu.CompilerParams(collective_id=2, has_side_effects=True, vmem_limit_bytes=56 << 20),
         name="attend_back",
-    )(lengths, mixed, mixed, mixed, pre, pre, grad, attended, lse, gain, full_mixer, x, grad_middle)
-
-
-def split(value):
-    high = value.astype(BF16)
-    return high, (value - high.astype(F32)).astype(BF16)
-
-
-def dot_fine(left, right, dims):
-    lh, ll = split(left)
-    rh, rl = split(right)
-    one = lambda a, b: lax.dot_general(a, b, (dims, ((), ())), preferred_element_type=F32)
-    return one(lh, rh) + (one(lh, rl) + one(ll, rh))
+    )(lengths, mixed, pre, pre, grad, attended, lse, gain, full_mixer, x, grad_middle)
 
 
 def reparam_kernel(prefix, total_ref, sq_ref, embed_ref, ro_ref, ri_ref, gx_hbm, out_hbm,
@@ -657,8 +735,6 @@
 ):
     row_count, length, model_width = tokens.shape
     total_rows = row_count * length
-    full_mixer = lax.all_gather(mixer_weight, ("wide", "narrow"), axis=0, tiled=True)
-    full_output = lax.all_gather(output_weight, ("wide", "narrow"), axis=0, tiled=True)
     devices = math.prod(dims)
     hidden = expand_weight.shape[1]
     part = hidden // devices // CHUNKS
@@ -668,31 +744,24 @@
     contract_parts = contract_weight.reshape(CHUNKS, part, model_width)
     prefix_count = prefix_embed.shape[0]
     tall = lambda array: jnp.pad(array, ((0, PAD - prefix_count), (0, 0)))
-    squashed = jnp.tanh(
-        jnp.dot(prefix_embed, reparam_in, precision=lax.Precision.HIGHEST) + reparam_in_bias
-    )
-    prefix_kv = jnp.dot(squashed, reparam_out, precision=lax.Precision.HIGHEST) + reparam_out_bias
-    pre = tall(prefix_kv.astype(jnp.bfloat16))
-    inputs = tokens.reshape(total_rows, model_width).astype(jnp.float32)
-    normed_one = norm_layer(inputs, norm_gains[0], norm_shifts[0])
-    mixed = (
-        jnp.dot(normed_one.astype(jnp.bfloat16), full_mixer, preferred_element_type=jnp.float32)
-        + mixer_bias
-    )
-    mixed_low = mixed.astype(jnp.bfloat16)
-    attended, log_sums = attend(mixed_low, lengths, pre, prefix_count, MOST)
+    rows = mixer_weight.shape[0]
+    pairs = model_width // 128
+    mixer_parts = mixer_weight.reshape(rows, 3, pairs, 128).transpose(2, 0, 1, 3).reshape(pairs, rows, 384)
+    x = tokens.reshape(total_rows, model_width)
     as_row = lambda array: array.reshape(1, -1)
-    out_tokens, grad_middle, grad_attended = feed_forward(
-        dims, tokens.reshape(total_rows, model_width), cotangent.reshape(total_rows, model_width), attended, full_output,
-        expand_parts, contract_parts, as_row(output_bias), expand_bias_parts, as_row(contract_bias),
-        norm_gains[1:2], norm_shifts[1:2],
+    embed = tall(prefix_embed)
+    mixed, attended, log_sums, pre, squashed, full_mixer, out_tokens, grad_middle, grad_attended = layer(
+        dims, x, lengths, cotangent.reshape(total_rows, model_width), mixer_parts,
+        output_weight.reshape(2, rows // 2, model_width), expand_parts, contract_parts, reparam_in, reparam_out, embed,
+        as_row(reparam_in_bias), as_row(reparam_out_bias), as_row(mixer_bias), as_row(output_bias), expand_bias_parts,
+        as_row(contract_bias), norm_gains, norm_shifts, prefix_count, MOST,
     )
     grad_tokens, total = attend_back(
-        dims, mixed_low, lengths, pre, grad_attended, attended, log_sums, norm_gains[0:1], full_mixer,
-        tokens.reshape(total_rows, model_width), grad_middle, prefix_count, MOST,
+        dims, mixed, lengths, pre, grad_attended, attended, log_sums, norm_gains[0:1],
+        full_mixer.reshape(pairs, model_width, 384), x, grad_middle, prefix_count, MOST,
     )
     grad_tokens, out_tokens, grad_embed, grad_in, grad_in_bias, grad_out, grad_out_bias = reparam_back(
-        total, tall(squashed), tall(prefix_embed), reparam_out, reparam_in, grad_tokens, out_tokens, prefix_count
+        total, squashed, embed, reparam_out, reparam_in, grad_tokens, out_tokens, prefix_count
     )
     return (
         out_tokens.reshape(tokens.shape), grad_tokens.reshape(tokens.shape), grad_embed, grad_in, grad_in_bias[0],

time: 331 us -> 245 us (0.74)
  waiting for transfers between devices: 77.7 us -> 0 us
  Pallas kernels: 208 us -> 232 us
  matrix products: 17.4 us -> 0 us
  between operations: 14.3 us -> 0.93 us
    all_gather x2 -> x0, waiting for transfers between devices: 76.4 us -> none  [the longest x1 61.8 us: shards(): lax.all_gather(mixer_weight, ('wide', 'narrow'), axis=0, tiled=True)]
    pallas_call x2 -> x1, Pallas kernels: 138 us -> 162 us  [layer(): pl.pallas_call(functools.partial(layer_kernel, dims, prefix, most, length...]
    dot_general x3 -> x0, matrix products: 17.4 us -> none  [the longest x1 12 us: shards(): jnp.dot(normed_one.astype(jnp.bfloat16), full_mixer, preferred_element_ty...]
    unnamed x37 -> x18, local copies, waits for them, and re-layouts: 8.35 us -> 5.53 us
  transfers between devices with their start and end apart: 2 -> 0, of which waited for: 2 -> 0; matrix products, arithmetic and copies ran while one was open for 7% -> 0% of each run, Pallas kernels for 9% -> 0%
where the time goes in v4:
time: 245 us
  Pallas kernels  232 us (95%)
  local copies, waits for them, and re-layouts  12.1 us (5%)
    pallas_call x1, Pallas kernels, layer(): pl.pallas_call(functools.partial(layer_kernel, dims, prefix, most, length...  162 us
    pallas_call x1, Pallas kernels, attend_back(): pl.pallas_call(functools.partial(back_kernel, dims, prefix, most, count),...  61.4 us
    pallas_call x1, Pallas kernels, reparam_back(): pl.pallas_call(functools.partial(reparam_kernel, prefix), grid=(steps,),...  7.96 us
    unnamed x18, local copies, waits for them, and re-layouts  5.53 us

profile of v4, /device:TPU:0, one launch (start us, length us, event | category | flops | bytes accessed | tf_op | source)
XLA Modules:
  0.0 244.7 jit_solution(4960089315713507412)
XLA Ops:
  0.6 0.0 copy-start.7
  0.6 1.3 slice.3.gain_ref
  2.0 1.5 pad.4.embed_ref
  3.5 0.8 reshape.77
  4.3 0.7 squeeze_reshape.3.be_ref
  5.0 1.0 copy.32
  6.0 0.1 copy.34
  6.1 0.8 reshape.68.m_hbm
  6.9 0.0 copy-done.7
  6.9 0.5 copy.28
  7.4 0.2 copy.29
  7.6 1.0 copy.31.e_hbm
  8.6 162.3 %layer.1 = (bf16[8,1024,384]{2,1,0:T(8,128)(2,1)}, bf16[1024,1024]{1,0:T(8,128)(2,1)}, f32[8,2,1024]{2,1,0:T(2,128)}, bf16[16,2048]{1,0:T(8,128)(2,1)}, f32[16,5...) custom-call(s32[1,8]{1,0:T(1,128)} %len_ref.3, ...), custom_call_target="tpu_custom_call" | custom-call | tf_op jit(solution)/shard_map/layer/pallas_call | solution.py:425
  171.0 0.0 copy-start
  171.0 0.0 copy-start.1
  171.0 0.0 copy-start.4
  171.0 0.0 copy-start.6
  171.0 61.4 %attend_back.1 = (bf16[1024,1024]{1,0:T(8,128)(2,1)}, f32[32,8,128]{2,1,0:T(8,128)}) custom-call(s32[1,8]{1,0:T(1,128)} %len_ref.3, bf16[8,1024,384]{2,1,0:T(8,128)(2,1)} %get-tuple-element.25.mixed_ref, bf16[16,2048]{1,0:T(8,128)(2,1)} %get-tuple-element.26.pk_ref.pv_ref, bf16[16,2048]{1,0:T(8,128)(2,1)} %get-tuple-element.26.pk_ref.pv_ref, ...), custom_call_target="tpu_custom_call" | custom-call | tf_op jit(solution)/shard_map/attend_back/pallas_call | solution.py:633
  232.5 0.0 copy-done
  232.5 0.0 copy-done.1
  232.5 0.0 copy-done.4
  232.5 0.0 copy-done.6
  232.5 0.0 copy-start.2
  232.5 1.6 copy-done.2
  234.1 0.0 copy-start.3
  234.1 1.6 copy-done.3
  235.7 0.0 copy-start.5
  235.7 0.9 copy-done.5
  236.6 8.0 %reparam_back.1 = (bf16[1024,1024]{1,0:T(8,128)(2,1)}, bf16[1024,1024]{1,0:T(8,128)(2,1)}, f32[10,1024]{1,0:T(8,128)}, f32[1024,512]{1,0:T(8,128)}, f32[1,512]{1...) custom-call(f32[32,8,128]{2,1,0:T(8,128)S(1)} %copy-done.5, f32[16,512]{1,0:T(8,128)S(1)} %copy-done.6, ...), custom_call_target="tpu_custom_call" | custom-call | tf_op jit(solution)/shard_map/reparam_back/pallas_call | solution.py:698
  (1 shorter events, 0.0 us)
Async XLA Ops:
  0.6 6.3 %copy-start.7 = (bf16[32,4096]{1,0:T(8,128)(2,1)S(1)}, bf16[32,4096]{1,0:T(8,128)(2,1)}, u32[]{:S(2)}) copy-start(bf16[32,4096]{1,0:T(8,128)(2,1)} %param.23) | copy-start | bytes 786436
  171.0 61.5 %copy-start = (f32[512,2048]{1,0:T(8,128)S(1)}, f32[512,2048]{1,0:T(8,128)}, u32[]{:S(2)}) copy-start(f32[512,2048]{1,0:T(8,128)} %ro_ref.1) | copy-start | bytes 12582916
  171.0 61.5 %copy-start.1 = (f32[1024,512]{1,0:T(8,128)S(1)}, f32[1024,512]{1,0:T(8,128)}, u32[]{:S(2)}) copy-start(f32[1024,512]{1,0:T(8,128)} %ri_ref.1) | copy-start | bytes 6291460
  171.0 61.5 %copy-start.4 = (f32[16,1024]{1,0:T(8,128)S(1)}, f32[16,1024]{1,0:T(8,128)}, u32[]{:S(2)}) copy-start(f32[16,1024]{1,0:T(8,128)} %pad.4.embed_ref) | copy-start | bytes 196612
  171.0 61.5 %copy-start.6 = (f32[16,512]{1,0:T(8,128)S(1)}, f32[16,512]{1,0:T(8,128)}, u32[]{:S(2)}) copy-start(f32[16,512]{1,0:T(8,128)} %get-tuple-element.33.sq_ref) | copy-start | bytes 98308
  232.5 1.6 copy-start.2
  234.1 1.6 copy-start.3
  235.7 0.9 copy-start.5

commit v5 on v4

--- a/solution.py
+++ b/solution.py
@@ -47,19 +47,19 @@
     return max(0, qi - most // BLOCK)
 
 
-def fwd_pair(q2, k_ref, v_ref, pk, pv, start, prefix, most, o_ref, lse_ref):
-    length = q2.shape[0]
+def fwd_pair(q_ref, k_ref, v_ref, pk, pv, start, prefix, most, o_ref, lse_ref, blocks):
     lane = lax.broadcasted_iota(jnp.int32, (1, 128), 1)
     pre_seen = lax.broadcasted_iota(jnp.int32, (PAD, BLOCK), 0) < prefix
-    v_t = v_ref[...].T
+    v_t = v_ref[:(max(blocks) + 1) * BLOCK, :].T
     pv_t = pv.T
-    for qi in range(length // BLOCK):
+    for qi in blocks:
         rows = slice(qi * BLOCK, (qi + 1) * BLOCK)
         lo = span(qi, most)
         st = start[:, rows]
+        q2 = q_ref[rows, :] * jnp.asarray(0.125, BF16)
         halves = []
         for h in range(2):
-            qh = jnp.where((lane // 64) == h, q2[rows], jnp.zeros((), BF16))
+            qh = jnp.where((lane // 64) == h, q2, jnp.zeros((), BF16))
             s_pre = jnp.where(pre_seen, dot_nt(pk, qh), -1e30)
             peak = jnp.max(s_pre, axis=0, keepdims=True)
             parts = []
@@ -92,25 +92,30 @@
 
 
 class Family:
-    def __init__(self, source, target, order, sems, count, first=0, stride=1, offset=0, pace=1, lag=1, ahead=3):
-        self.source, self.target, self.order = source, target, order
+    def __init__(self, source, target, order, sems, part=()):
+        self.source, self.target, self.order, self.part = source, target, order, part
         self.send, self.recv, self.own = sems
-        self.count, self.first, self.stride = count, first, stride
-        self.offset, self.pace, self.lag, self.ahead = offset, pace, lag, ahead
-
-    def block(self, j):
-        return self.first + self.stride * j
-
-    def end(self):
-        return self.offset + self.pace * (self.count - 1) + 3 * self.lag + 1
+
+
+class Group:
+    def __init__(self, families, offset, lag, ahead):
+        self.families, self.offset, self.lag, self.ahead = families, offset, lag, ahead
+        self.count = families[0].source.shape[0]
+
+    def tick(self, stage):
+        return self.offset + (self.lag * stage if stage >= 0 else -self.ahead)
 
 
 class Gather:
-    def __init__(self, dims, families):
+    def __init__(self, dims, groups):
         self.dims = dims
         wide, narrow = lax.axis_index("wide"), lax.axis_index("narrow")
         self.at = (wide // dims[1], lax.rem(wide, dims[1]), narrow // dims[3], lax.rem(narrow, dims[3]))
-        self.families = families
+        self.groups = groups
+        self.peers = [
+            [self.device(dim, lax.rem(self.at[dim] + step, size)) for step in range(1, size)]
+            for dim, size in enumerate(dims)
+        ]
 
     def device(self, dim, index):
         at = list(self.at)
@@ -119,48 +124,45 @@
 
     def greet(self):
         barrier = pltpu.get_barrier_semaphore()
-        count = 0
-        for dim, size in enumerate(self.dims):
-            for step in range(1, size):
-                peer = self.device(dim, lax.rem(self.at[dim] + step, size))
+        for peers in self.peers:
+            for peer in peers:
                 pl.semaphore_signal(barrier, inc=1, device_id=peer, device_id_type=MESH)
-                count += 1
-        pl.semaphore_wait(barrier, count)
+        pl.semaphore_wait(barrier, sum(len(peers) for peers in self.peers))
 
     def view(self, family, j, stage, index):
         done, dim = family.order[:stage], family.order[stage]
         return family.target.at[
-            (family.block(j),)
+            (j,)
             + tuple(slice(None) if d in done else (index if d == dim else self.at[d]) for d in range(4))
+            + family.part
         ]
 
     def keep(self, family, j):
-        block = family.block(j)
-        return pltpu.make_async_copy(family.source.at[block], family.target.at[(block,) + self.at], family.own.at[j])
+        return pltpu.make_async_copy(
+            family.source.at[(j,) + family.part], family.target.at[(j,) + self.at + family.part], family.own.at[j]
+        )
 
     def start(self, family, j, stage):
         dim = family.order[stage]
-        size = self.dims[dim]
         if stage == 0:
             self.keep(family, j).start()
         mine = self.view(family, j, stage, self.at[dim])
-        for step in range(1, size):
+        for peer in self.peers[dim]:
             pltpu.make_async_remote_copy(
-                src_ref=family.source.at[family.block(j)] if stage == 0 else mine,
+                src_ref=family.source.at[(j,) + family.part] if stage == 0 else mine,
                 dst_ref=mine,
                 send_sem=family.send.at[j, stage],
                 recv_sem=family.recv.at[j, stage],
-                device_id=self.device(dim, lax.rem(self.at[dim] + step, size)),
+                device_id=peer,
                 device_id_type=MESH,
             ).start()
 
     def whole(self, family, j, stage):
         dim = family.order[stage]
-        size = self.dims[dim]
-        part = self.view(family, j, stage, pl.ds(0, size - 1))
+        part = self.view(family, j, stage, pl.ds(0, self.dims[dim] - 1))
         return pltpu.make_async_remote_copy(
             src_ref=part, dst_ref=part, send_sem=family.send.at[j, stage], recv_sem=family.recv.at[j, stage],
-            device_id=self.device(dim, lax.rem(self.at[dim] + 1, size)), device_id_type=MESH,
+            device_id=self.peers[dim][0], device_id_type=MESH,
         )
 
     def arrive(self, family, j, stage):
@@ -169,31 +171,36 @@
         self.whole(family, j, stage).wait_recv()
 
     def begin(self):
-        for family in self.families:
-            for j in range(family.count):
-                if family.offset + family.pace * j < family.ahead:
-                    self.start(family, j, 0)
-
-    def tick(self, t):
+        for group in self.groups:
+            for j in range(group.count):
+                if group.tick(-1) + 2 * j < 0:
+                    for family in group.families:
+                        self.start(family, j, 0)
+
+    def tick(self, double, half):
         for stage in (3, 2, 1, 0, -1):
-            for family in self.families:
-                past = t - family.offset - (family.lag * stage if stage >= 0 else -family.ahead)
-                j = past // family.pace
-
-                @pl.when((past >= 0) & (j < family.count) & (lax.rem(past, family.pace) == 0))
+            for group in self.groups:
+                past = half - group.tick(stage)
+                if past % 2:
+                    continue
+                j = double + past // 2
+
+                @pl.when((j >= 0) & (j < group.count))
                 def _():
-                    if stage >= 0:
-                        self.arrive(family, j, stage)
-                    if stage < 3:
-                        self.start(family, j, stage + 1)
+                    for family in group.families:
+                        if stage >= 0:
+                            self.arrive(family, j, stage)
+                        if stage < 3:
+                            self.start(family, j, stage + 1)
 
     def finish(self):
-        for family in self.families:
-
-            @pl.loop(0, family.count)
+        for group in self.groups:
+
+            @pl.loop(0, group.count)
             def _(j):
-                for stage in range(4):
-                    self.whole(family, j, stage).wait_send()
+                for family in group.families:
+                    for stage in range(4):
+                        self.whole(family, j, stage).wait_send()
 
 
 def gather_sems(count):
@@ -237,8 +244,13 @@
     return v * half, slope
 
 
-PAIR_TICK = 3
-FF_TICK = 12
+M_LAG = 3
+PAIR_TICK = 9
+MID_TICK = 25
+FF_TICK = 27
+FF_LAG = 3
+W_TICK = 12
+AHEAD = 5
 
 
 def layer_kernel(dims, prefix, most, count, len_ref, x_hbm, cot_hbm, m_hbm, w_hbm, e_hbm, c_hbm, ri_hbm, ro_hbm,
@@ -251,14 +263,19 @@
     length, width = x.shape
     pairs, chunks = m_hbm.shape[0], e_hbm.shape[0]
     rep = sq_ref.shape[1]
-    half = pairs // 2
+    both = lambda rows: [(order, (pl.ds(n * rows // 2, rows // 2),)) for n, order in enumerate((XY, YX))]
+    m_sems = ((m0_send, m0_recv, m0_own), (m1_send, m1_recv, m1_own))
+    w_sems = ((w0_send, w0_recv, w0_own), (w1_send, w1_recv, w1_own))
+    halves = lambda rows: [(order, (pl.ds(n * rows // 2, rows // 2),)) for n, order in enumerate((XY, YX))]
+    m_sems = ((m0_send, m0_recv, m0_own), (m1_send, m1_recv, m1_own))
+    w_sems = ((w0_send, w0_recv, w0_own), (w1_send, w1_recv, w1_own))
     gather = Gather(dims, [
-        Family(m_hbm, mixer, XY, (m0_send, m0_recv, m0_own), half, first=0, stride=2, offset=0, pace=2),
-        Family(m_hbm, mixer, YX, (m1_send, m1_recv, m1_own), half, first=1, stride=2, offset=1, pace=2),
-        Family(w_hbm, wo, XY, (w0_send, w0_recv, w0_own), 1, first=0, offset=FF_TICK - 6),
-        Family(w_hbm, wo, YX, (w1_send, w1_recv, w1_own), 1, first=1, offset=FF_TICK - 6),
-        Family(e_hbm, ew, XY, (e_send, e_recv, e_own), chunks, offset=FF_TICK - 6, lag=2),
-        Family(c_hbm, cw, YX, (c_send, c_recv, c_own), chunks, offset=FF_TICK - 6, lag=2),
+        Group([Family(m_hbm, mixer, order, m_sems[n], part) for n, (order, part) in enumerate(halves(m_hbm.shape[1]))],
+              0, M_LAG, AHEAD),
+        Group([Family(w_hbm, wo, order, w_sems[n], part) for n, (order, part) in enumerate(halves(w_hbm.shape[1]))],
+              W_TICK, 2, AHEAD),
+        Group([Family(e_hbm, ew, XY, (e_send, e_recv, e_own)), Family(c_hbm, cw, YX, (c_send, c_recv, c_own))],
+              FF_TICK - 3 * FF_LAG, FF_LAG, AHEAD),
     ])
     loads = [
         pltpu.make_async_copy(src, dst, in_sems.at[n])
@@ -306,38 +323,42 @@
     def keep_mixer(p):
         return pltpu.make_async_copy(mixer.at[p], mixer_hbm.at[p], mixer_sems.at[p])
 
-    def pair(p):
+    def pair(p, part):
         slot = lax.rem(p, 2)
-
-        @pl.when(p >= 2)
-        def _():
-            for store in stores(p - 2, slot):
-                store.wait()
-
-        keep_mixer(p).start()
-        weight = mixer[pl.ds(p, 1)].reshape(width, 384)
-        at = [pl.ds(pl.multiple_of(part * width + p * 128, 128), 128) for part in range(3)]
-        bias = jnp.concatenate([mb_ref[:, columns] for columns in at], axis=1)
-        mixed[pl.ds(slot, 1)] = (dot_nn(norm[...], weight) + bias).astype(BF16)[None]
+        at = [pl.ds(pl.multiple_of(third * width + p * 128, 128), 128) for third in range(3)]
         here = mixed.at[slot]
-        q2 = here[:, 0:128] * jnp.asarray(0.125, BF16)
-        start = start_row(len_ref, count, length)
+
+        if part == 0:
+
+            @pl.when(p >= 2)
+            def _():
+                for store in stores(p - 2, slot):
+                    store.wait()
+
+            keep_mixer(p).start()
+            weight = mixer[pl.ds(p, 1)].reshape(width, 384)
+            bias = jnp.concatenate([mb_ref[:, columns] for columns in at], axis=1)
+            mixed[pl.ds(slot, 1)] = (dot_nn(norm[...], weight) + bias).astype(BF16)[None]
+        blocks = length // BLOCK
         fwd_pair(
-            q2, here.at[:, 128:256], here.at[:, 256:384], pre_ref[:, at[0]], pre_ref[:, at[1]],
-            start, prefix, most, att.at[:, pl.ds(pl.multiple_of(p * 128, 128), 128)], lse_ref.at[p],
+            here.at[:, 0:128], here.at[:, 128:256], here.at[:, 256:384], pre_ref[:, at[0]], pre_ref[:, at[1]],
+            start_row(len_ref, count, length), prefix, most, att.at[:, at[0]], lse_ref.at[p],
+            range(blocks // 2) if part == 0 else range(blocks // 2, blocks),
         )
-        for store in stores(p, slot):
-            store.start()
+        if part == 1:
+            for store in stores(p, slot):
+                store.start()
 
     def output_weight():
-        return jnp.concatenate([wo[n].reshape(-1, wo.shape[5], width) for n in range(2)], axis=1).reshape(width, width)
-
-    def second_norm():
-        for p in (pairs - 2, pairs - 1):
-            for store in stores(p, p % 2):
-                store.wait()
-
-        @pl.loop(0, tiles)
+        return wo[0].reshape(width, width)
+
+    def second_norm(part):
+        if part == 0:
+            for p in (pairs - 2, pairs - 1):
+                for store in stores(p, p % 2):
+                    store.wait()
+
+        @pl.loop(part * tiles // 2, (part + 1) * tiles // 2)
         def _(i):
             rows = rows_of(i)
             value = x[rows, :].astype(F32) + (dot_nn(att[rows, :], output_weight()) + bo_ref[...])
@@ -347,12 +368,12 @@
             acc[rows, :] = jnp.zeros((TILE, width), F32)
             gacc[rows, :] = jnp.zeros((TILE, width), F32)
 
-    def chunk(j):
+    def chunk(j, part):
         e = ew.at[j]
         c = cw.at[j]
         bias = be_ref[pl.ds(j, 1), :]
 
-        @pl.loop(0, tiles)
+        @pl.loop(part * tiles // 2, (part + 1) * tiles // 2)
         def _(i):
             rows = rows_of(i)
             ev = e[...].reshape(width, -1)
@@ -362,23 +383,29 @@
             acc[rows, :] += dot_nn(active.astype(BF16), cv)
             gacc[rows, :] += dot_nt(grad, ev)
 
-    @pl.loop(0, FF_TICK + chunks)
-    def _(t):
-        gather.tick(t)
-        pl.when(t == 0)(first_norm)
-        pl.when(t == 1)(prefix_rows)
-        p = t - PAIR_TICK
-
-        @pl.when((p >= 0) & (p < pairs))
-        def _():
-            pair(p)
-
-        pl.when(t == PAIR_TICK + pairs)(second_norm)
-        j = t - FF_TICK
-
-        @pl.when(j >= 0)
-        def _():
-            chunk(j)
+    @pl.loop(0, (FF_TICK + 2 * chunks + 1) // 2)
+    def _(double):
+        for half in range(2):
+            gather.tick(double, half)
+            if half == 0:
+                pl.when(double == 0)(first_norm)
+            else:
+                pl.when(double == 0)(prefix_rows)
+            part = (half - PAIR_TICK) % 2
+            p = double + (half - PAIR_TICK) // 2
+
+            @pl.when((p >= 0) & (p < pairs))
+            def _():
+                pair(p, part)
+
+            part = (half - MID_TICK) % 2
+            pl.when(double + (half - MID_TICK) // 2 == 0)(functools.partial(second_norm, part))
+            part = (half - FF_TICK) % 2
+            j = double + (half - FF_TICK) // 2
+
+            @pl.when((j >= 0) & (j < chunks))
+            def _():
+                chunk(j, part)
 
     def results(i):
         rows = rows_of(i)
@@ -435,7 +462,7 @@
             full(BF16), full(BF16), pltpu.VMEM(held(m_shard), BF16), pltpu.VMEM((2, length, 384), BF16), full(BF16),
             full(BF16), pltpu.VMEM(held(w_shard), BF16), full(F32), full(F32), full(F32),
             pltpu.VMEM(held(e_shard), BF16), pltpu.VMEM(held(c_shard), BF16),
-            *gather_sems(pairs // 2), *gather_sems(pairs // 2), *gather_sems(1), *gather_sems(1),
+            *gather_sems(pairs), *gather_sems(pairs), *gather_sems(1), *gather_sems(1),
             *gather_sems(chunks), *gather_sems(chunks),
             dma((5,)), dma((2,)), dma((2,)), dma((pairs,)), dma((3, length // TILE)),
         ],
@@ -752,7 +779,7 @@
     embed = tall(prefix_embed)
     mixed, attended, log_sums, pre, squashed, full_mixer, out_tokens, grad_middle, grad_attended = layer(
         dims, x, lengths, cotangent.reshape(total_rows, model_width), mixer_parts,
-        output_weight.reshape(2, rows // 2, model_width), expand_parts, contract_parts, reparam_in, reparam_out, embed,
+        output_weight[None], expand_parts, contract_parts, reparam_in, reparam_out, embed,
         as_row(reparam_in_bias), as_row(reparam_out_bias), as_row(mixer_bias), as_row(output_bias), expand_bias_parts,
         as_row(contract_bias), norm_gains, norm_shifts, prefix_count, MOST,
     )

time: 245 us -> 230 us (0.939)
  Pallas kernels: 232 us -> 216 us
    pallas_call x1, Pallas kernels: 162 us -> 148 us  [layer(): pl.pallas_call(functools.partial(layer_kernel, dims, prefix, most, length...]
where the time goes in v5:
time: 230 us; the launch traced here: 229 us
  Pallas kernels  216 us (94%)
  local copies, waits for them, and re-layouts  12.1 us (5%)
    pallas_call x1, Pallas kernels, layer(): pl.pallas_call(functools.partial(layer_kernel, dims, prefix, most, length...  148 us
    pallas_call x1, Pallas kernels, attend_back(): pl.pallas_call(functools.partial(back_kernel, dims, prefix, most, count),...  60.5 us
    pallas_call x1, Pallas kernels, reparam_back(): pl.pallas_call(functools.partial(reparam_kernel, prefix), grid=(steps,),...  7.96 us
    unnamed x18, local copies, waits for them, and re-layouts  5.53 us

profile of v5, /device:TPU:0, one launch (start us, length us, event | category | flops | bytes accessed | tf_op | source)
XLA Modules:
  0.0 229.4 jit_solution(2793563696848961162)
XLA Ops:
  0.6 0.0 copy-start.7
  0.6 1.3 slice.3.gain_ref
  2.0 1.5 pad.4.embed_ref
  3.5 0.8 reshape.73
  4.3 0.7 squeeze_reshape.3.be_ref
  5.0 1.0 copy.32
  6.0 0.1 copy.34
  6.1 0.8 reshape.65.m_hbm
  6.9 0.0 copy-done.7
  6.9 0.5 copy.28
  7.4 0.2 copy.29
  7.6 1.0 copy.31.e_hbm
  8.6 147.9 %layer.1 = (bf16[8,1024,384]{2,1,0:T(8,128)(2,1)}, bf16[1024,1024]{1,0:T(8,128)(2,1)}, f32[8,2,1024]{2,1,0:T(2,128)}, bf16[16,2048]{1,0:T(8,128)(2,1)}, f32[16,5...) custom-call(s32[1,8]{1,0:T(1,128)} %len_ref.3, ...), custom_call_target="tpu_custom_call" | custom-call | tf_op jit(solution)/shard_map/layer/pallas_call | solution.py:452
  156.6 0.0 copy-start
  156.6 0.0 copy-start.1
  156.6 0.0 copy-start.4
  156.6 0.0 copy-start.6
  156.6 60.5 %attend_back.1 = (bf16[1024,1024]{1,0:T(8,128)(2,1)}, f32[32,8,128]{2,1,0:T(8,128)}) custom-call(s32[1,8]{1,0:T(1,128)} %len_ref.3, bf16[8,1024,384]{2,1,0:T(8,128)(2,1)} %get-tuple-element.25.mixed_ref, bf16[16,2048]{1,0:T(8,128)(2,1)} %get-tuple-element.26.pk_ref.pv_ref, bf16[16,2048]{1,0:T(8,128)(2,1)} %get-tuple-element.26.pk_ref.pv_ref, ...), custom_call_target="tpu_custom_call" | custom-call | tf_op jit(solution)/shard_map/attend_back/pallas_call | solution.py:660
  217.2 0.0 copy-done
  217.2 0.0 copy-done.1
  217.2 0.0 copy-done.4
  217.2 0.0 copy-done.6
  217.2 0.0 copy-start.2
  217.2 1.6 copy-done.2
  218.8 0.0 copy-start.3
  218.8 1.6 copy-done.3
  220.4 0.0 copy-start.5
  220.4 0.9 copy-done.5
  221.3 8.0 %reparam_back.1 = (bf16[1024,1024]{1,0:T(8,128)(2,1)}, bf16[1024,1024]{1,0:T(8,128)(2,1)}, f32[10,1024]{1,0:T(8,128)}, f32[1024,512]{1,0:T(8,128)}, f32[1,512]{1...) custom-call(f32[32,8,128]{2,1,0:T(8,128)S(1)} %copy-done.5, f32[16,512]{1,0:T(8,128)S(1)} %copy-done.6, ...), custom_call_target="tpu_custom_call" | custom-call | tf_op jit(solution)/shard_map/reparam_back/pallas_call | solution.py:725
  (1 shorter events, 0.0 us)
Async XLA Ops:
  0.6 6.3 %copy-start.7 = (bf16[32,4096]{1,0:T(8,128)(2,1)S(1)}, bf16[32,4096]{1,0:T(8,128)(2,1)}, u32[]{:S(2)}) copy-start(bf16[32,4096]{1,0:T(8,128)(2,1)} %param.23) | copy-start | bytes 786436
  156.6 60.6 %copy-start = (f32[512,2048]{1,0:T(8,128)S(1)}, f32[512,2048]{1,0:T(8,128)}, u32[]{:S(2)}) copy-start(f32[512,2048]{1,0:T(8,128)} %ro_ref.1) | copy-start | bytes 12582916
  156.6 60.6 %copy-start.1 = (f32[1024,512]{1,0:T(8,128)S(1)}, f32[1024,512]{1,0:T(8,128)}, u32[]{:S(2)}) copy-start(f32[1024,512]{1,0:T(8,128)} %ri_ref.1) | copy-start | bytes 6291460
  156.6 60.6 %copy-start.4 = (f32[16,1024]{1,0:T(8,128)S(1)}, f32[16,1024]{1,0:T(8,128)}, u32[]{:S(2)}) copy-start(f32[16,1024]{1,0:T(8,128)} %pad.4.embed_ref) | copy-start | bytes 196612
  156.6 60.6 %copy-start.6 = (f32[16,512]{1,0:T(8,128)S(1)}, f32[16,512]{1,0:T(8,128)}, u32[]{:S(2)}) copy-start(f32[16,512]{1,0:T(8,128)} %get-tuple-element.33.sq_ref) | copy-start | bytes 98308
  217.2 1.6 copy-start.2
  218.8 1.6 copy-start.3
  220.4 0.9 copy-start.5

commit v6 on v5

--- a/solution.py
+++ b/solution.py
@@ -250,7 +250,7 @@
 FF_TICK = 27
 FF_LAG = 3
 W_TICK = 12
-AHEAD = 5
+AHEAD = 7
 
 
 def layer_kernel(dims, prefix, most, count, len_ref, x_hbm, cot_hbm, m_hbm, w_hbm, e_hbm, c_hbm, ri_hbm, ro_hbm,
@@ -601,7 +601,7 @@
             rows = pl.ds(i * tall, tall)
             grad = dot_nt(gmix[rows, :], w[...])
             hat, rate = norm_parts(x[rows, :].astype(F32))
-            x[rows, :] = (gm[rows, :] + norm_back(hat, rate, grad, gain_ref[...])).astype(BF16)
+            x[rows, :] = (gm[rows, :] + norm_back(hat, rate, grad, gain_ref[0:1, :])).astype(BF16)
             store(i).start()
 
         def bytes_of(ref, n, send, recv):
@@ -662,7 +662,7 @@
         grid=(pairs,),
         in_specs=[pl.BlockSpec(memory_space=pltpu.SMEM), pl.BlockSpec((1, length, 384), lambda p: (p, 0, 0)),
                   pcol(0), pcol(pairs), col(0), col(0), pl.BlockSpec((1, 2, length), lambda p: (p, 0, 0)),
-                  pl.BlockSpec((1, width), lambda p: (0, 0)), anyspace, anyspace, anyspace],
+                  pl.BlockSpec((2, width), lambda p: (0, 0)), anyspace, anyspace, anyspace],
         out_specs=[anyspace, pl.BlockSpec((4 * pairs, 8, 128), lambda p: (0, 0, 0))],
         out_shape=[jax.ShapeDtypeStruct((length, width), BF16), jax.ShapeDtypeStruct((4 * pairs, 8, 128), F32)],
         scratch_shapes=[pltpu.VMEM((length, 128), F32)] * 2 + [pltpu.VMEM((PAD, 128), F32)] * 2 + [
@@ -784,7 +784,7 @@
         as_row(contract_bias), norm_gains, norm_shifts, prefix_count, MOST,
     )
     grad_tokens, total = attend_back(
-        dims, mixed, lengths, pre, grad_attended, attended, log_sums, norm_gains[0:1],
+        dims, mixed, lengths, pre, grad_attended, attended, log_sums, norm_gains,
         full_mixer.reshape(pairs, model_width, 384), x, grad_middle, prefix_count, MOST,
     )
     grad_tokens, out_tokens, grad_embed, grad_in, grad_in_bias, grad_out, grad_out_bias = reparam_back(

time: 230 us -> 229 us (level)
  no operation moved by 1% of the time
where the time goes in v6:
time: 229 us
  Pallas kernels  217 us (95%)
  local copies, waits for them, and re-layouts  10.8 us (5%)
    pallas_call x1, Pallas kernels, layer(): pl.pallas_call(functools.partial(layer_kernel, dims, prefix, most, length...  148 us
    pallas_call x1, Pallas kernels, attend_back(): pl.pallas_call(functools.partial(back_kernel, dims, prefix, most, count),...  61.2 us
    pallas_call x1, Pallas kernels, reparam_back(): pl.pallas_call(functools.partial(reparam_kernel, prefix), grid=(steps,),...  7.96 us
    unnamed x18, local copies, waits for them, and re-layouts  5.53 us

profile of v6, /device:TPU:0, one launch (start us, length us, event | category | flops | bytes accessed | tf_op | source)
XLA Modules:
  0.0 228.6 jit_solution(10439685899949306504)
XLA Ops:
  0.6 0.0 copy-start.7
  0.6 1.5 pad.4.embed_ref
  2.2 0.8 reshape.73
  3.0 0.7 squeeze_reshape.3.be_ref
  3.7 1.0 copy.32
  4.7 0.1 copy.34
  4.8 0.8 reshape.65.m_hbm
  5.6 0.0 copy-done.7
  5.6 0.5 copy.28
  6.1 0.2 copy.29
  6.3 1.0 copy.31.e_hbm
  7.4 147.8 %layer.1 = (bf16[8,1024,384]{2,1,0:T(8,128)(2,1)}, bf16[1024,1024]{1,0:T(8,128)(2,1)}, f32[8,2,1024]{2,1,0:T(2,128)}, bf16[16,2048]{1,0:T(8,128)(2,1)}, f32[16,5...) custom-call(s32[1,8]{1,0:T(1,128)} %len_ref.3, ...), custom_call_target="tpu_custom_call" | custom-call | tf_op jit(solution)/shard_map/layer/pallas_call | solution.py:452
  155.2 0.0 copy-start
  155.2 0.0 copy-start.1
  155.2 0.0 copy-start.4
  155.2 0.0 copy-start.6
  155.2 61.2 %attend_back.1 = (bf16[1024,1024]{1,0:T(8,128)(2,1)}, f32[32,8,128]{2,1,0:T(8,128)}) custom-call(s32[1,8]{1,0:T(1,128)} %len_ref.3, bf16[8,1024,384]{2,1,0:T(8,128)(2,1)} %get-tuple-element.25.mixed_ref, bf16[16,2048]{1,0:T(8,128)(2,1)} %get-tuple-element.26.pk_ref.pv_ref, bf16[16,2048]{1,0:T(8,128)(2,1)} %get-tuple-element.26.pk_ref.pv_ref, ...), custom_call_target="tpu_custom_call" | custom-call | tf_op jit(solution)/shard_map/attend_back/pallas_call | solution.py:660
  216.4 0.0 copy-done
  216.4 0.0 copy-done.1
  216.4 0.0 copy-done.4
  216.4 0.0 copy-done.6
  216.4 0.0 copy-start.2
  216.4 1.6 copy-done.2
  218.0 0.0 copy-start.3
  218.0 1.6 copy-done.3
  219.6 0.0 copy-start.5
  219.6 0.9 copy-done.5
  220.5 8.0 %reparam_back.1 = (bf16[1024,1024]{1,0:T(8,128)(2,1)}, bf16[1024,1024]{1,0:T(8,128)(2,1)}, f32[10,1024]{1,0:T(8,128)}, f32[1024,512]{1,0:T(8,128)}, f32[1,512]{1...) custom-call(f32[32,8,128]{2,1,0:T(8,128)S(1)} %copy-done.5, f32[16,512]{1,0:T(8,128)S(1)} %copy-done.6, ...), custom_call_target="tpu_custom_call" | custom-call | tf_op jit(solution)/shard_map/reparam_back/pallas_call | solution.py:725
  (1 shorter events, 0.0 us)
Async XLA Ops:
  0.6 5.0 %copy-start.7 = (bf16[32,4096]{1,0:T(8,128)(2,1)S(1)}, bf16[32,4096]{1,0:T(8,128)(2,1)}, u32[]{:S(2)}) copy-start(bf16[32,4096]{1,0:T(8,128)(2,1)} %param.23) | copy-start | bytes 786436
  155.2 61.2 %copy-start = (f32[512,2048]{1,0:T(8,128)S(1)}, f32[512,2048]{1,0:T(8,128)}, u32[]{:S(2)}) copy-start(f32[512,2048]{1,0:T(8,128)} %ro_ref.1) | copy-start | bytes 12582916
  155.2 61.2 %copy-start.1 = (f32[1024,512]{1,0:T(8,128)S(1)}, f32[1024,512]{1,0:T(8,128)}, u32[]{:S(2)}) copy-start(f32[1024,512]{1,0:T(8,128)} %ri_ref.1) | copy-start | bytes 6291460
  155.2 61.2 %copy-start.4 = (f32[16,1024]{1,0:T(8,128)S(1)}, f32[16,1024]{1,0:T(8,128)}, u32[]{:S(2)}) copy-start(f32[16,1024]{1,0:T(8,128)} %pad.4.embed_ref) | copy-start | bytes 196612
  155.2 61.2 %copy-start.6 = (f32[16,512]{1,0:T(8,128)S(1)}, f32[16,512]{1,0:T(8,128)}, u32[]{:S(2)}) copy-start(f32[16,512]{1,0:T(8,128)} %get-tuple-element.33.sq_ref) | copy-start | bytes 98308
  216.4 1.6 copy-start.2
  218.0 1.6 copy-start.3
  219.6 0.9 copy-start.5
